TPU v7x, 32 devices: a whole 2x2x4 slice. The times are simulated.
32 devices in a mesh: dp: 4 (over y, x), fsdp: 8 (over z, core).
Axes of the slice: x: 2, y: 2, z: 4, core: 2. Of those that a mesh axis runs over, the one named last changes fastest.
Arguments:
- tokens: bfloat16 [32768, 512], P(('dp', 'fsdp')), may hold values from -6 to 6
- encoded: bfloat16 [32768, 512], P(('dp', 'fsdp')), may hold values from -6 to 6
- cotangent: bfloat16 [32768, 512], P(('dp', 'fsdp')), may hold values from -6 to 6
- target_ids: int32 [32, 1024], P(('dp', 'fsdp')), may hold values from 0 to 9, never falling along the last dimension, each value on 1 to 200 neighbouring positions
- source_ids: int32 [32, 1024], P(('dp', 'fsdp')), may hold values from 0 to 9, never falling along the last dimension, each value on 1 to 200 neighbouring positions
- qkv_master: float32 [6, 512, 512], P(None, ('dp', 'fsdp')), may hold values from -0.25 to 0.25
- qkv_first: float32 [6, 512, 512], P(None, ('dp', 'fsdp')), may hold values from -16 to 16
- qkv_second: float32 [6, 512, 512], P(None, ('dp', 'fsdp')), may hold values from 0 to 100, as said below
- out_master: float32 [2, 512, 512], P(None, ('dp', 'fsdp')), may hold values from -1.75 to 1.75
- out_first: float32 [2, 512, 512], P(None, ('dp', 'fsdp')), may hold values from -16 to 16
- out_second: float32 [2, 512, 512], P(None, ('dp', 'fsdp')), may hold values from 0 to 100, as said below
- ffn_in_master: float32 [512, 2048], P(('dp', 'fsdp')), may hold values from -0.25 to 0.25
- ffn_in_first: float32 [512, 2048], P(('dp', 'fsdp')), may hold values from -16 to 16
- ffn_in_second: float32 [512, 2048], P(('dp', 'fsdp')), may hold values from 0 to 100, as said below
- ffn_out_master: float32 [2048, 512], P(('dp', 'fsdp')), may hold values from -0.125 to 0.125
- ffn_out_first: float32 [2048, 512], P(('dp', 'fsdp')), may hold values from -16 to 16
- ffn_out_second: float32 [2048, 512], P(('dp', 'fsdp')), may hold values from 0 to 100, as said below
- vector_master: float32 [17, 512], P(None, ('dp', 'fsdp')), may hold values from -3 to 3
- vector_first: float32 [17, 512], P(None, ('dp', 'fsdp')), may hold values from -16 to 16
- vector_second: float32 [17, 512], P(None, ('dp', 'fsdp')), may hold values from 0 to 120, as said below
Outputs:
- layer_out: bfloat16 [32768, 512], P(('dp', 'fsdp'))
- tokens_grad: float32 [32768, 512], P(('dp', 'fsdp'))
- encoded_grad: float32 [32768, 512], P(('dp', 'fsdp'))
- qkv_first_new: float32 [6, 512, 512], P(None, ('dp', 'fsdp'))
- qkv_second_new: float32 [6, 512, 512], P(None, ('dp', 'fsdp'))
- qkv_master_new: float32 [6, 512, 512], P(None, ('dp', 'fsdp'))
- qkv_copy: bfloat16 [6, 512, 512], P(None, ('dp', 'fsdp'))
- out_first_new: float32 [2, 512, 512], P(None, ('dp', 'fsdp'))
- out_second_new: float32 [2, 512, 512], P(None, ('dp', 'fsdp'))
- out_master_new: float32 [2, 512, 512], P(None, ('dp', 'fsdp'))
- out_copy: bfloat16 [2, 512, 512], P(None, ('dp', 'fsdp'))
- ffn_in_first_new: float32 [512, 2048], P(('dp', 'fsdp'))
- ffn_in_second_new: float32 [512, 2048], P(('dp', 'fsdp'))
- ffn_in_master_new: float32 [512, 2048], P(('dp', 'fsdp'))
- ffn_in_copy: bfloat16 [512, 2048], P(('dp', 'fsdp'))
- ffn_out_first_new: float32 [2048, 512], P(('dp', 'fsdp'))
- ffn_out_second_new: float32 [2048, 512], P(('dp', 'fsdp'))
- ffn_out_master_new: float32 [2048, 512], P(('dp', 'fsdp'))
- ffn_out_copy: bfloat16 [2048, 512], P(('dp', 'fsdp'))
- vector_first_new: float32 [17, 512], P(None, ('dp', 'fsdp'))
- vector_second_new: float32 [17, 512], P(None, ('dp', 'fsdp'))
- vector_master_new: float32 [17, 512], P(None, ('dp', 'fsdp'))
- vector_copy: bfloat16 [17, 512], P(None, ('dp', 'fsdp'))
Inputs may be any that keep to these rules, and one draw needn't show every extreme that they name: `target_ids`: in each row (one group) ids never fall and every id of 0 to 9 occurs, in a run of 1 to 200 positions; one run has exactly 200. `source_ids`: in each row (one group) ids never fall and every id of 0 to 9 occurs, in a run of 1 to 200 positions; one run has exactly 200. `qkv_second`: positive. `out_second`: positive. `ffn_in_second`: positive. `ffn_out_second`: positive. `vector_second`: positive.
All inputs are finite; a program needn't handle non-finite values.
Results may differ from a plain program's by a relative error of at most 0.02.
The roundings to bfloat16 on the way count: a program that leaves them out, or rounds other values in their place, can miss the bound.
Values may be sent and summed in bfloat16 or wider, within the bound.
No kernel may reach another device: no remote copies, remote signals or barrier semaphores. Data moves between devices by JAX's collectives and lax.ppermute only.
A program may use at most 192 MiB of HBM per device.

v0:
```python
import functools
import math

import jax
import jax.numpy as jnp
from jax import lax
from jax.experimental import pallas as pl
from jax.experimental.pallas import tpu as pltpu
from jax.sharding import PartitionSpec as P

HEADS = 8
STEP = 5
SEGMENTS = 10
norm_eps = 1e-05
beta_first = 0.5
beta_second = 0.5
adam_eps = 1e-08
weight_decay = 0.01
mask_fill = -1000000000.0
LOW = jnp.bfloat16
FULL = jnp.float32


def dot_nn(left, right):
    return lax.dot_general(left, right, (((1,), (0,)), ((), ())), preferred_element_type=FULL)


def dot_nt(left, right):
    return lax.dot_general(left, right, (((1,), (1,)), ((), ())), preferred_element_type=FULL)


def dot_tn(left, right):
    return lax.dot_general(left, right, (((0,), (0,)), ((), ())), preferred_element_type=FULL)


def head_masks(width, group, factor):
    lane = lax.broadcasted_iota(jnp.int32, (1, group * width), 1) // width
    return [jnp.where(lane == h, factor, 0.0).astype(LOW) for h in range(group)]


def window(start, size, total):
    return pl.multiple_of(jnp.minimum(start // 16 * 16, total - size), 16)


def inside(base, size, begin, end):
    place = lax.broadcasted_iota(jnp.int32, (size, 1), 0) + base
    return (place >= begin) & (place < end)


def each_span(row_starts, col_starts, total, same, work):
    def segment(s, carry):
        row_begin, row_end = row_starts[s], row_starts[s + 1]
        col_begin, col_end = col_starts[s], col_starts[s + 1]
        row_short = row_end - window(row_begin, 128, total) <= 128
        col_short = col_end - window(col_begin, 128, total) <= 128
        for row_span in (128, 256):
            for col_span in (128, 256):
                if same and row_span != col_span:
                    continue
                wanted = row_short if row_span == 128 else jnp.logical_not(row_short)
                if not same:
                    other = col_short if col_span == 128 else jnp.logical_not(col_short)
                    wanted = jnp.logical_and(wanted, other)

                @pl.when(wanted)
                def _(row_span=row_span, col_span=col_span):
                    row_base = window(row_begin, row_span, total)
                    col_base = window(col_begin, col_span, total)
                    work(
                        s,
                        pl.ds(row_base, row_span),
                        pl.ds(col_base, col_span),
                        inside(row_base, row_span, row_begin, row_end),
                        inside(col_base, col_span, col_begin, col_end),
                        row_span,
                    )

        return carry

    lax.fori_loop(0, SEGMENTS, segment, 0)


def attend_forward(row_starts, col_starts, q_ref, k_ref, v_ref, out_ref, sums_ref):
    total, model = q_ref.shape
    width = model // HEADS
    group = 256 // width
    scales = head_masks(width, group, 1.0 / math.sqrt(width))
    parts = [slice(g * 256, (g + 1) * 256) for g in range(HEADS // group)]

    def work(s, rows, cols, row_mask, col_mask, span):
        raw = []
        for lanes in parts:
            query, keys = q_ref[rows, lanes], k_ref[cols, lanes]
            stacked = jnp.concatenate([query * scale for scale in scales], axis=0)
            raw.append(dot_nt(keys, stacked))
        turned = [v_ref[cols, lanes].T for lanes in parts]
        probs = []
        for g, item in enumerate(raw):
            scores = jnp.where(col_mask, item, mask_fill)
            largest = jnp.max(scores, axis=0, keepdims=True)
            expo = jnp.exp(scores - largest)
            totals = jnp.sum(expo, axis=0, keepdims=True)
            sums_ref[s, g, :, : group * span] = largest + jnp.log(totals)
            probs.append((expo * (1.0 / totals)).astype(LOW))
        mixed = [
            [
                dot_nn(side[h * width : (h + 1) * width], prob[:, h * span : (h + 1) * span])
                for h in range(group)
            ]
            for side, prob in zip(turned, probs)
        ]
        for lanes, items in zip(parts, mixed):
            value = jnp.concatenate(items, axis=0).T
            old = out_ref[rows, lanes].astype(FULL)
            out_ref[rows, lanes] = jnp.where(row_mask, value, old).astype(LOW)

    each_span(row_starts, col_starts, total, row_starts is col_starts, work)


def attend_backward(
    row_starts, col_starts, q_ref, k_ref, v_ref, grad_ref, sums_ref, dq_ref, dk_ref, dv_ref
):
    total, model = q_ref.shape
    width = model // HEADS
    group = 256 // width
    factor = 1.0 / math.sqrt(width)
    scales = head_masks(width, group, factor)
    picks = head_masks(width, group, 1.0)
    parts = [slice(g * 256, (g + 1) * 256) for g in range(HEADS // group)]

    def work(s, rows, cols, row_mask, col_mask, span):
        stacks, grads, raw, grad_probs = [], [], [], []
        for lanes in parts:
            query, keys, values = q_ref[rows, lanes], k_ref[cols, lanes], v_ref[cols, lanes]
            grad = jnp.where(row_mask, grad_ref[rows, lanes].astype(FULL), 0.0).astype(LOW)
            stacks.append(jnp.concatenate([query * scale for scale in scales], axis=0))
            grads.append(jnp.concatenate([grad * item for item in picks], axis=0))
            raw.append(dot_nt(keys, stacks[-1]))
            grad_probs.append(dot_nt(values, grads[-1]))
        grad_values, grad_scores = [], []
        for g, (item, grad_prob) in enumerate(zip(raw, grad_probs)):
            scores = jnp.where(col_mask, item, mask_fill)
            probs = jnp.exp(scores - sums_ref[s, g, :, : group * span])
            grad_values.append(dot_nn(probs.astype(LOW), grads[g]))
            weighted = probs * grad_prob
            inner = jnp.sum(weighted, axis=0, keepdims=True)
            grad_scores.append((weighted - probs * inner).astype(LOW))
        grad_keys, grad_queries = [], []
        for lanes, item, stacked in zip(parts, grad_scores, stacks):
            grad_keys.append(dot_nn(item, stacked))
            turned = k_ref[cols, lanes].T
            grad_queries.append(
                [
                    dot_nn(turned[h * width : (h + 1) * width], item[:, h * span : (h + 1) * span])
                    for h in range(group)
                ]
            )
        for g, lanes in enumerate(parts):
            grad_query = jnp.concatenate(grad_queries[g], axis=0).T * factor
            for ref, place, mask, value in (
                (dq_ref, rows, row_mask, grad_query),
                (dk_ref, cols, col_mask, grad_keys[g]),
                (dv_ref, cols, col_mask, grad_values[g]),
            ):
                old = ref[place, lanes].astype(FULL)
                ref[place, lanes] = jnp.where(mask, value, old).astype(LOW)

    each_span(row_starts, col_starts, total, row_starts is col_starts, work)


def normalize(values):
    center = values - jnp.mean(values, axis=-1, keepdims=True)
    inverse = lax.rsqrt(jnp.mean(center * center, axis=-1, keepdims=True) + norm_eps)
    return center * inverse, inverse


def normalize_back(grad, gain, unit, inverse):
    scaled = grad * (1.0 + gain)
    mean = jnp.mean(scaled, axis=-1, keepdims=True)
    along = jnp.mean(scaled * unit, axis=-1, keepdims=True)
    return (scaled - mean - unit * along) * inverse


def column_sum(values):
    return jnp.sum(values.astype(FULL), axis=0, keepdims=True)


STEP_ROWS = 512


def row_steps(total, step, size=256):
    def run(i, carry):
        step(pl.ds(pl.multiple_of(i * size, size), size))
        return carry

    lax.fori_loop(0, total // size, run, 0)


def load_weights(place, depth, sources, targets, semaphores):
    if len(sources) == 1:
        offset = 0
        for target, semaphore in zip(targets, semaphores):
            source = sources[0].at[:, offset : offset + target.shape[1]]
            offset += target.shape[1]
            pltpu.make_async_copy(source, target, semaphore).start()
        return
    half = len(sources) // 2
    for k, source in enumerate(sources):
        base = (k % half) * 2 * depth + k // half
        for layer in range(depth):
            other = place ^ (base + 2 * layer)
            offset = 0
            for target, semaphore in zip(targets, semaphores):
                rows = source.shape[1]
                span = target.shape[1]
                to_rows = pl.ds(pl.multiple_of(other * rows, rows), rows)
                pltpu.make_async_copy(
                    source.at[layer, :, offset : offset + span], target.at[to_rows, :], semaphore
                ).start()
                offset += span


def await_weights(target, semaphore):
    pltpu.make_async_copy(target, target, semaphore).wait()


def store_grad(refs, core, lanes, value):
    value = value.astype(LOW)
    if len(refs) == 1:
        refs[0][:, lanes] = value
        return
    sent, kept = refs
    chips, rows = kept.shape[0], kept.shape[1]
    parts = value.reshape(chips, 2, rows, value.shape[1])
    first = core == 0
    kept[:, :, lanes] = jnp.where(first, parts[:, 0], parts[:, 1])
    sent[:, :, lanes] = jnp.where(first, parts[:, 1], parts[:, 0])


def self_forward_kernel(count, depth, place, row_starts, tokens, *rest):
    sources = rest[:count]
    weights, vectors, queries, keys, values, mixed, sums, semaphores = rest[count:]
    model = tokens.shape[1]
    load_weights(place[0], depth, sources, [weights], [semaphores.at[0]])
    await_weights(weights, semaphores.at[0])
    turned = weights[:, 3 * model : 3 * model + 128].astype(FULL).T
    vectors[...] = turned[: vectors.shape[0]]

    def project(rows):
        block = tokens[rows, :]
        queries[rows, :] = (dot_nn(block, weights[:, :model]) + vectors[0:1, :]).astype(LOW)
        keys[rows, :] = dot_nn(block, weights[:, model : 2 * model]).astype(LOW)
        values[rows, :] = (
            dot_nn(block, weights[:, 2 * model : 3 * model]) + vectors[1:2, :]
        ).astype(LOW)

    row_steps(tokens.shape[0], project)
    attend_forward(row_starts, row_starts, queries, keys, values, mixed, sums)


def cross_project_kernel(count, depth, place, tokens, encoded, mixed, vectors, *rest):
    sources = rest[:count]
    weights, unit_one, inverse_one, queries, keys, values, semaphores = rest[count:]
    model = tokens.shape[1]
    load_weights(place[0], depth, sources, [weights], [semaphores.at[0]])
    await_weights(weights, semaphores.at[0])

    def project(rows):
        block = encoded[rows, :]
        keys[rows, :] = dot_nn(block, weights[:, 2 * model : 3 * model]).astype(LOW)
        values[rows, :] = (
            dot_nn(block, weights[:, 3 * model : 4 * model]) + vectors[4:5, :]
        ).astype(LOW)
        summed = tokens[rows, :].astype(FULL) + dot_nn(mixed[rows, :], weights[:, :model])
        unit, inverse = normalize(summed + vectors[2:3, :])
        unit_one[rows, :] = unit
        inverse_one[rows, :] = inverse
        low = (unit * (1.0 + vectors[7:8, :]) + vectors[10:11, :]).astype(LOW)
        queries[rows, :] = (dot_nn(low, weights[:, model : 2 * model]) + vectors[3:4, :]).astype(LOW)

    row_steps(tokens.shape[0], project, 512)


def cross_attend_kernel(row_starts, col_starts, queries, keys, values, cross_mixed, sums):
    attend_forward(row_starts, col_starts, queries, keys, values, cross_mixed, sums)


def cross_finish_kernel(unit_one, cross_mixed, weights, vectors, unit_two, inverse_two):
    model = cross_mixed.shape[1]

    def finish(rows):
        first = unit_one[rows, :] * (1.0 + vectors[7:8, :]) + vectors[10:11, :]
        summed = first + dot_nn(cross_mixed[rows, :], weights[:, 4 * model : 5 * model])
        unit, inverse = normalize(summed + vectors[5:6, :])
        unit_two[rows, :] = unit
        inverse_two[rows, :] = inverse

    row_steps(unit_one.shape[0], finish, 512)


gelu_scale = math.sqrt(2.0 / math.pi)
gelu_cubic = 0.044715


def ffn_kernel(count, depth, place, unit_two, inverse_two, cotangent, weights, vectors, *rest):
    sources = rest[:count]
    (
        layer_out, grad_sum, grad_out, grad_mixed, sums, bias_sums, *grads,
        first_weights, second_weights, hidden, grad_ffn, grad_pre, slopes, semaphores,
    ) = rest[count:]
    model = unit_two.shape[1]
    pieces = first_weights.shape[1] // model
    load_ffn(place[0], depth, sources, first_weights, second_weights, semaphores)
    sums[...] = jnp.zeros_like(sums)
    bias_sums[...] = jnp.zeros_like(bias_sums)
    await_weights(first_weights, semaphores.at[0])
    await_weights(second_weights, semaphores.at[1])

    def step(rows):
        unit = unit_two[rows, :]
        second = unit * (1.0 + vectors[8:9, :]) + vectors[11:12, :]
        low = second.astype(LOW)
        total = second + vectors[6:7, :]
        for j in range(pieces):
            lanes = slice(j * model, (j + 1) * model)
            pre = dot_nn(low, first_weights[:, lanes]) + vectors[13 + j : 14 + j, :]
            square = pre * pre
            bend = jnp.tanh(gelu_scale * pre * (1.0 + gelu_cubic * square))
            half = 0.5 * (1.0 + bend)
            value = (pre * half).astype(LOW)
            hidden[rows, lanes] = value
            inner = gelu_scale * (1.0 + 3.0 * gelu_cubic * square)
            slopes[:, lanes] = half + 0.5 * pre * (1.0 - bend * bend) * inner
            total = total + dot_nn(value, second_weights[lanes, :])
        unit_three, inverse_three = normalize(total)
        layer_out[rows, :] = (unit_three * (1.0 + vectors[9:10, :]) + vectors[12:13, :]).astype(LOW)
        upper = cotangent[rows, :].astype(FULL)
        third = normalize_back(upper, vectors[9:10, :], unit_three, inverse_three)
        third_low = third.astype(LOW)
        grad_ffn[rows, :] = third_low
        sums[0:1, :] += column_sum(third_low)
        sums[1:2, :] += column_sum(upper * unit_three)
        sums[2:3, :] += column_sum(upper)
        below = third
        for j in range(pieces):
            lanes = slice(j * model, (j + 1) * model)
            pre = (dot_nt(third_low, second_weights[lanes, :]) * slopes[:, lanes]).astype(LOW)
            grad_pre[rows, lanes] = pre
            bias_sums[j : j + 1, :] += column_sum(pre)
            below = below + dot_nt(pre, first_weights[:, lanes])
        sums[3:4, :] += column_sum(below * unit)
        sums[4:5, :] += column_sum(below)
        second_sum = normalize_back(below, vectors[8:9, :], unit, inverse_two[rows, :])
        grad_sum[rows, :] = second_sum
        out_low = second_sum.astype(LOW)
        grad_out[rows, :] = out_low
        sums[5:6, :] += column_sum(out_low)
        grad_mixed[rows, :] = dot_nt(out_low, weights[:, 4 * model : 5 * model]).astype(LOW)

    row_steps(unit_two.shape[0], step, STEP_ROWS)
    core = place[0] % 2
    second_low = (unit_two[...] * (1.0 + vectors[8:9, :]) + vectors[11:12, :]).astype(LOW)

    def block_grads(j, carry):
        lanes = pl.ds(pl.multiple_of(j * model, model), model)
        store_grad(grads, core, lanes, dot_tn(second_low, grad_pre[:, lanes]))
        store_ffn_out(grads, core, j, pieces, dot_tn(hidden[:, lanes], grad_ffn[...]))
        return carry

    lax.fori_loop(0, pieces, block_grads, 0)


def load_ffn(place, depth, sources, first_weights, second_weights, semaphores):
    first_width = first_weights.shape[1]
    if len(sources) == 1:
        pltpu.make_async_copy(
            sources[0].at[:, :first_width], first_weights, semaphores.at[0]
        ).start()
        pieces = first_width // first_weights.shape[0]
        model = first_weights.shape[0]
        for j in range(pieces):
            pltpu.make_async_copy(
                sources[0].at[:, first_width + j * model : first_width + (j + 1) * model],
                second_weights.at[pl.ds(j * model, model), :],
                semaphores.at[1],
            ).start()
        return
    half = len(sources) // 2
    model = second_weights.shape[1]
    for k, source in enumerate(sources):
        base = (k % half) * 2 * depth + k // half
        rows = source.shape[1]
        for layer in range(depth):
            other = place ^ (base + 2 * layer)
            to_rows = pl.ds(pl.multiple_of(other * rows, rows), rows)
            pltpu.make_async_copy(
                source.at[layer, :, :first_width], first_weights.at[to_rows, :], semaphores.at[0]
            ).start()
            pieces = first_width // model
            for j in range(pieces):
                start = pl.multiple_of((other * pieces + j) * rows, rows)
                pltpu.make_async_copy(
                    source.at[layer, :, first_width + j * model : first_width + (j + 1) * model],
                    second_weights.at[pl.ds(start, rows), :],
                    semaphores.at[1],
                ).start()


def store_ffn_out(refs, core, block, pieces, value):
    value = value.astype(LOW)
    model = value.shape[1]
    if len(refs) == 1:
        offset = pl.multiple_of((pieces + block) * model, model)
        refs[0][:, pl.ds(offset, model)] = value
        return
    sent, kept = refs
    rows = kept.shape[1]
    chips = kept.shape[0] // pieces
    parts = value.reshape(chips, 2, pieces, rows, model)
    first = core == 0
    place = pl.ds(block * chips, chips)
    for j in range(pieces):
        lanes = slice((pieces + j) * model, (pieces + j + 1) * model)
        kept[place, :, lanes] = jnp.where(first, parts[:, 0, j], parts[:, 1, j])
        sent[place, :, lanes] = jnp.where(first, parts[:, 1, j], parts[:, 0, j])


def cross_backward_kernel(
    row_starts, col_starts, queries, keys, values, grad_mixed, sums_in, dq, dk, dv
):
    attend_backward(row_starts, col_starts, queries, keys, values, grad_mixed, sums_in, dq, dk, dv)


def cross_grads_kernel(
    place, dq, dk, dv, weights, vectors, grad_sum, unit_one, inverse_one,
    encoded, cross_mixed, grad_out,
    first_sum, self_low, grad_mixed, sums, encoded_grad, *grads,
):
    model = dq.shape[1]
    sums[...] = jnp.zeros_like(sums)

    def finish(rows):
        query, key, value = dq[rows, :], dk[rows, :], dv[rows, :]
        sums[0:1, :] += column_sum(query)
        sums[1:2, :] += column_sum(value)
        encoded_grad[rows, :] = dot_nt(key, weights[:, 2 * model : 3 * model]) + dot_nt(
            value, weights[:, 3 * model : 4 * model]
        )
        upper = grad_sum[rows, :] + dot_nt(query, weights[:, model : 2 * model])
        unit = unit_one[rows, :]
        sums[2:3, :] += column_sum(upper * unit)
        sums[3:4, :] += column_sum(upper)
        below = normalize_back(upper, vectors[7:8, :], unit, inverse_one[rows, :])
        first_sum[rows, :] = below
        low = below.astype(LOW)
        self_low[rows, :] = low
        sums[4:5, :] += column_sum(low)
        grad_mixed[rows, :] = dot_nt(low, weights[:, :model]).astype(LOW)

    row_steps(dq.shape[0], finish)
    core = place[0] % 2
    first_low = (unit_one[...] * (1.0 + vectors[7:8, :]) + vectors[10:11, :]).astype(LOW)
    pairs = ((first_low, dq), (encoded, dk), (encoded, dv), (cross_mixed, grad_out))
    for j, (left, right) in enumerate(pairs):
        lanes = slice(j * model, (j + 1) * model)
        store_grad(grads, core, lanes, dot_tn(left[...], right[...]))


def self_backward_kernel(
    place, row_starts, queries, keys, values, grad_mixed, sums_in, tokens, mixed, self_low,
    cross_sums, ffn_sums, bias_sums, dq, dk, dv, *rest,
):
    *grads, stack = rest
    attend_backward(row_starts, row_starts, queries, keys, values, grad_mixed, sums_in, dq, dk, dv)
    model = dq.shape[1]
    core = place[0] % 2
    pairs = ((tokens, dq), (tokens, dk), (tokens, dv), (mixed, self_low))
    for j, (left, right) in enumerate(pairs):
        lanes = slice(j * model, (j + 1) * model)
        store_grad(grads, core, lanes, dot_tn(left[...], right[...]))
    stack[...] = jnp.zeros_like(stack)
    stack[0:1, :] = column_sum(dq[...])
    stack[1:2, :] = column_sum(dv[...])
    order = (
        (2, cross_sums, 4), (3, cross_sums, 0), (4, cross_sums, 1), (5, ffn_sums, 5),
        (6, ffn_sums, 0), (7, cross_sums, 2), (8, ffn_sums, 3), (9, ffn_sums, 1),
        (10, cross_sums, 3), (11, ffn_sums, 4), (12, ffn_sums, 2),
    )
    for to, ref, at in order:
        stack[to : to + 1, :] = ref[at : at + 1, :]
    extra = bias_sums.shape[0]
    stack[13 : 13 + extra, :] = bias_sums[...]
    start = len(pairs) * model
    store_grad(grads, core, slice(start, start + 128), stack[...].T)


def tokens_grad_kernel(dq, dk, dv, first_sum, weights, tokens_grad):
    model = dq.shape[1]

    def finish(rows):
        below = first_sum[rows, :] + dot_nt(dq[rows, :], weights[:, :model])
        below = below + dot_nt(dk[rows, :], weights[:, model : 2 * model])
        tokens_grad[rows, :] = below + dot_nt(dv[rows, :], weights[:, 2 * model : 3 * model])

    row_steps(dq.shape[0], finish, 512)


def fold_core_kernel(shape, place, kept, received, own, *sends):
    dp_count, depth = shape
    at = place[0] // (2 * depth)
    for k, ref in enumerate((own, *sends)):
        spot = pl.ds((at ^ k) * depth, depth)
        value = kept[spot].astype(FULL) + received[spot].astype(FULL)
        ref[...] = value.astype(ref.dtype)


def fold_square_kernel(shape, place, kept, *rest):
    dp_count, depth = shape
    received, outs = rest[: dp_count - 1], rest[dp_count - 1 :]
    at = place[0] // 2 % depth
    for k, ref in enumerate(outs):
        spot = pl.ds(at ^ k, 1)
        value = kept[spot]
        for item in received:
            value = value + item[spot].astype(FULL)
        ref[...] = value[0].astype(ref.dtype)


def fold_halves_kernel(depth, place, kept, received, keep_first, send_first, keep_second, send_second):
    at = place[0] // (2 * depth)
    half = kept.shape[2] // 2
    low, high = slice(0, half), slice(half, 2 * half)
    for ref, lanes, offsets in (
        (keep_first, low, (0, 1)),
        (send_first, low, (2, 3)),
        (keep_second, high, (0, 2)),
        (send_second, high, (1, 3)),
    ):
        for slot, k in enumerate(offsets):
            spot = pl.ds((at ^ k) * depth, depth)
            value = kept[spot, :, lanes].astype(FULL) + received[spot, :, lanes].astype(FULL)
            ref[slot] = value.astype(ref.dtype)


def fold_pairs_kernel(keep_first, got_first, keep_second, got_second, *outs):
    own_first, send_first, own_second, send_second = outs
    own_first[...] = keep_first[0] + got_first[0].astype(FULL)
    send_first[...] = (keep_first[1] + got_first[1].astype(FULL)).astype(LOW)
    own_second[...] = keep_second[0] + got_second[0].astype(FULL)
    send_second[...] = (keep_second[1] + got_second[1].astype(FULL)).astype(LOW)


def fold_layers_kernel(depth, place, first, got_first, second, got_second, cross, *rest):
    *got_cross, keep, send = rest
    at = place[0] // 2 % depth
    half = first.shape[2]
    for ref, offsets in ((keep, (0, 1)), (send, (2, 3))):
        for slot, k in enumerate(offsets):
            spot = pl.ds(at ^ k, 1)
            value = first[spot] + got_first[spot].astype(FULL)
            ref[slot, :, :half] = value[0].astype(ref.dtype)
            value = second[spot] + got_second[spot].astype(FULL)
            ref[slot, :, half : 2 * half] = value[0].astype(ref.dtype)
            value = cross[spot]
            for item in got_cross:
                value = value + item[spot].astype(FULL)
            ref[slot, :, 2 * half :] = value[0].astype(ref.dtype)


def fold_last_kernel(keep, got, own, send):
    own[...] = keep[0] + got[0].astype(FULL)
    send[...] = (keep[1] + got[1].astype(FULL)).astype(LOW)


def update_into(outs, index, state, grad, rate):
    for ref, value in zip(outs, adamw(state[0][index], grad, state[1][index], state[2][index], rate)):
        ref[index] = value


def ffn_update_kernel(grad_scale, own, got, *rest):
    first_state, second_state, outs = rest[:3], rest[3:6], rest[6:]
    rows, width = first_state[0].shape
    model = second_state[0].shape[1]
    grad = (own[:, :width] + got[:, :width].astype(FULL)) * grad_scale
    update_into(outs[:4], (slice(None), slice(None)), first_state, grad, 0.04)
    for j in range(second_state[0].shape[0] // rows):
        lanes = slice(width + j * model, width + (j + 1) * model)
        grad = (own[:, lanes] + got[:, lanes].astype(FULL)) * grad_scale
        index = (slice(j * rows, (j + 1) * rows), slice(None))
        update_into(outs[4:], index, second_state, grad, 0.02)


def final_update_kernel(grad_scale, start, own, got, kept, *rest):
    moved, states, outs = rest[:-21], rest[-21:-12], rest[-12:]
    qkv_state, out_state, vector_state = states[:3], states[3:6], states[6:]
    model = qkv_state[0].shape[2]

    def self_grad(lanes):
        value = kept[:, lanes]
        for item in moved:
            value = value + item[:, lanes].astype(FULL)
        return value * grad_scale

    def cross_grad(index):
        lanes = slice(start + index * model, start + (index + 1) * model)
        return (own[:, lanes] + got[:, lanes].astype(FULL)) * grad_scale

    for j in range(4):
        grad = self_grad(slice(j * model, (j + 1) * model))
        if j < 3:
            update_into(outs[:4], j, qkv_state, grad, 0.04)
            update_into(outs[:4], 3 + j, qkv_state, cross_grad(j), 0.04)
        else:
            update_into(outs[4:8], 0, out_state, grad, 0.3)
            update_into(outs[4:8], 1, out_state, cross_grad(j), 0.3)
    grad = self_grad(slice(4 * model, 4 * model + vector_state[0].shape[1]))
    update_into(outs[8:], (slice(None), slice(None)), vector_state, grad, 0.35)


LIMITS = {
    "fold_halves": 16,
    "fold_pairs": 14,
    "fold_layers": 12,
    "fold_last": 8,
    "ffn_update": 8,
    "final_update": 10,
    "fold_core": 12,
    "fold_square": 10,
    "self_forward": 14,
    "cross_project": 14,
    "cross_attend": 10,
    "cross_finish": 9,
    "ffn": 33,
    "cross_backward": 11,
    "cross_grads": 20,
    "self_backward": 16,
    "tokens_grad": 11,
}


def out_kind(item):
    if len(item) == 3:
        return pltpu.VMEM(item[0], item[1])
    return jax.ShapeDtypeStruct(*item)


def keep(item):
    return (item[0], item[1], True)


def limit(name):
    return pltpu.CompilerParams(vmem_limit_bytes=LIMITS[name] << 20)


def pinned(sources):
    if len(sources) == 1:
        return sources
    return [pltpu.with_memory_space_constraint(item, pltpu.VMEM) for item in sources]


def source_spec(sources):
    return pl.BlockSpec(memory_space=pltpu.VMEM if len(sources) > 1 else pl.ANY)


def call(kernel, name, scalars, arrays, outs, flops, sources=(), scratch=()):
    specs = [pl.BlockSpec(memory_space=pltpu.SMEM)] * len(scalars)
    specs += [pl.BlockSpec(memory_space=pltpu.VMEM)] * len(arrays)
    specs += [source_spec(sources)] * len(sources)
    shapes = [out_kind(item) for item in outs]
    moved = sum(item.size * item.dtype.itemsize for item in [*arrays, *sources])
    return pl.pallas_call(
        kernel,
        out_shape=shapes,
        in_specs=specs,
        out_specs=[pl.BlockSpec(memory_space=pltpu.VMEM)] * len(outs),
        scratch_shapes=list(scratch),
        compiler_params=limit(name),
        cost_estimate=pl.CostEstimate(flops=flops, transcendentals=0, bytes_accessed=moved),
        name=name,
    )(*scalars, *arrays, *pinned(sources))


def segment_starts(ids):
    marks = jnp.arange(SEGMENTS + 1, dtype=ids.dtype)
    return jnp.sum((ids[None, :] < marks[:, None]).astype(jnp.int32), axis=1)


def adamw(master, grad, first, second, rate):
    first_new = beta_first * first + (1.0 - beta_first) * grad
    second_new = beta_second * second + (1.0 - beta_second) * grad * grad
    first_hat = first_new / (1.0 - beta_first**STEP)
    second_hat = second_new / (1.0 - beta_second**STEP)
    master_new = master - rate * (
        first_hat / (jnp.sqrt(second_hat) + adam_eps) + weight_decay * master
    )
    return (first_new, second_new, master_new, master_new.astype(jnp.bfloat16))


AXES = ("dp", "fsdp")


def exchange(values, offset):
    count = lax.axis_size("dp") * lax.axis_size("fsdp")
    return lax.ppermute(values, AXES, [(i, i ^ offset) for i in range(count)])


def after(value, *others):
    return lax.optimization_barrier((value, *others))[0]


def layer_stack(piece):
    depth = lax.axis_size("fsdp") // 2
    return jnp.stack([piece] + [exchange(piece, 2 * k) for k in range(1, depth)])


def layer_double(piece, gate=None):
    stack, step = piece[None], 1
    while step < lax.axis_size("fsdp") // 2:
        if gate is not None and step > 1:
            stack = after(stack, gate)
        stack = jnp.concatenate([stack, exchange(stack, 2 * step)])
        step *= 2
    return stack


def square_list(stack):
    dp_count, fsdp_count = lax.axis_size("dp"), lax.axis_size("fsdp")
    return [stack] + [exchange(stack, fsdp_count * k) for k in range(1, dp_count)]


def forward_list(stack):
    stride, near = lax.axis_size("fsdp"), [stack]
    for k in range(1, lax.axis_size("dp")):
        near.append(None if k & (k - 1) else exchange(stack, stride * k))
    return near


def forward_rest(near, gate):
    stride = lax.axis_size("fsdp")
    for k, item in enumerate(near):
        if item is None:
            high = 1 << (k.bit_length() - 1)
            near[k] = exchange(after(near[k - high], gate), stride * high)
    return near


def core_list(near):
    return near + [exchange(item, 1) for item in near]


def ordered(parts, place):
    half = len(parts) // 2
    both = jnp.stack([jnp.stack(parts[:half]), jnp.stack(parts[half:])], axis=2)
    flat = both.reshape((-1,) + both.shape[3:])
    return flat[jnp.arange(flat.shape[0]) ^ place]


def pick(values, index, axis):
    return lax.dynamic_index_in_dim(values, index, axis, keepdims=False)


def split_core(grads):
    if len(grads) == 2:
        return grads
    count = lax.axis_size("dp") * lax.axis_size("fsdp")
    core = lax.axis_index("fsdp") % 2
    parts = grads[0].reshape((count // 2, 2, -1) + grads[0].shape[1:])
    return pick(parts, 1 - core, 1), pick(parts, core, 1)


def fold_core(spot, kept, received):
    dp_count, depth = lax.axis_size("dp"), lax.axis_size("fsdp") // 2
    shape = (depth,) + kept.shape[1:]
    if kept.shape[1] % 16:
        place = lax.axis_index("dp")
        pair = (kept.astype(FULL) + received.astype(FULL)).reshape((dp_count,) + shape)
        sends = [pick(pair, place ^ k, 0).astype(LOW) for k in range(1, dp_count)]
        return pick(pair, place, 0), sends
    own, *sends = call(
        functools.partial(fold_core_kernel, (dp_count, depth)), "fold_core", [spot],
        [kept, received], [(shape, FULL)] + [(shape, LOW)] * (dp_count - 1), kept.size,
    )
    return own, sends


def fold_square(spot, kept, received):
    dp_count, depth = lax.axis_size("dp"), lax.axis_size("fsdp") // 2
    shape = kept.shape[1:]
    if kept.shape[1] % 16:
        place = lax.axis_index("fsdp") // 2
        square = add_all(kept, received)
        sends = [pick(square, place ^ k, 0).astype(LOW) for k in range(1, depth)]
        return pick(square, place, 0), sends
    own, *sends = call(
        functools.partial(fold_square_kernel, (dp_count, depth)), "fold_square", [spot],
        [kept, *received], [(shape, FULL)] + [(shape, LOW)] * (depth - 1), kept.size,
    )
    return own, sends


def move_square(sends):
    stride = lax.axis_size("fsdp")
    return [exchange(item, stride * (k + 1)) for k, item in enumerate(sends)]


def move_layers(sends):
    return [exchange(item, 2 * (k + 1)) for k, item in enumerate(sends)]


def add_all(kept, moved):
    for item in moved:
        kept = kept + item.astype(FULL)
    return kept


def body(
    tokens,
    encoded,
    cotangent,
    target_ids,
    source_ids,
    qkv_master,
    qkv_first,
    qkv_second,
    out_master,
    out_first,
    out_second,
    ffn_in_master,
    ffn_in_first,
    ffn_in_second,
    ffn_out_master,
    ffn_out_first,
    ffn_out_second,
    vector_master,
    vector_first,
    vector_second,
):
    total, model = tokens.shape
    dp_count, fsdp_count = lax.axis_size("dp"), lax.axis_size("fsdp")
    count, depth = dp_count * fsdp_count, fsdp_count // 2
    rows = model // count
    aligned = rows % 16 == 0
    place = lax.axis_index("dp") * fsdp_count + lax.axis_index("fsdp")
    spot = place.reshape(1).astype(jnp.int32)
    low_qkv = after(qkv_master, spot).astype(LOW)
    low_out = out_master.astype(LOW)
    low_vector = jnp.pad(vector_master.astype(LOW).T, ((0, 0), (0, 128 - vector_master.shape[0])))
    pieces = ffn_in_master.shape[1] // model

    def to_columns(values):
        return values.reshape(-1, rows, model).transpose(1, 0, 2).reshape(rows, -1)

    self_piece = jnp.concatenate([low_qkv[0], low_qkv[1], low_qkv[2], low_vector], axis=1)
    cross_piece = jnp.concatenate([low_out[0], low_qkv[3], low_qkv[4], low_qkv[5], low_out[1]], axis=1)
    ffn_piece = jnp.concatenate(
        [ffn_in_master.astype(LOW), to_columns(ffn_out_master.astype(LOW))], axis=1
    )
    row_starts, col_starts = segment_starts(target_ids[0]), segment_starts(source_ids[0])

    def sources_of(parts):
        if aligned:
            return parts
        flat = ordered(parts, place)
        return [flat.reshape(model, -1)]

    def ffn_sources_of(parts):
        if aligned:
            return parts
        flat = ordered(parts, place)
        width = pieces * model
        second = flat[:, :, width:].reshape(count, rows, pieces, model).transpose(0, 2, 1, 3)
        second = second.reshape(pieces, model, model).transpose(1, 0, 2).reshape(model, -1)
        return [jnp.concatenate([flat[:, :, :width].reshape(model, -1), second], axis=1)]

    wide, tall, thin = ((total, model), LOW), ((total, model), FULL), ((total, 1), FULL)
    log_sums = ((SEGMENTS, model // 256, 1, 1024), FULL)
    small = ((8, model), FULL)
    unit = 2 * total * model * model
    attend = 2 * SEGMENTS * HEADS * 256 * 256 * 256
    wait_one, wait_two = pltpu.SemaphoreType.DMA((1,)), pltpu.SemaphoreType.DMA((2,))

    def grad_outs(columns):
        if aligned:
            return [((count // 2, rows, columns), LOW)] * 2
        return [((model, columns), LOW)]

    self_stack = layer_stack(self_piece)
    self_near = square_list(self_stack)
    cross_own = layer_double(after(cross_piece, self_stack))
    ffn_own = layer_double(after(ffn_piece, self_stack), cross_own)
    self_parts = core_list(self_near)
    cross_columns = cross_piece.shape[1]
    cross_near = square_list(cross_own)
    ffn_near = forward_list(ffn_own)

    sources = sources_of(self_parts)
    (
        self_weights, vectors, queries, keys, values, mixed, self_sums,
    ) = call(
        functools.partial(self_forward_kernel, len(sources), depth), "self_forward",
        [spot, row_starts], [after(tokens, cross_own)],
        [
            keep(((model, self_piece.shape[1]), LOW)), ((24, model), FULL),
            keep(wide), keep(wide), keep(wide), keep(wide), keep(log_sums),
        ],
        3 * unit + 2 * attend, sources, [wait_one],
    )
    sources = sources_of(core_list([after(item, mixed) for item in cross_near]))
    cross_weights, unit_one, inverse_one, cross_queries, cross_keys, cross_values = call(
        functools.partial(cross_project_kernel, len(sources), depth), "cross_project", [spot],
        [tokens, encoded, mixed, vectors],
        [
            keep(((model, cross_columns), LOW)), keep(tall), thin, keep(wide), keep(wide),
            keep(wide),
        ],
        4 * unit, sources, [wait_one],
    )
    ffn_near = forward_rest(ffn_near, cross_queries)
    cross_mixed, cross_log = call(
        cross_attend_kernel, "cross_attend", [row_starts, col_starts],
        [cross_queries, cross_keys, cross_values], [keep(wide), keep(log_sums)], 2 * attend,
    )
    unit_two, inverse_two = call(
        cross_finish_kernel, "cross_finish", [], [unit_one, cross_mixed, cross_weights, vectors],
        [keep(tall), thin], unit,
    )
    gates = [mixed] * (dp_count // 2) + [cross_mixed] * (dp_count // 2)
    sources = ffn_sources_of(core_list([after(*pair) for pair in zip(ffn_near, gates)]))
    hidden = pieces * model
    (
        layer_out, grad_sum, grad_cross_out, grad_cross_mixed, ffn_sums, bias_sums, *ffn_grads
    ) = call(
        functools.partial(ffn_kernel, len(sources), depth), "ffn", [spot],
        [unit_two, inverse_two, cotangent, cross_weights, vectors],
        [wide, keep(tall), keep(wide), keep(wide), small, small, *grad_outs(2 * hidden)],
        (5 * pieces + 1) * unit, sources,
        [
            pltpu.VMEM((model, hidden), LOW), pltpu.VMEM((hidden, model), LOW),
            pltpu.VMEM((total, hidden), LOW), pltpu.VMEM((total, model), LOW),
            pltpu.VMEM((total, hidden), LOW),
            pltpu.VMEM((STEP_ROWS, hidden), FULL), wait_two,
        ],
    )
    if not aligned:
        first, second = ffn_grads[0][:, :hidden], ffn_grads[0][:, hidden:]
        second = second.reshape(model, pieces, model).transpose(1, 0, 2)
        second = second.reshape(count, pieces, rows, model).transpose(0, 2, 1, 3)
        ffn_grads = [jnp.concatenate([first, second.reshape(model, -1)], axis=1)]
    sent, kept = split_core(ffn_grads)
    ffn_moved = exchange(sent, 1)
    cross_dq, cross_dk, cross_dv = call(
        cross_backward_kernel, "cross_backward", [row_starts, col_starts],
        [cross_queries, cross_keys, cross_values, after(grad_cross_mixed, sent), cross_log],
        [keep(wide), keep(wide), keep(wide)], 5 * attend,
    )
    fast = aligned and dp_count == 4 and depth == 4
    ffn_moved = after(ffn_moved, cross_dq)
    if fast:
        pair = (2, depth, rows, hidden)
        keep_first, send_first, keep_second, send_second = call(
            functools.partial(fold_halves_kernel, depth), "fold_halves", [spot], [kept, ffn_moved],
            [(pair, FULL), (pair, LOW), (pair, FULL), (pair, LOW)], 1,
        )
        ffn_sends = [send_first, send_second]
        got_first = exchange(send_first, 2 * fsdp_count)
        got_second = exchange(send_second, fsdp_count)
    else:
        ffn_kept, ffn_sends = fold_core(spot, kept, ffn_moved)
        ffn_moved = move_square(ffn_sends)
    first_sum, self_low, grad_mixed, cross_vector, encoded_grad, *cross_grads = call(
        cross_grads_kernel, "cross_grads", [spot],
        [
            after(cross_dq, *ffn_sends), cross_dk, cross_dv, cross_weights, vectors, grad_sum,
            unit_one, inverse_one, encoded, cross_mixed, grad_cross_out,
        ],
        [keep(tall), keep(wide), keep(wide), small, tall, *grad_outs(4 * model)], 8 * unit,
    )
    sent, kept = split_core(cross_grads)
    ffn_sends = [sent]
    if fast:
        half = (depth, rows, hidden)
        own_first, send_first, own_second, send_second = call(
            fold_pairs_kernel, "fold_pairs", [],
            [keep_first, after(got_first, sent), keep_second, got_second],
            [(half, FULL), (half, LOW), (half, FULL), (half, LOW)], 1,
        )
        ffn_sends = [send_first, send_second]
        got_first = exchange(send_first, fsdp_count)
        got_second = exchange(send_second, 2 * fsdp_count)
    cross_moved = exchange(after(sent, *ffn_sends), 1)
    cross_kept, cross_sends = fold_core(spot, kept, cross_moved)
    cross_moved = move_square(cross_sends)
    self_dq, self_dk, self_dv, *self_grads = call(
        self_backward_kernel, "self_backward", [spot, row_starts],
        [
            queries, keys, values, after(grad_mixed, *cross_sends, *ffn_sends), self_sums,
            tokens, mixed, self_low, cross_vector, ffn_sums, bias_sums,
        ],
        [keep(wide), keep(wide), keep(wide), *grad_outs(4 * model + 128)],
        5 * attend + 4 * unit, (), [pltpu.VMEM((128, model), FULL)],
    )
    sent, kept = split_core(self_grads)
    if fast:
        wide_pair = (2, rows, 2 * hidden + 4 * model)
        layer_keep, layer_send = call(
            functools.partial(fold_layers_kernel, depth), "fold_layers", [spot],
            [own_first, after(got_first, sent), own_second, got_second, cross_kept, *cross_moved],
            [(wide_pair, FULL), (wide_pair, LOW)], 1,
        )
        ffn_sends = [layer_send]
        layer_got = exchange(layer_send, 4)
        self_moved = exchange(after(sent, layer_send), 1)
    else:
        self_moved = exchange(sent, 1)
        ffn_kept, ffn_sends = fold_square(spot, ffn_kept, [after(item, sent) for item in ffn_moved])
        ffn_moved = move_layers(ffn_sends)
    (tokens_grad,) = call(
        tokens_grad_kernel, "tokens_grad", [],
        [after(self_dq, *ffn_sends), self_dk, self_dv, first_sum, self_weights], [tall], 3 * unit,
    )
    self_kept, self_sends = fold_core(spot, kept, after(self_moved, tokens_grad))
    self_moved = move_square(self_sends)
    grad_scale = 1.0 / math.sqrt(total * count)
    if fast:
        wide_row = wide_pair[1:]
        layer_own, layer_send = call(
            fold_last_kernel, "fold_last", [], [layer_keep, after(layer_got, *self_sends)],
            [(wide_row, FULL), (wide_row, LOW)], 1,
        )
        layer_got = exchange(layer_send, 2)
        kinds = [FULL, FULL, FULL, LOW]
        ffn_out_state = (ffn_out_master, ffn_out_first, ffn_out_second)
        ffn_in_state = (ffn_in_master, ffn_in_first, ffn_in_second)
        ffn_new = call(
            functools.partial(ffn_update_kernel, grad_scale), "ffn_update", [],
            [layer_own, layer_got, *ffn_in_state, *ffn_out_state],
            [(ffn_in_master.shape, kind) for kind in kinds]
            + [(ffn_out_master.shape, kind) for kind in kinds], 1,
        )
        self_kept, self_sends = fold_square(
            spot, self_kept, [after(item, layer_send) for item in self_moved]
        )
        self_moved = move_layers(self_sends)
        states = [
            qkv_master, qkv_first, qkv_second, out_master, out_first, out_second,
            vector_master.T, vector_first.T, vector_second.T,
        ]
        final_new = call(
            functools.partial(final_update_kernel, grad_scale, 2 * hidden), "final_update", [],
            [layer_own, layer_got, self_kept, *self_moved, *states],
            [(item.shape, kind) for item in states[::3] for kind in kinds], 1,
        )
        return (
            layer_out, tokens_grad, encoded_grad, *final_new[:8], *ffn_new,
            *[item.T for item in final_new[8:]],
        )
    cross_kept, cross_sends = fold_square(
        spot, cross_kept, [after(item, *self_sends) for item in cross_moved]
    )
    cross_moved = move_layers(cross_sends)
    ffn_total = add_all(ffn_kept, ffn_moved)
    cross_total = add_all(cross_kept, cross_moved)
    self_kept, self_sends = fold_square(
        spot, self_kept, [after(item, *cross_sends) for item in self_moved]
    )
    self_moved = move_layers(self_sends)
    self_total = add_all(self_kept, self_moved)

    def block(values, index):
        return values[:, index * model : (index + 1) * model]

    summed_qkv = jnp.stack(
        [block(self_total, i) for i in range(3)] + [block(cross_total, i) for i in range(3)]
    )
    summed_out = jnp.stack([block(self_total, 3), block(cross_total, 3)])
    summed_ffn_in = ffn_total[:, :hidden]
    summed_ffn_out = (
        ffn_total[:, hidden:].reshape(rows, pieces, model).transpose(1, 0, 2).reshape(-1, model)
    )
    summed_vector = self_total[:, 4 * model : 4 * model + vector_master.shape[0]].T
    qkv_first_new, qkv_second_new, qkv_master_new, qkv_copy = adamw(
        qkv_master, summed_qkv * grad_scale, qkv_first, qkv_second, 0.04
    )
    out_first_new, out_second_new, out_master_new, out_copy = adamw(
        out_master, summed_out * grad_scale, out_first, out_second, 0.3
    )
    ffn_in_first_new, ffn_in_second_new, ffn_in_master_new, ffn_in_copy = adamw(
        ffn_in_master, summed_ffn_in * grad_scale, ffn_in_first, ffn_in_second, 0.04
    )
    ffn_out_first_new, ffn_out_second_new, ffn_out_master_new, ffn_out_copy = adamw(
        ffn_out_master, summed_ffn_out * grad_scale, ffn_out_first, ffn_out_second, 0.02
    )
    vector_first_new, vector_second_new, vector_master_new, vector_copy = adamw(
        vector_master, summed_vector * grad_scale, vector_first, vector_second, 0.35
    )
    return (
        layer_out,
        tokens_grad,
        encoded_grad,
        qkv_first_new,
        qkv_second_new,
        qkv_master_new,
        qkv_copy,
        out_first_new,
        out_second_new,
        out_master_new,
        out_copy,
        ffn_in_first_new,
        ffn_in_second_new,
        ffn_in_master_new,
        ffn_in_copy,
        ffn_out_first_new,
        ffn_out_second_new,
        ffn_out_master_new,
        ffn_out_copy,
        vector_first_new,
        vector_second_new,
        vector_master_new,
        vector_copy,
    )


def solution(mesh):
    return jax.shard_map(
        body,
        mesh=mesh,
        in_specs=(
            P(("dp", "fsdp"), None),
            P(("dp", "fsdp"), None),
            P(("dp", "fsdp"), None),
            P(("dp", "fsdp"), None),
            P(("dp", "fsdp"), None),
            P(None, ("dp", "fsdp"), None),
            P(None, ("dp", "fsdp"), None),
            P(None, ("dp", "fsdp"), None),
            P(None, ("dp", "fsdp"), None),
            P(None, ("dp", "fsdp"), None),
            P(None, ("dp", "fsdp"), None),
            P(("dp", "fsdp"), None),
            P(("dp", "fsdp"), None),
            P(("dp", "fsdp"), None),
            P(("dp", "fsdp"), None),
            P(("dp", "fsdp"), None),
            P(("dp", "fsdp"), None),
            P(None, ("dp", "fsdp")),
            P(None, ("dp", "fsdp")),
            P(None, ("dp", "fsdp")),
        ),
        out_specs=(
            P(("dp", "fsdp"), None),
            P(("dp", "fsdp"), None),
            P(("dp", "fsdp"), None),
            P(None, ("dp", "fsdp"), None),
            P(None, ("dp", "fsdp"), None),
            P(None, ("dp", "fsdp"), None),
            P(None, ("dp", "fsdp"), None),
            P(None, ("dp", "fsdp"), None),
            P(None, ("dp", "fsdp"), None),
            P(None, ("dp", "fsdp"), None),
            P(None, ("dp", "fsdp"), None),
            P(("dp", "fsdp"), None),
            P(("dp", "fsdp"), None),
            P(("dp", "fsdp"), None),
            P(("dp", "fsdp"), None),
            P(("dp", "fsdp"), None),
            P(("dp", "fsdp"), None),
            P(("dp", "fsdp"), None),
            P(("dp", "fsdp"), None),
            P(None, ("dp", "fsdp")),
            P(None, ("dp", "fsdp")),
            P(None, ("dp", "fsdp")),
            P(None, ("dp", "fsdp")),
        ),
        check_vma=False,
    )
```

profile of v0, /device:TPU:0, one launch (start us, length us, event | category | flops | bytes accessed | tf_op | source)
XLA Modules:
  0.0 192.1 jit_solution(16622561825570332583)
XLA Ops:
  1.4 1.0 convert_element_type.25
  2.4 4.1 %collective-permute-start.1 = (bf16[16,1664]{1,0:T(8,128)(2,1)S(1)}, bf16[16,1664]{1,0:T(8,128)(2,1)S(1)}, u32[]{:S(2)}, u32[]{:S(2)}) collective-permute-start(bf16[16,1664]{1,0:T(8,128)(2,1)S(1)} %fusion.1), channel_id=1, source_target_pairs={{0,4},{1,5},{2,6},{3,7},{4,0},{5,1},{6,2},{7,3},{8,12},{9,13},{10,... | collective-permute-start | bytes 159752 | tf_op jit(solution)/shard_map/ppermute | solution.py:704
  6.5 1.6 collective-permute-start
  8.1 0.8 convert_element_type.24
  9.0 0.9 convert_element_type.28
  9.9 0.9 convert_element_type.29
  11.0 3.1 %collective-permute-done.2 = bf16[16,1664]{1,0:T(8,128)(2,1)S(1)} collective-permute-done((bf16[16,1664]{1,0:T(8,128)(2,1)S(1)}, bf16[16,1664]{1,0:T(8,128)(2,1)S(1)}, u32[]{:S(2)}, u32[]{:S(2)}) %collective-permute-start.2) | collective-permute-done | bytes 53280 | tf_op jit(solution)/shard_map/ppermute | solution.py:704
  14.4 2.5 %collective-permute-start.7 = (bf16[4,16,1664]{2,1,0:T(8,128)(2,1)S(1)}, bf16[4,16,1664]{2,1,0:T(8,128)(2,1)S(1)}, u32[]{:S(2)}, u32[]{:S(2)}) collective-permute-start(bf16[4,16,1664]{2,1,0:T(8,128)(2,1)S(1)} %pad_maximum_fusion.2.rest_0_), channel_id=1, source_target_pairs={{0,24},{1,25},{2,26},{3,27},{4,28},{5,29},{6,30},{7,31},{8,16},{9,... | collective-permute-start | bytes 638984 | tf_op jit(solution)/shard_map/ppermute | solution.py:704
  18.6 1.3 collective-permute-start.19
  20.0 3.6 %collective-permute-done.19 = bf16[1,16,4096]{2,1,0:T(8,128)(2,1)S(1)} collective-permute-done((bf16[1,16,4096]{2,1,0:T(8,128)(2,1)S(1)}, bf16[1,16,4096]{2,1,0:T(8,128)(2,1)S(1)}, u32[]{:S(2)}, u32[]{:S(2)}) %collective-permute-start.19) | collective-permute-done | bytes 131104 | tf_op jit(solution)/shard_map/ppermute | solution.py:704
  24.4 3.1 %collective-permute-done.6.rest_2_ = bf16[4,16,1664]{2,1,0:T(8,128)(2,1)S(1)} collective-permute-done((bf16[4,16,1664]{2,1,0:T(8,128)(2,1)S(1)}, bf16[4,16,1664]{2,1,0:T(8,128)(2,1)S(1)}, u32[]{:S(2)}, u32[]{:S(2)}) %collective-permute-start.6) | collective-permute-done | bytes 213024 | tf_op jit(solution)/shard_map/ppermute | solution.py:704
  28.0 4.4 %collective-permute-done.4 = bf16[2,16,2560]{2,1,0:T(8,128)(2,1)S(1)} collective-permute-done((bf16[2,16,2560]{2,1,0:T(8,128)(2,1)S(1)}, bf16[2,16,2560]{2,1,0:T(8,128)(2,1)S(1)}, u32[]{:S(2)}, u32[]{:S(2)}) %collective-permute-start.4) | collective-permute-done | bytes 163872 | tf_op jit(solution)/shard_map/ppermute | solution.py:704
  32.6 2.5 %collective-permute-start.14 = (bf16[4,16,2560]{2,1,0:T(8,128)(2,1)S(1)}, bf16[4,16,2560]{2,1,0:T(8,128)(2,1)S(1)}, u32[]{:S(2)}, u32[]{:S(2)}) collective-permute-start(bf16[4,16,2560]{2,1,0:T(8,128)(2,1)S(1)} %pad_maximum_fusion.rest_0_), channel_id=1, source_target_pairs={{0,24},{1,25},{2,26},{3,27},{4,28},{5,29},{6,30},{7,31},{8,16},{9,... | collective-permute-start | bytes 983048 | tf_op jit(solution)/shard_map/ppermute | solution.py:704
  36.2 14.6 %self_forward.1 = (bf16[512,1664]{1,0:T(8,128)(2,1)S(1)}, f32[24,512]{1,0:T(8,128)S(1)}, bf16[1024,512]{1,0:T(8,128)(2,1)S(1)}, bf16[1024,512]{1,0:T(8,128)(2,1)...) custom-call(s32[1]{0:T(128)} %bitcast.place, ...), custom_call_target="tpu_custom_call" | custom-call | flops 6979321856 | bytes 2752512 | tf_op jit(solution)/shard_map/self_forward/pallas_call | solution.py:671
  52.5 2.6 %collective-permute-start.22 = (bf16[4,16,4096]{2,1,0:T(8,128)(2,1)S(1)}, bf16[4,16,4096]{2,1,0:T(8,128)(2,1)S(1)}, u32[]{:S(2)}, u32[]{:S(2)}) collective-permute-start(bf16[4,16,4096]{2,1,0:T(8,128)(2,1)S(1)} %constant_dynamic-update-slice_fusion.rest_0_), channel_id=1, source_target_pairs={{0,16},{1,17},{2,18},{3,19},{4,20},{5,21},{6,22},{7,23},{8,24},{9,... | collective-permute-start | bytes 1572872 | tf_op jit(solution)/shard_map/ppermute | solution.py:704
  55.1 6.8 %cross_project.1 = (bf16[512,2560]{1,0:T(8,128)(2,1)S(1)}, f32[1024,512]{1,0:T(8,128)S(1)}, f32[1024,1]{1,0:T(8,128)S(1)}, bf16[1024,512]{1,0:T(8,128)(2,1)S(1)}...) custom-call(s32[1]{0:T(128)} %bitcast.place, bf16[1024,512]{1,0:T(8,128)(2,1)S(1)} %copy-done.17, ...), custom_call_target="tpu_custom_call" | custom-call | flops 2147483648 | bytes 5816320 | tf_op jit(solution)/shard_map/cross_project/pallas_call | solution.py:671
  62.0 4.0 %collective-permute-done.21.rest_1_ = bf16[4,16,4096]{2,1,0:T(8,128)(2,1)S(1)} collective-permute-done((bf16[4,16,4096]{2,1,0:T(8,128)(2,1)S(1)}, bf16[4,16,4096]{2,1,0:T(8,128)(2,1)S(1)}, u32[]{:S(2)}, u32[]{:S(2)}) %collective-permute-start.21) | collective-permute-done | bytes 524320 | tf_op jit(solution)/shard_map/ppermute | solution.py:704
  66.0 1.3 collective-permute-start.23
  67.5 8.6 %cross_attend.1 = (bf16[1024,512]{1,0:T(8,128)(2,1)S(1)}, f32[10,2,1,1024]{3,2,1,0:T(1,128)S(1)}) custom-call(s32[11]{0:T(128)S(1)} %convert_reduce_fusion.1.row_starts, s32[11]{0:T(128)S(1)} %convert_reduce_fusion.col_starts, bf16[1024,512]{1,0:T(8,128)(2,1)S(1)} %get-tuple-element.145.queries, bf16[1024,512]{1,0:T(8,128)(2,1)S(1)} %get-tuple-element.146.keys, ...), custom_call_target="tpu_custom_call" | custom-call | flops 5368709120 | bytes 3145728 | tf_op jit(solution)/shard_map/cross_attend/pallas_call | solution.py:671
  76.1 1.3 collective-permute-start.25
  77.5 1.5 collective-permute-done.23.rest_3_
  79.1 1.4 cross_finish.1
  81.0 22.6 %ffn.1 = (bf16[1024,512]{1,0:T(8,128)(2,1)}, f32[1024,512]{1,0:T(8,128)S(1)}, bf16[1024,512]{1,0:T(8,128)(2,1)S(1)}, bf16[1024,512]{1,0:T(8,128)(2,1)S(1)}, f32[...) custom-call(s32[1]{0:T(128)} %bitcast.place, ...), custom_call_target="tpu_custom_call" | custom-call | flops 11274289152 | bytes 10014720 | tf_op jit(solution)/shard_map/ffn/pallas_call | solution.py:671
  103.6 1.0 copy-done.22
  104.7 1.2 copy-done.23
  105.9 12.3 %cross_backward.1 = (bf16[1024,512]{1,0:T(8,128)(2,1)S(1)}, bf16[1024,512]{1,0:T(8,128)(2,1)S(1)}, bf16[1024,512]{1,0:T(8,128)(2,1)S(1)}) custom-call(s32[11]{0:T(128)S(1)} %convert_reduce_fusion.1.row_starts, s32[11]{0:T(128)S(1)} %convert_reduce_fusion.col_starts, bf16[1024,512]{1,0:T(8,128)(2,1)S(1)} %get-tuple-element.145.queries, ...), custom_call_target="tpu_custom_call" | custom-call | flops 13421772800 | bytes 4276224 | tf_op jit(solution)/shard_map/cross_backward/pallas_call | solution.py:671
  118.7 2.2 %collective-permute-start.29 = (bf16[2,4,16,2048]{3,2,1,0:T(8,128)(2,1)S(1)}, bf16[2,4,16,2048]{3,2,1,0:T(8,128)(2,1)S(1)}, u32[]{:S(2)}, u32[]{:S(2)}) collective-permute-start(bf16[2,4,16,2048]{3,2,1,0:T(8,128)(2,1)S(1)} %get-tuple-element.170), channel_id=1, source_target_pairs={{0,16},{1,17},{2,18},{3,19},{4,20},{5,21},{6,22},{7,23},{8,24},{9,... | collective-permute-start | bytes 1572872 | tf_op jit(solution)/shard_map/ppermute | solution.py:704
  120.9 2.2 %collective-permute-start.30 = (bf16[2,4,16,2048]{3,2,1,0:T(8,128)(2,1)S(1)}, bf16[2,4,16,2048]{3,2,1,0:T(8,128)(2,1)S(1)}, u32[]{:S(2)}, u32[]{:S(2)}) collective-permute-start(bf16[2,4,16,2048]{3,2,1,0:T(8,128)(2,1)S(1)} %get-tuple-element.171), channel_id=1, source_target_pairs={{0,8},{1,9},{2,10},{3,11},{4,12},{5,13},{6,14},{7,15},{8,0},{9,1},... | collective-permute-start | bytes 1572872 | tf_op jit(solution)/shard_map/ppermute | solution.py:704
  123.1 6.5 %cross_grads.1 = (f32[1024,512]{1,0:T(8,128)S(1)}, bf16[1024,512]{1,0:T(8,128)(2,1)S(1)}, bf16[1024,512]{1,0:T(8,128)(2,1)S(1)}, f32[8,512]{1,0:T(8,128)S(1)}, f...) custom-call(s32[1]{0:T(128)} %bitcast.place, ...), custom_call_target="tpu_custom_call" | custom-call | flops 4294967296 | bytes 13160448 | tf_op jit(solution)/shard_map/cross_grads/pallas_call | solution.py:671
  129.6 3.7 %collective-permute-done.29.got_first = bf16[2,4,16,2048]{3,2,1,0:T(8,128)(2,1)S(1)} collective-permute-done((bf16[2,4,16,2048]{3,2,1,0:T(8,128)(2,1)S(1)}, bf16[2,4,16,2048]{3,2,1,0:T(8,128)(2,1)S(1)}, u32[]{:S(2)}, u32[]{:S(2)}) %collective-permute-start.29) | collective-permute-done | bytes 524320 | tf_op jit(solution)/shard_map/ppermute | solution.py:704
  133.3 1.2 collective-permute-done.30.got_second
  135.5 0.9 collective-permute-start.33
  136.4 1.1 collective-permute-done.31.received
  137.7 0.8 collective-permute-start.34
  138.4 0.8 collective-permute-start.35
  139.3 2.0 %collective-permute-start.36 = (bf16[4,16,2048]{2,1,0:T(8,128)(2,1)S(1)}, bf16[4,16,2048]{2,1,0:T(8,128)(2,1)S(1)}, u32[]{:S(2)}, u32[]{:S(2)}) collective-permute-start(bf16[4,16,2048]{2,1,0:T(8,128)(2,1)S(1)} %get-tuple-element.189), channel_id=1, source_target_pairs={{0,24},{1,25},{2,26},{3,27},{4,28},{5,29},{6,30},{7,31},{8,16},{9,... | collective-permute-start | bytes 786440 | tf_op jit(solution)/shard_map/ppermute | solution.py:704
  141.2 16.9 %self_backward.1 = (bf16[1024,512]{1,0:T(8,128)(2,1)S(1)}, bf16[1024,512]{1,0:T(8,128)(2,1)S(1)}, bf16[1024,512]{1,0:T(8,128)(2,1)S(1)}, bf16[16,16,2176]{2,1,0:T(8,128)(2,1)S(1)}, bf16[16,16,2176]{2,1,0:T(8,128)(2,1)S(1)}) custom-call(s32[1]{0:T(128)} %bitcast.place, s32[11]{0:T(128)S(1)} %convert_reduce_fusion.1.row_starts, ...), custom_call_target="tpu_custom_call" | custom-call | flops 15569256448 | bytes 7471104 | tf_op jit(solution)/shard_map/self_backward/pallas_call | solution.py:671
  158.5 1.9 collective-permute-start.37
  160.4 3.3 %tokens_grad.1 = f32[1024,512]{1,0:T(8,128)} custom-call(bf16[1024,512]{1,0:T(8,128)(2,1)S(1)} %get-tuple-element.203.dq, bf16[1024,512]{1,0:T(8,128)(2,1)S(1)} %get-tuple-element.204.dk, bf16[1024,512]{1,0:T(8,128)(2,1)S(1)} %get-tuple-element.205.dv, f32[1024,512]{1,0:T(8,128)S(1)} %get-tuple-element.206.first_sum, ...), custom_call_target="tpu_custom_call" | custom-call | flops 1610612736 | bytes 6946816 | tf_op jit(solution)/shard_map/tokens_grad/pallas_call | solution.py:671
  164.1 0.9 collective-permute-start.40
  165.8 1.9 %collective-permute-start.42 = (bf16[4,16,2176]{2,1,0:T(8,128)(2,1)S(1)}, bf16[4,16,2176]{2,1,0:T(8,128)(2,1)S(1)}, u32[]{:S(2)}, u32[]{:S(2)}) collective-permute-start(bf16[4,16,2176]{2,1,0:T(8,128)(2,1)S(1)} %get-tuple-element.215), channel_id=1, source_target_pairs={{0,24},{1,25},{2,26},{3,27},{4,28},{5,29},{6,30},{7,31},{8,16},{9,... | collective-permute-start | bytes 835592 | tf_op jit(solution)/shard_map/ppermute | solution.py:704
  167.7 11.6 %collective-permute-done.37.got = bf16[2,16,6144]{2,1,0:T(8,128)(2,1)S(1)} collective-permute-done((bf16[2,16,6144]{2,1,0:T(8,128)(2,1)S(1)}, bf16[2,16,6144]{2,1,0:T(8,128)(2,1)S(1)}, u32[]{:S(2)}, u32[]{:S(2)}) %collective-permute-start.37) | collective-permute-done | bytes 393248 | tf_op jit(solution)/shard_map/ppermute | solution.py:704
  179.7 2.1 %collective-permute-start.43 = (bf16[16,2176]{1,0:T(8,128)(2,1)S(1)}, bf16[16,2176]{1,0:T(8,128)(2,1)S(1)}, u32[]{:S(2)}, u32[]{:S(2)}) collective-permute-start(bf16[16,2176]{1,0:T(8,128)(2,1)S(1)} %get-tuple-element.224), channel_id=1, source_target_pairs={{0,2},{1,3},{2,0},{3,1},{4,6},{5,7},{6,4},{7,5},{8,10},{9,11},{10,... | collective-permute-start | bytes 208904 | tf_op jit(solution)/shard_map/ppermute | solution.py:704
  182.4 1.8 collective-permute-start.45
  184.2 4.4 %collective-permute-done.39.got = bf16[16,6144]{1,0:T(8,128)(2,1)S(1)} collective-permute-done((bf16[16,6144]{1,0:T(8,128)(2,1)S(1)}, bf16[16,6144]{1,0:T(8,128)(2,1)S(1)}, u32[]{:S(2)}, u32[]{:S(2)}) %collective-permute-start.39) | collective-permute-done | bytes 196640 | tf_op jit(solution)/shard_map/ppermute | solution.py:704
  188.6 1.1 ffn_update.1
  189.9 0.9 collective-permute-done.45.rest_2_
  190.8 1.1 final_update.1
  (138 shorter events, 12.1 us)
Async XLA Ops:
  1.4 34.8 %copy-start.17 = (bf16[1024,512]{1,0:T(8,128)(2,1)S(1)}, bf16[1024,512]{1,0:T(8,128)(2,1)}, u32[]{:S(2)}) copy-start(bf16[1024,512]{1,0:T(8,128)(2,1)} %tokens.4) | copy-start | bytes 3145732
  2.4 8.5 %collective-permute-start.1 = (bf16[16,1664]{1,0:T(8,128)(2,1)S(1)}, bf16[16,1664]{1,0:T(8,128)(2,1)S(1)}, u32[]{:S(2)}, u32[]{:S(2)}) collective-permute-start(bf16[16,1664]{1,0:T(8,128)(2,1)S(1)} %fusion.1), channel_id=1, source_target_pairs={{0,4},{1,5},{2,6},{3,7},{4,0},{5,1},{6,2},{7,3},{8,12},{9,13},{10,... | collective-permute-start | bytes 159752 | tf_op jit(solution)/shard_map/ppermute | solution.py:704
  6.5 4.4 %collective-permute-start = (bf16[16,1664]{1,0:T(8,128)(2,1)S(1)}, bf16[16,1664]{1,0:T(8,128)(2,1)S(1)}, u32[]{:S(2)}, u32[]{:S(2)}) collective-permute-start(bf16[16,1664]{1,0:T(8,128)(2,1)S(1)} %fusion.1), channel_id=1, source_target_pairs={{0,2},{1,3},{2,0},{3,1},{4,6},{5,7},{6,4},{7,5},{8,10},{9,11},{10,... | collective-permute-start | bytes 159752 | tf_op jit(solution)/shard_map/ppermute | solution.py:704
  8.1 5.9 %collective-permute-start.2 = (bf16[16,1664]{1,0:T(8,128)(2,1)S(1)}, bf16[16,1664]{1,0:T(8,128)(2,1)S(1)}, u32[]{:S(2)}, u32[]{:S(2)}) collective-permute-start(bf16[16,1664]{1,0:T(8,128)(2,1)S(1)} %fusion.1), channel_id=1, source_target_pairs={{0,6},{1,7},{2,4},{3,5},{4,2},{5,3},{6,0},{7,1},{8,14},{9,15},{10,... | collective-permute-start | bytes 159752 | tf_op jit(solution)/shard_map/ppermute | solution.py:704
  14.1 4.5 %collective-permute-start.3 = (bf16[1,16,2560]{2,1,0:T(8,128)(2,1)S(1)}, bf16[1,16,2560]{2,1,0:T(8,128)(2,1)S(1)}, u32[]{:S(2)}, u32[]{:S(2)}) collective-permute-start(bf16[1,16,2560]{2,1,0:T(8,128)(2,1)S(1)} %bitcast.54), channel_id=1, source_target_pairs={{0,2},{1,3},{2,0},{3,1},{4,6},{5,7},{6,4},{7,5},{8,10},{9,11},{10,... | collective-permute-start | bytes 245768 | tf_op jit(solution)/shard_map/ppermute | solution.py:704
  14.3 18.3 %collective-permute-start.8 = (bf16[4,16,1664]{2,1,0:T(8,128)(2,1)S(1)}, bf16[4,16,1664]{2,1,0:T(8,128)(2,1)S(1)}, u32[]{:S(2)}, u32[]{:S(2)}) collective-permute-start(bf16[4,16,1664]{2,1,0:T(8,128)(2,1)S(1)} %pad_maximum_fusion.2.rest_0_), channel_id=1, source_target_pairs={{0,1},{1,0},{2,3},{3,2},{4,5},{5,4},{6,7},{7,6},{8,9},{9,8},{10,11... | collective-permute-start | bytes 638984 | tf_op jit(solution)/shard_map/ppermute | solution.py:704
  14.4 10.0 %collective-permute-start.7 = (bf16[4,16,1664]{2,1,0:T(8,128)(2,1)S(1)}, bf16[4,16,1664]{2,1,0:T(8,128)(2,1)S(1)}, u32[]{:S(2)}, u32[]{:S(2)}) collective-permute-start(bf16[4,16,1664]{2,1,0:T(8,128)(2,1)S(1)} %pad_maximum_fusion.2.rest_0_), channel_id=1, source_target_pairs={{0,24},{1,25},{2,26},{3,27},{4,28},{5,29},{6,30},{7,31},{8,16},{9,... | collective-permute-start | bytes 638984 | tf_op jit(solution)/shard_map/ppermute | solution.py:704
  16.9 10.6 %collective-permute-start.6 = (bf16[4,16,1664]{2,1,0:T(8,128)(2,1)S(1)}, bf16[4,16,1664]{2,1,0:T(8,128)(2,1)S(1)}, u32[]{:S(2)}, u32[]{:S(2)}) collective-permute-start(bf16[4,16,1664]{2,1,0:T(8,128)(2,1)S(1)} %pad_maximum_fusion.2.rest_0_), channel_id=1, source_target_pairs={{0,16},{1,17},{2,18},{3,19},{4,20},{5,21},{6,22},{7,23},{8,24},{9,... | collective-permute-start | bytes 638984 | tf_op jit(solution)/shard_map/ppermute | solution.py:704
  17.4 10.2 %collective-permute-start.5 = (bf16[4,16,1664]{2,1,0:T(8,128)(2,1)S(1)}, bf16[4,16,1664]{2,1,0:T(8,128)(2,1)S(1)}, u32[]{:S(2)}, u32[]{:S(2)}) collective-permute-start(bf16[4,16,1664]{2,1,0:T(8,128)(2,1)S(1)} %pad_maximum_fusion.2.rest_0_), channel_id=1, source_target_pairs={{0,8},{1,9},{2,10},{3,11},{4,12},{5,13},{6,14},{7,15},{8,0},{9,1},... | collective-permute-start | bytes 638984 | tf_op jit(solution)/shard_map/ppermute | solution.py:704
  18.6 5.0 %collective-permute-start.19 = (bf16[1,16,4096]{2,1,0:T(8,128)(2,1)S(1)}, bf16[1,16,4096]{2,1,0:T(8,128)(2,1)S(1)}, u32[]{:S(2)}, u32[]{:S(2)}) collective-permute-start(bf16[1,16,4096]{2,1,0:T(8,128)(2,1)S(1)} %bitcast.52), channel_id=1, source_target_pairs={{0,2},{1,3},{2,0},{3,1},{4,6},{5,7},{6,4},{7,5},{8,10},{9,11},{10,... | collective-permute-start | bytes 393224 | tf_op jit(solution)/shard_map/ppermute | solution.py:704
  23.6 8.9 %collective-permute-start.4 = (bf16[2,16,2560]{2,1,0:T(8,128)(2,1)S(1)}, bf16[2,16,2560]{2,1,0:T(8,128)(2,1)S(1)}, u32[]{:S(2)}, u32[]{:S(2)}) collective-permute-start(bf16[2,16,2560]{2,1,0:T(8,128)(2,1)S(1)} %pad_maximum_fusion.3), channel_id=1, source_target_pairs={{0,4},{1,5},{2,6},{3,7},{4,0},{5,1},{6,2},{7,3},{8,12},{9,13},{10,... | collective-permute-start | bytes 491528 | tf_op jit(solution)/shard_map/ppermute | solution.py:704
  24.3 10.8 %collective-permute-start.11 = (bf16[4,16,1664]{2,1,0:T(8,128)(2,1)S(1)}, bf16[4,16,1664]{2,1,0:T(8,128)(2,1)S(1)}, u32[]{:S(2)}, u32[]{:S(2)}) collective-permute-start(bf16[4,16,1664]{2,1,0:T(8,128)(2,1)S(1)} %collective-permute-done.7.rest_3_), channel_id=1, source_target_pairs={{0,1},{1,0},{2,3},{3,2},{4,5},{5,4},{6,7},{7,6},{8,9},{9,8},{10,11... | collective-permute-start | bytes 638984 | tf_op jit(solution)/shard_map/ppermute | solution.py:704
  27.5 8.1 %collective-permute-start.10 = (bf16[4,16,1664]{2,1,0:T(8,128)(2,1)S(1)}, bf16[4,16,1664]{2,1,0:T(8,128)(2,1)S(1)}, u32[]{:S(2)}, u32[]{:S(2)}) collective-permute-start(bf16[4,16,1664]{2,1,0:T(8,128)(2,1)S(1)} %collective-permute-done.6.rest_2_), channel_id=1, source_target_pairs={{0,1},{1,0},{2,3},{3,2},{4,5},{5,4},{6,7},{7,6},{8,9},{9,8},{10,11... | collective-permute-start | bytes 638984 | tf_op jit(solution)/shard_map/ppermute | solution.py:704
  27.6 8.6 %collective-permute-start.9 = (bf16[4,16,1664]{2,1,0:T(8,128)(2,1)S(1)}, bf16[4,16,1664]{2,1,0:T(8,128)(2,1)S(1)}, u32[]{:S(2)}, u32[]{:S(2)}) collective-permute-start(bf16[4,16,1664]{2,1,0:T(8,128)(2,1)S(1)} %collective-permute-done.5.rest_1_), channel_id=1, source_target_pairs={{0,1},{1,0},{2,3},{3,2},{4,5},{5,4},{6,7},{7,6},{8,9},{9,8},{10,11... | collective-permute-start | bytes 638984 | tf_op jit(solution)/shard_map/ppermute | solution.py:704
  32.5 19.5 %collective-permute-start.20 = (bf16[2,16,4096]{2,1,0:T(8,128)(2,1)S(1)}, bf16[2,16,4096]{2,1,0:T(8,128)(2,1)S(1)}, u32[]{:S(2)}, u32[]{:S(2)}) collective-permute-start(bf16[2,16,4096]{2,1,0:T(8,128)(2,1)S(1)} %pad_maximum_fusion.1), channel_id=1, source_target_pairs={{0,4},{1,5},{2,6},{3,7},{4,0},{5,1},{6,2},{7,3},{8,12},{9,13},{10,... | collective-permute-start | bytes 786440 | tf_op jit(solution)/shard_map/ppermute | solution.py:704
  32.6 18.3 %collective-permute-start.14 = (bf16[4,16,2560]{2,1,0:T(8,128)(2,1)S(1)}, bf16[4,16,2560]{2,1,0:T(8,128)(2,1)S(1)}, u32[]{:S(2)}, u32[]{:S(2)}) collective-permute-start(bf16[4,16,2560]{2,1,0:T(8,128)(2,1)S(1)} %pad_maximum_fusion.rest_0_), channel_id=1, source_target_pairs={{0,24},{1,25},{2,26},{3,27},{4,28},{5,29},{6,30},{7,31},{8,16},{9,... | collective-permute-start | bytes 983048 | tf_op jit(solution)/shard_map/ppermute | solution.py:704
  35.1 15.8 %collective-permute-start.13 = (bf16[4,16,2560]{2,1,0:T(8,128)(2,1)S(1)}, bf16[4,16,2560]{2,1,0:T(8,128)(2,1)S(1)}, u32[]{:S(2)}, u32[]{:S(2)}) collective-permute-start(bf16[4,16,2560]{2,1,0:T(8,128)(2,1)S(1)} %pad_maximum_fusion.rest_0_), channel_id=1, source_target_pairs={{0,16},{1,17},{2,18},{3,19},{4,20},{5,21},{6,22},{7,23},{8,24},{9,... | collective-permute-start | bytes 983048 | tf_op jit(solution)/shard_map/ppermute | solution.py:704
  35.6 15.3 %collective-permute-start.12 = (bf16[4,16,2560]{2,1,0:T(8,128)(2,1)S(1)}, bf16[4,16,2560]{2,1,0:T(8,128)(2,1)S(1)}, u32[]{:S(2)}, u32[]{:S(2)}) collective-permute-start(bf16[4,16,2560]{2,1,0:T(8,128)(2,1)S(1)} %pad_maximum_fusion.rest_0_), channel_id=1, source_target_pairs={{0,8},{1,9},{2,10},{3,11},{4,12},{5,13},{6,14},{7,15},{8,0},{9,1},... | collective-permute-start | bytes 983048 | tf_op jit(solution)/shard_map/ppermute | solution.py:704
  50.8 1.7 collective-permute-start.15
  50.9 4.2 %collective-permute-start.16 = (bf16[4,16,2560]{2,1,0:T(8,128)(2,1)S(1)}, bf16[4,16,2560]{2,1,0:T(8,128)(2,1)S(1)}, u32[]{:S(2)}, u32[]{:S(2)}) collective-permute-start(bf16[4,16,2560]{2,1,0:T(8,128)(2,1)S(1)} %collective-permute-done.12.rest_1_), channel_id=1, source_target_pairs={{0,1},{1,0},{2,3},{3,2},{4,5},{5,4},{6,7},{7,6},{8,9},{9,8},{10,11... | collective-permute-start | bytes 983048 | tf_op jit(solution)/shard_map/ppermute | solution.py:704
  51.5 3.6 %collective-permute-start.17 = (bf16[4,16,2560]{2,1,0:T(8,128)(2,1)S(1)}, bf16[4,16,2560]{2,1,0:T(8,128)(2,1)S(1)}, u32[]{:S(2)}, u32[]{:S(2)}) collective-permute-start(bf16[4,16,2560]{2,1,0:T(8,128)(2,1)S(1)} %collective-permute-done.13.rest_2_), channel_id=1, source_target_pairs={{0,1},{1,0},{2,3},{3,2},{4,5},{5,4},{6,7},{7,6},{8,9},{9,8},{10,11... | collective-permute-start | bytes 983048 | tf_op jit(solution)/shard_map/ppermute | solution.py:704
  51.6 3.5 %collective-permute-start.18 = (bf16[4,16,2560]{2,1,0:T(8,128)(2,1)S(1)}, bf16[4,16,2560]{2,1,0:T(8,128)(2,1)S(1)}, u32[]{:S(2)}, u32[]{:S(2)}) collective-permute-start(bf16[4,16,2560]{2,1,0:T(8,128)(2,1)S(1)} %collective-permute-done.14.rest_3_), channel_id=1, source_target_pairs={{0,1},{1,0},{2,3},{3,2},{4,5},{5,4},{6,7},{7,6},{8,9},{9,8},{10,11... | collective-permute-start | bytes 983048 | tf_op jit(solution)/shard_map/ppermute | solution.py:704
  52.0 14.0 %collective-permute-start.21 = (bf16[4,16,4096]{2,1,0:T(8,128)(2,1)S(1)}, bf16[4,16,4096]{2,1,0:T(8,128)(2,1)S(1)}, u32[]{:S(2)}, u32[]{:S(2)}) collective-permute-start(bf16[4,16,4096]{2,1,0:T(8,128)(2,1)S(1)} %constant_dynamic-update-slice_fusion.rest_0_), channel_id=1, source_target_pairs={{0,8},{1,9},{2,10},{3,11},{4,12},{5,13},{6,14},{7,15},{8,0},{9,1},... | collective-permute-start | bytes 1572872 | tf_op jit(solution)/shard_map/ppermute | solution.py:704
  52.5 24.9 %collective-permute-start.22 = (bf16[4,16,4096]{2,1,0:T(8,128)(2,1)S(1)}, bf16[4,16,4096]{2,1,0:T(8,128)(2,1)S(1)}, u32[]{:S(2)}, u32[]{:S(2)}) collective-permute-start(bf16[4,16,4096]{2,1,0:T(8,128)(2,1)S(1)} %constant_dynamic-update-slice_fusion.rest_0_), channel_id=1, source_target_pairs={{0,16},{1,17},{2,18},{3,19},{4,20},{5,21},{6,22},{7,23},{8,24},{9,... | collective-permute-start | bytes 1572872 | tf_op jit(solution)/shard_map/ppermute | solution.py:704
  66.0 13.1 %collective-permute-start.23 = (bf16[4,16,4096]{2,1,0:T(8,128)(2,1)S(1)}, bf16[4,16,4096]{2,1,0:T(8,128)(2,1)S(1)}, u32[]{:S(2)}, u32[]{:S(2)}) collective-permute-start(bf16[4,16,4096]{2,1,0:T(8,128)(2,1)S(1)} %collective-permute-done.21.rest_1_), channel_id=1, source_target_pairs={{0,16},{1,17},{2,18},{3,19},{4,20},{5,21},{6,22},{7,23},{8,24},{9,... | collective-permute-start | bytes 1572872 | tf_op jit(solution)/shard_map/ppermute | solution.py:704
  67.4 13.1 %collective-permute-start.24 = (bf16[4,16,4096]{2,1,0:T(8,128)(2,1)S(1)}, bf16[4,16,4096]{2,1,0:T(8,128)(2,1)S(1)}, u32[]{:S(2)}, u32[]{:S(2)}) collective-permute-start(bf16[4,16,4096]{2,1,0:T(8,128)(2,1)S(1)} %constant_dynamic-update-slice_fusion.rest_0_), channel_id=1, source_target_pairs={{0,1},{1,0},{2,3},{3,2},{4,5},{5,4},{6,7},{7,6},{8,9},{9,8},{10,11... | collective-permute-start | bytes 1572872 | tf_op jit(solution)/shard_map/ppermute | solution.py:704
  76.1 4.4 %collective-permute-start.25 = (bf16[4,16,4096]{2,1,0:T(8,128)(2,1)S(1)}, bf16[4,16,4096]{2,1,0:T(8,128)(2,1)S(1)}, u32[]{:S(2)}, u32[]{:S(2)}) collective-permute-start(bf16[4,16,4096]{2,1,0:T(8,128)(2,1)S(1)} %collective-permute-done.21.rest_1_), channel_id=1, source_target_pairs={{0,1},{1,0},{2,3},{3,2},{4,5},{5,4},{6,7},{7,6},{8,9},{9,8},{10,11... | collective-permute-start | bytes 1572872 | tf_op jit(solution)/shard_map/ppermute | solution.py:704
  77.4 3.0 %collective-permute-start.26 = (bf16[4,16,4096]{2,1,0:T(8,128)(2,1)S(1)}, bf16[4,16,4096]{2,1,0:T(8,128)(2,1)S(1)}, u32[]{:S(2)}, u32[]{:S(2)}) collective-permute-start(bf16[4,16,4096]{2,1,0:T(8,128)(2,1)S(1)} %collective-permute-done.22.rest_2_), channel_id=1, source_target_pairs={{0,1},{1,0},{2,3},{3,2},{4,5},{5,4},{6,7},{7,6},{8,9},{9,8},{10,11... | collective-permute-start | bytes 1572872 | tf_op jit(solution)/shard_map/ppermute | solution.py:704
  79.1 1.9 collective-permute-start.27
  104.6 13.7 %collective-permute-start.28 = (bf16[16,16,4096]{2,1,0:T(8,128)(2,1)S(1)}, bf16[16,16,4096]{2,1,0:T(8,128)(2,1)S(1)}, u32[]{:S(2)}, u32[]{:S(2)}) collective-permute-start(bf16[16,16,4096]{2,1,0:T(8,128)(2,1)S(1)} %get-tuple-element.164), channel_id=1, source_target_pairs={{0,1},{1,0},{2,3},{3,2},{4,5},{5,4},{6,7},{7,6},{8,9},{9,8},{10,11... | collective-permute-start | bytes 6291464 | tf_op jit(solution)/shard_map/ppermute | solution.py:704
  118.7 14.6 %collective-permute-start.29 = (bf16[2,4,16,2048]{3,2,1,0:T(8,128)(2,1)S(1)}, bf16[2,4,16,2048]{3,2,1,0:T(8,128)(2,1)S(1)}, u32[]{:S(2)}, u32[]{:S(2)}) collective-permute-start(bf16[2,4,16,2048]{3,2,1,0:T(8,128)(2,1)S(1)} %get-tuple-element.170), channel_id=1, source_target_pairs={{0,16},{1,17},{2,18},{3,19},{4,20},{5,21},{6,22},{7,23},{8,24},{9,... | collective-permute-start | bytes 1572872 | tf_op jit(solution)/shard_map/ppermute | solution.py:704
  120.9 13.7 %collective-permute-start.30 = (bf16[2,4,16,2048]{3,2,1,0:T(8,128)(2,1)S(1)}, bf16[2,4,16,2048]{3,2,1,0:T(8,128)(2,1)S(1)}, u32[]{:S(2)}, u32[]{:S(2)}) collective-permute-start(bf16[2,4,16,2048]{3,2,1,0:T(8,128)(2,1)S(1)} %get-tuple-element.171), channel_id=1, source_target_pairs={{0,8},{1,9},{2,10},{3,11},{4,12},{5,13},{6,14},{7,15},{8,0},{9,1},... | collective-permute-start | bytes 1572872 | tf_op jit(solution)/shard_map/ppermute | solution.py:704
  134.7 2.7 %collective-permute-start.31 = (bf16[16,16,2048]{2,1,0:T(8,128)(2,1)S(1)}, bf16[16,16,2048]{2,1,0:T(8,128)(2,1)S(1)}, u32[]{:S(2)}, u32[]{:S(2)}) collective-permute-start(bf16[16,16,2048]{2,1,0:T(8,128)(2,1)S(1)} %get-tuple-element.186), channel_id=1, source_target_pairs={{0,1},{1,0},{2,3},{3,2},{4,5},{5,4},{6,7},{7,6},{8,9},{9,8},{10,11... | collective-permute-start | bytes 3145736 | tf_op jit(solution)/shard_map/ppermute | solution.py:704
  134.8 23.3 %collective-permute-start.32 = (bf16[4,16,2048]{2,1,0:T(8,128)(2,1)S(1)}, bf16[4,16,2048]{2,1,0:T(8,128)(2,1)S(1)}, u32[]{:S(2)}, u32[]{:S(2)}) collective-permute-start(bf16[4,16,2048]{2,1,0:T(8,128)(2,1)S(1)} %get-tuple-element.184), channel_id=1, source_target_pairs={{0,8},{1,9},{2,10},{3,11},{4,12},{5,13},{6,14},{7,15},{8,0},{9,1},... | collective-permute-start | bytes 786440 | tf_op jit(solution)/shard_map/ppermute | solution.py:704
  135.5 22.6 %collective-permute-start.33 = (bf16[4,16,2048]{2,1,0:T(8,128)(2,1)S(1)}, bf16[4,16,2048]{2,1,0:T(8,128)(2,1)S(1)}, u32[]{:S(2)}, u32[]{:S(2)}) collective-permute-start(bf16[4,16,2048]{2,1,0:T(8,128)(2,1)S(1)} %get-tuple-element.185), channel_id=1, source_target_pairs={{0,16},{1,17},{2,18},{3,19},{4,20},{5,21},{6,22},{7,23},{8,24},{9,... | collective-permute-start | bytes 786440 | tf_op jit(solution)/shard_map/ppermute | solution.py:704
  137.7 20.4 %collective-permute-start.34 = (bf16[4,16,2048]{2,1,0:T(8,128)(2,1)S(1)}, bf16[4,16,2048]{2,1,0:T(8,128)(2,1)S(1)}, u32[]{:S(2)}, u32[]{:S(2)}) collective-permute-start(bf16[4,16,2048]{2,1,0:T(8,128)(2,1)S(1)} %get-tuple-element.187), channel_id=1, source_target_pairs={{0,8},{1,9},{2,10},{3,11},{4,12},{5,13},{6,14},{7,15},{8,0},{9,1},... | collective-permute-start | bytes 786440 | tf_op jit(solution)/shard_map/ppermute | solution.py:704
  138.4 19.7 %collective-permute-start.35 = (bf16[4,16,2048]{2,1,0:T(8,128)(2,1)S(1)}, bf16[4,16,2048]{2,1,0:T(8,128)(2,1)S(1)}, u32[]{:S(2)}, u32[]{:S(2)}) collective-permute-start(bf16[4,16,2048]{2,1,0:T(8,128)(2,1)S(1)} %get-tuple-element.188), channel_id=1, source_target_pairs={{0,16},{1,17},{2,18},{3,19},{4,20},{5,21},{6,22},{7,23},{8,24},{9,... | collective-permute-start | bytes 786440 | tf_op jit(solution)/shard_map/ppermute | solution.py:704
  139.3 18.9 %collective-permute-start.36 = (bf16[4,16,2048]{2,1,0:T(8,128)(2,1)S(1)}, bf16[4,16,2048]{2,1,0:T(8,128)(2,1)S(1)}, u32[]{:S(2)}, u32[]{:S(2)}) collective-permute-start(bf16[4,16,2048]{2,1,0:T(8,128)(2,1)S(1)} %get-tuple-element.189), channel_id=1, source_target_pairs={{0,24},{1,25},{2,26},{3,27},{4,28},{5,29},{6,30},{7,31},{8,16},{9,... | collective-permute-start | bytes 786440 | tf_op jit(solution)/shard_map/ppermute | solution.py:704
  158.4 5.3 %collective-permute-start.38 = (bf16[16,16,2176]{2,1,0:T(8,128)(2,1)S(1)}, bf16[16,16,2176]{2,1,0:T(8,128)(2,1)S(1)}, u32[]{:S(2)}, u32[]{:S(2)}) collective-permute-start(bf16[16,16,2176]{2,1,0:T(8,128)(2,1)S(1)} %get-tuple-element.211), channel_id=1, source_target_pairs={{0,1},{1,0},{2,3},{3,2},{4,5},{5,4},{6,7},{7,6},{8,9},{9,8},{10,11... | collective-permute-start | bytes 3342344 | tf_op jit(solution)/shard_map/ppermute | solution.py:704
  158.5 20.9 %collective-permute-start.37 = (bf16[2,16,6144]{2,1,0:T(8,128)(2,1)S(1)}, bf16[2,16,6144]{2,1,0:T(8,128)(2,1)S(1)}, u32[]{:S(2)}, u32[]{:S(2)}) collective-permute-start(bf16[2,16,6144]{2,1,0:T(8,128)(2,1)S(1)} %get-tuple-element.202), channel_id=1, source_target_pairs={{0,4},{1,5},{2,6},{3,7},{4,0},{5,1},{6,2},{7,3},{8,12},{9,13},{10,... | collective-permute-start | bytes 1179656 | tf_op jit(solution)/shard_map/ppermute | solution.py:704
  164.0 26.7 %copy-start = (f32[6,16,512]{2,1,0:T(8,128)S(1)}, f32[6,16,512]{2,1,0:T(8,128)}, u32[]{:S(2)}) copy-start(f32[6,16,512]{2,1,0:T(8,128)} %rest_3_.2) | copy-start | bytes 589828
  164.1 15.4 %collective-permute-start.40 = (bf16[4,16,2176]{2,1,0:T(8,128)(2,1)S(1)}, bf16[4,16,2176]{2,1,0:T(8,128)(2,1)S(1)}, u32[]{:S(2)}, u32[]{:S(2)}) collective-permute-start(bf16[4,16,2176]{2,1,0:T(8,128)(2,1)S(1)} %get-tuple-element.213), channel_id=1, source_target_pairs={{0,8},{1,9},{2,10},{3,11},{4,12},{5,13},{6,14},{7,15},{8,0},{9,1},... | collective-permute-start | bytes 835592 | tf_op jit(solution)/shard_map/ppermute | solution.py:704
  165.1 14.4 %collective-permute-start.41 = (bf16[4,16,2176]{2,1,0:T(8,128)(2,1)S(1)}, bf16[4,16,2176]{2,1,0:T(8,128)(2,1)S(1)}, u32[]{:S(2)}, u32[]{:S(2)}) collective-permute-start(bf16[4,16,2176]{2,1,0:T(8,128)(2,1)S(1)} %get-tuple-element.214), channel_id=1, source_target_pairs={{0,16},{1,17},{2,18},{3,19},{4,20},{5,21},{6,22},{7,23},{8,24},{9,... | collective-permute-start | bytes 835592 | tf_op jit(solution)/shard_map/ppermute | solution.py:704
  165.8 13.7 %collective-permute-start.42 = (bf16[4,16,2176]{2,1,0:T(8,128)(2,1)S(1)}, bf16[4,16,2176]{2,1,0:T(8,128)(2,1)S(1)}, u32[]{:S(2)}, u32[]{:S(2)}) collective-permute-start(bf16[4,16,2176]{2,1,0:T(8,128)(2,1)S(1)} %get-tuple-element.215), channel_id=1, source_target_pairs={{0,24},{1,25},{2,26},{3,27},{4,28},{5,29},{6,30},{7,31},{8,16},{9,... | collective-permute-start | bytes 835592 | tf_op jit(solution)/shard_map/ppermute | solution.py:704
  179.4 9.2 %collective-permute-start.39 = (bf16[16,6144]{1,0:T(8,128)(2,1)S(1)}, bf16[16,6144]{1,0:T(8,128)(2,1)S(1)}, u32[]{:S(2)}, u32[]{:S(2)}) collective-permute-start(bf16[16,6144]{1,0:T(8,128)(2,1)S(1)} %get-tuple-element.218), channel_id=1, source_target_pairs={{0,2},{1,3},{2,0},{3,1},{4,6},{5,7},{6,4},{7,5},{8,10},{9,11},{10,... | collective-permute-start | bytes 589832 | tf_op jit(solution)/shard_map/ppermute | solution.py:704
  179.7 10.2 %collective-permute-start.43 = (bf16[16,2176]{1,0:T(8,128)(2,1)S(1)}, bf16[16,2176]{1,0:T(8,128)(2,1)S(1)}, u32[]{:S(2)}, u32[]{:S(2)}) collective-permute-start(bf16[16,2176]{1,0:T(8,128)(2,1)S(1)} %get-tuple-element.224), channel_id=1, source_target_pairs={{0,2},{1,3},{2,0},{3,1},{4,6},{5,7},{6,4},{7,5},{8,10},{9,11},{10,... | collective-permute-start | bytes 208904 | tf_op jit(solution)/shard_map/ppermute | solution.py:704
  181.7 8.1 %collective-permute-start.44 = (bf16[16,2176]{1,0:T(8,128)(2,1)S(1)}, bf16[16,2176]{1,0:T(8,128)(2,1)S(1)}, u32[]{:S(2)}, u32[]{:S(2)}) collective-permute-start(bf16[16,2176]{1,0:T(8,128)(2,1)S(1)} %get-tuple-element.225), channel_id=1, source_target_pairs={{0,4},{1,5},{2,6},{3,7},{4,0},{5,1},{6,2},{7,3},{8,12},{9,13},{10,... | collective-permute-start | bytes 208904 | tf_op jit(solution)/shard_map/ppermute | solution.py:704
  182.4 8.4 %collective-permute-start.45 = (bf16[16,2176]{1,0:T(8,128)(2,1)S(1)}, bf16[16,2176]{1,0:T(8,128)(2,1)S(1)}, u32[]{:S(2)}, u32[]{:S(2)}) collective-permute-start(bf16[16,2176]{1,0:T(8,128)(2,1)S(1)} %get-tuple-element.226), channel_id=1, source_target_pairs={{0,6},{1,7},{2,4},{3,5},{4,2},{5,3},{6,0},{7,1},{8,14},{9,15},{10,... | collective-permute-start | bytes 208904 | tf_op jit(solution)/shard_map/ppermute | solution.py:704
  (24 other events, 450.7 us)
where the time goes:
time: 192 us
  Pallas kernels  96.8 us (50%)
  waiting for transfers between devices  44.2 us (23%)
  starting transfers between devices  42.3 us (22%)
  other arithmetic  4.79 us (2%)
  local copies, waits for them, and re-layouts  2.45 us (1%)
    pallas_call x18, Pallas kernels, call(): pl.pallas_call(kernel, out_shape=shapes, in_specs=specs, out_specs=[pl.Bl...  96.8 us
    ppermute x46, waiting for transfers between devices, exchange(): return lax.ppermute(values, AXES, [(i, i ^ offset) for i in range(count)])  44.2 us
    ppermute x46, starting transfers between devices, exchange(): return lax.ppermute(values, AXES, [(i, i ^ offset) for i in range(count)])  42.3 us
  transfers between devices with their start and end apart: 46, of which 17 were waited for; matrix products, arithmetic and copies ran while one was open for 2% of the time, Pallas kernels for 38%

commit v1 on v0

--- a/solution.py
+++ b/solution.py
@@ -100,7 +100,7 @@
             largest = jnp.max(scores, axis=0, keepdims=True)
             expo = jnp.exp(scores - largest)
             totals = jnp.sum(expo, axis=0, keepdims=True)
-            sums_ref[s, g, :, : group * span] = largest + jnp.log(totals)
+            sums_ref[pl.ds(len(parts) * s + g, 1), : group * span] = largest + jnp.log(totals)
             probs.append((expo * (1.0 / totals)).astype(LOW))
         mixed = [
             [
@@ -140,7 +140,8 @@
         grad_values, grad_scores = [], []
         for g, (item, grad_prob) in enumerate(zip(raw, grad_probs)):
             scores = jnp.where(col_mask, item, mask_fill)
-            probs = jnp.exp(scores - sums_ref[s, g, :, : group * span])
+            log_sums = sums_ref[pl.ds(len(parts) * s + g, 1), : group * span]
+            probs = jnp.exp(scores - log_sums)
             grad_values.append(dot_nn(probs.astype(LOW), grads[g]))
             weighted = probs * grad_prob
             inner = jnp.sum(weighted, axis=0, keepdims=True)
@@ -302,14 +303,14 @@
 gelu_cubic = 0.044715
 
 
-def ffn_kernel(count, depth, place, unit_two, inverse_two, cotangent, weights, vectors, *rest):
+def ffn_kernel(count, depth, blocks, place, unit_two, inverse_two, cotangent, vectors, *rest):
     sources = rest[:count]
     (
-        layer_out, grad_sum, grad_out, grad_mixed, sums, bias_sums, *grads,
+        layer_out, grad_sum, grad_out, sums, bias_sums, *grads,
         first_weights, second_weights, hidden, grad_ffn, grad_pre, slopes, semaphores,
     ) = rest[count:]
     model = unit_two.shape[1]
-    pieces = first_weights.shape[1] // model
+    pieces = blocks
     load_ffn(place[0], depth, sources, first_weights, second_weights, semaphores)
     sums[...] = jnp.zeros_like(sums)
     bias_sums[...] = jnp.zeros_like(bias_sums)
@@ -323,7 +324,7 @@
         total = second + vectors[6:7, :]
         for j in range(pieces):
             lanes = slice(j * model, (j + 1) * model)
-            pre = dot_nn(low, first_weights[:, lanes]) + vectors[13 + j : 14 + j, :]
+            pre = dot_nn(low, first_block(first_weights, j, model)) + vectors[13 + j : 14 + j, :]
             square = pre * pre
             bend = jnp.tanh(gelu_scale * pre * (1.0 + gelu_cubic * square))
             half = 0.5 * (1.0 + bend)
@@ -331,7 +332,7 @@
             hidden[rows, lanes] = value
             inner = gelu_scale * (1.0 + 3.0 * gelu_cubic * square)
             slopes[:, lanes] = half + 0.5 * pre * (1.0 - bend * bend) * inner
-            total = total + dot_nn(value, second_weights[lanes, :])
+            total = total + dot_nn(value, second_block(second_weights, j, model))
         unit_three, inverse_three = normalize(total)
         layer_out[rows, :] = (unit_three * (1.0 + vectors[9:10, :]) + vectors[12:13, :]).astype(LOW)
         upper = cotangent[rows, :].astype(FULL)
@@ -344,10 +345,10 @@
         below = third
         for j in range(pieces):
             lanes = slice(j * model, (j + 1) * model)
-            pre = (dot_nt(third_low, second_weights[lanes, :]) * slopes[:, lanes]).astype(LOW)
+            pre = (dot_nt(third_low, second_block(second_weights, j, model)) * slopes[:, lanes]).astype(LOW)
             grad_pre[rows, lanes] = pre
             bias_sums[j : j + 1, :] += column_sum(pre)
-            below = below + dot_nt(pre, first_weights[:, lanes])
+            below = below + dot_nt(pre, first_block(first_weights, j, model))
         sums[3:4, :] += column_sum(below * unit)
         sums[4:5, :] += column_sum(below)
         second_sum = normalize_back(below, vectors[8:9, :], unit, inverse_two[rows, :])
@@ -355,7 +356,6 @@
         out_low = second_sum.astype(LOW)
         grad_out[rows, :] = out_low
         sums[5:6, :] += column_sum(out_low)
-        grad_mixed[rows, :] = dot_nt(out_low, weights[:, 4 * model : 5 * model]).astype(LOW)
 
     row_steps(unit_two.shape[0], step, STEP_ROWS)
     core = place[0] % 2
@@ -371,8 +371,8 @@
 
 
 def load_ffn(place, depth, sources, first_weights, second_weights, semaphores):
-    first_width = first_weights.shape[1]
     if len(sources) == 1:
+        first_width = first_weights.shape[1]
         pltpu.make_async_copy(
             sources[0].at[:, :first_width], first_weights, semaphores.at[0]
         ).start()
@@ -386,24 +386,31 @@
             ).start()
         return
     half = len(sources) // 2
-    model = second_weights.shape[1]
     for k, source in enumerate(sources):
         base = (k % half) * 2 * depth + k // half
-        rows = source.shape[1]
+        pieces, rows = source.shape[1] // 2, source.shape[2]
         for layer in range(depth):
             other = place ^ (base + 2 * layer)
             to_rows = pl.ds(pl.multiple_of(other * rows, rows), rows)
             pltpu.make_async_copy(
-                source.at[layer, :, :first_width], first_weights.at[to_rows, :], semaphores.at[0]
+                source.at[layer, :pieces], first_weights.at[:, to_rows, :], semaphores.at[0]
             ).start()
-            pieces = first_width // model
-            for j in range(pieces):
-                start = pl.multiple_of((other * pieces + j) * rows, rows)
-                pltpu.make_async_copy(
-                    source.at[layer, :, first_width + j * model : first_width + (j + 1) * model],
-                    second_weights.at[pl.ds(start, rows), :],
-                    semaphores.at[1],
-                ).start()
+            pltpu.make_async_copy(
+                source.at[layer, pieces:],
+                second_weights.at[pl.ds(other * pieces, pieces)],
+                semaphores.at[1],
+            ).start()
+
+
+def first_block(ref, j, model):
+    return ref[j] if len(ref.shape) == 3 else ref[:, j * model : (j + 1) * model]
+
+
+def second_block(ref, j, model):
+    if len(ref.shape) == 2:
+        return ref[j * model : (j + 1) * model, :]
+    count = model // ref.shape[1]
+    return ref[j * count : (j + 1) * count].reshape(model, model)
 
 
 def store_ffn_out(refs, core, block, pieces, value):
@@ -426,8 +433,15 @@
 
 
 def cross_backward_kernel(
-    row_starts, col_starts, queries, keys, values, grad_mixed, sums_in, dq, dk, dv
+    row_starts, col_starts, queries, keys, values, grad_out, weights, sums_in, dq, dk, dv, grad_mixed
 ):
+    model = queries.shape[1]
+
+    def project(rows):
+        low = dot_nt(grad_out[rows, :], weights[:, 4 * model : 5 * model]).astype(LOW)
+        grad_mixed[rows, :] = low
+
+    row_steps(queries.shape[0], project)
     attend_backward(row_starts, col_starts, queries, keys, values, grad_mixed, sums_in, dq, dk, dv)
 
 
@@ -630,8 +644,8 @@
     "cross_project": 14,
     "cross_attend": 10,
     "cross_finish": 9,
-    "ffn": 33,
-    "cross_backward": 11,
+    "ffn": 32.8,
+    "cross_backward": 13,
     "cross_grads": 20,
     "self_backward": 16,
     "tokens_grad": 11,
@@ -649,7 +663,7 @@
 
 
 def limit(name):
-    return pltpu.CompilerParams(vmem_limit_bytes=LIMITS[name] << 20)
+    return pltpu.CompilerParams(vmem_limit_bytes=int(LIMITS[name] * (1 << 20)))
 
 
 def pinned(sources):
@@ -855,6 +869,13 @@
     ffn_piece = jnp.concatenate(
         [ffn_in_master.astype(LOW), to_columns(ffn_out_master.astype(LOW))], axis=1
     )
+    if aligned:
+        ffn_piece = jnp.concatenate(
+            [
+                ffn_in_master.astype(LOW).reshape(rows, pieces, model).transpose(1, 0, 2),
+                ffn_out_master.astype(LOW).reshape(pieces, rows, model),
+            ]
+        )
     row_starts, col_starts = segment_starts(target_ids[0]), segment_starts(source_ids[0])
 
     def sources_of(parts):
@@ -873,7 +894,7 @@
         return [jnp.concatenate([flat[:, :, :width].reshape(model, -1), second], axis=1)]
 
     wide, tall, thin = ((total, model), LOW), ((total, model), FULL), ((total, 1), FULL)
-    log_sums = ((SEGMENTS, model // 256, 1, 1024), FULL)
+    log_sums = ((SEGMENTS * (model // 256), 1024), FULL)
     small = ((8, model), FULL)
     unit = 2 * total * model * model
     attend = 2 * SEGMENTS * HEADS * 256 * 256 * 256
@@ -927,15 +948,21 @@
     gates = [mixed] * (dp_count // 2) + [cross_mixed] * (dp_count // 2)
     sources = ffn_sources_of(core_list([after(*pair) for pair in zip(ffn_near, gates)]))
     hidden = pieces * model
+    if aligned:
+        ffn_scratch = [
+            pltpu.VMEM((pieces, model, model), LOW), pltpu.VMEM((count * pieces, rows, model), LOW),
+        ]
+    else:
+        ffn_scratch = [pltpu.VMEM((model, hidden), LOW), pltpu.VMEM((hidden, model), LOW)]
     (
-        layer_out, grad_sum, grad_cross_out, grad_cross_mixed, ffn_sums, bias_sums, *ffn_grads
+        layer_out, grad_sum, grad_cross_out, ffn_sums, bias_sums, *ffn_grads
     ) = call(
-        functools.partial(ffn_kernel, len(sources), depth), "ffn", [spot],
-        [unit_two, inverse_two, cotangent, cross_weights, vectors],
-        [wide, keep(tall), keep(wide), keep(wide), small, small, *grad_outs(2 * hidden)],
+        functools.partial(ffn_kernel, len(sources), depth, pieces), "ffn", [spot],
+        [unit_two, inverse_two, cotangent, vectors],
+        [wide, keep(tall), keep(wide), small, small, *grad_outs(2 * hidden)],
         (5 * pieces + 1) * unit, sources,
         [
-            pltpu.VMEM((model, hidden), LOW), pltpu.VMEM((hidden, model), LOW),
+            *ffn_scratch,
             pltpu.VMEM((total, hidden), LOW), pltpu.VMEM((total, model), LOW),
             pltpu.VMEM((total, hidden), LOW),
             pltpu.VMEM((STEP_ROWS, hidden), FULL), wait_two,
@@ -950,8 +977,11 @@
     ffn_moved = exchange(sent, 1)
     cross_dq, cross_dk, cross_dv = call(
         cross_backward_kernel, "cross_backward", [row_starts, col_starts],
-        [cross_queries, cross_keys, cross_values, after(grad_cross_mixed, sent), cross_log],
-        [keep(wide), keep(wide), keep(wide)], 5 * attend,
+        [
+            cross_queries, cross_keys, cross_values, after(grad_cross_out, sent), cross_weights,
+            cross_log,
+        ],
+        [keep(wide), keep(wide), keep(wide)], 5 * attend, (), [pltpu.VMEM((total, model), LOW)],
     )
     fast = aligned and dp_count == 4 and depth == 4
     ffn_moved = after(ffn_moved, cross_dq)
@@ -1023,6 +1053,8 @@
     grad_scale = 1.0 / math.sqrt(total * count)
     if fast:
         wide_row = wide_pair[1:]
+        self_kept, self_sends = fold_square(spot, self_kept, self_moved)
+        self_moved = move_layers(self_sends)
         layer_own, layer_send = call(
             fold_last_kernel, "fold_last", [], [layer_keep, after(layer_got, *self_sends)],
             [(wide_row, FULL), (wide_row, LOW)], 1,
@@ -1037,10 +1069,6 @@
             [(ffn_in_master.shape, kind) for kind in kinds]
             + [(ffn_out_master.shape, kind) for kind in kinds], 1,
         )
-        self_kept, self_sends = fold_square(
-            spot, self_kept, [after(item, layer_send) for item in self_moved]
-        )
-        self_moved = move_layers(self_sends)
         states = [
             qkv_master, qkv_first, qkv_second, out_master, out_first, out_second,
             vector_master.T, vector_first.T, vector_second.T,

time: 192 us -> 187 us (0.974)
  starting transfers between devices: 42.3 us -> 37.2 us
  Pallas kernels: 96.8 us -> 100 us
  local copies, waits for them, and re-layouts: 2.45 us -> 0.19 us
    ppermute x46, starting transfers between devices: 42.3 us -> 37.2 us  [exchange(): return lax.ppermute(values, AXES, [(i, i ^ offset) for i in range(count)])]
    pallas_call x18, Pallas kernels: 96.8 us -> 100 us  [call(): pl.pallas_call(kernel, out_shape=shapes, in_specs=specs, out_specs=[pl.Bl...]
    unnamed x58 -> x53, local copies, waits for them, and re-layouts: 2.37 us -> 0.16 us
  transfers between devices with their start and end apart: 46 -> 46, of which waited for: 17 -> 16; matrix products, arithmetic and copies ran while one was open for 2% -> 2% of each run, Pallas kernels for 38% -> 41%
where the time goes in v1:
time: 187 us; the launch traced here: 186 us
  Pallas kernels  100 us (53%)
  waiting for transfers between devices  42.4 us (23%)
  starting transfers between devices  37.2 us (20%)
  other arithmetic  4.8 us (3%)
    pallas_call x18, Pallas kernels, call(): pl.pallas_call(kernel, out_shape=shapes, in_specs=specs, out_specs=[pl.Bl...  100 us
    ppermute x46, waiting for transfers between devices, exchange(): return lax.ppermute(values, AXES, [(i, i ^ offset) for i in range(count)])  42.4 us
    ppermute x46, starting transfers between devices, exchange(): return lax.ppermute(values, AXES, [(i, i ^ offset) for i in range(count)])  37.2 us
  transfers between devices with their start and end apart: 46, of which 16 were waited for; matrix products, arithmetic and copies ran while one was open for 2% of the time, Pallas kernels for 41%

profile of v1, /device:TPU:0, one launch (start us, length us, event | category | flops | bytes accessed | tf_op | source)
XLA Modules:
  0.0 186.5 jit_solution(2886097331339532953)
XLA Ops:
  0.7 0.8 convert_bitcast_fusion
  1.5 0.9 convert_element_type.25
  2.4 4.1 %collective-permute-start.1 = (bf16[16,1664]{1,0:T(8,128)(2,1)S(1)}, bf16[16,1664]{1,0:T(8,128)(2,1)S(1)}, u32[]{:S(2)}, u32[]{:S(2)}) collective-permute-start(bf16[16,1664]{1,0:T(8,128)(2,1)S(1)} %fusion.1), channel_id=1, source_target_pairs={{0,4},{1,5},{2,6},{3,7},{4,0},{5,1},{6,2},{7,3},{8,12},{9,13},{10,... | collective-permute-start | bytes 159752 | tf_op jit(solution)/shard_map/ppermute | solution.py:718
  6.5 1.6 collective-permute-start
  8.1 0.8 convert_element_type.24
  9.0 0.9 convert_element_type.28
  10.0 0.9 convert_element_type.29
  10.9 3.2 %collective-permute-done.2 = bf16[16,1664]{1,0:T(8,128)(2,1)S(1)} collective-permute-done((bf16[16,1664]{1,0:T(8,128)(2,1)S(1)}, bf16[16,1664]{1,0:T(8,128)(2,1)S(1)}, u32[]{:S(2)}, u32[]{:S(2)}) %collective-permute-start.2) | collective-permute-done | bytes 53280 | tf_op jit(solution)/shard_map/ppermute | solution.py:718
  14.2 2.5 %collective-permute-start.7 = (bf16[4,16,1664]{2,1,0:T(8,128)(2,1)S(1)}, bf16[4,16,1664]{2,1,0:T(8,128)(2,1)S(1)}, u32[]{:S(2)}, u32[]{:S(2)}) collective-permute-start(bf16[4,16,1664]{2,1,0:T(8,128)(2,1)S(1)} %pad_maximum_fusion.2.rest_0_), channel_id=1, source_target_pairs={{0,24},{1,25},{2,26},{3,27},{4,28},{5,29},{6,30},{7,31},{8,16},{9,... | collective-permute-start | bytes 638984 | tf_op jit(solution)/shard_map/ppermute | solution.py:718
  16.7 0.5 collective-permute-start.6
  17.2 0.5 collective-permute-start.5
  17.8 2.0 %collective-permute-start.19 = (bf16[1,8,16,512]{3,2,1,0:T(8,128)(2,1)S(1)}, bf16[1,8,16,512]{3,2,1,0:T(8,128)(2,1)S(1)}, u32[]{:S(2)}, u32[]{:S(2)}) collective-permute-start(bf16[1,8,16,512]{3,2,1,0:T(8,128)(2,1)S(1)} %bitcast.56), channel_id=1, source_target_pairs={{0,2},{1,3},{2,0},{3,1},{4,6},{5,7},{6,4},{7,5},{8,10},{9,11},{10,... | collective-permute-start | bytes 393224 | tf_op jit(solution)/shard_map/ppermute | solution.py:718
  20.4 3.9 %collective-permute-done.19 = bf16[1,8,16,512]{3,2,1,0:T(8,128)(2,1)S(1)} collective-permute-done((bf16[1,8,16,512]{3,2,1,0:T(8,128)(2,1)S(1)}, bf16[1,8,16,512]{3,2,1,0:T(8,128)(2,1)S(1)}, u32[]{:S(2)}, u32[]{:S(2)}) %collective-permute-start.19) | collective-permute-done | bytes 131104 | tf_op jit(solution)/shard_map/ppermute | solution.py:718
  24.3 0.6 collective-permute-start.11
  25.6 1.6 collective-permute-done.4
  27.6 2.5 %collective-permute-start.14 = (bf16[4,16,2560]{2,1,0:T(8,128)(2,1)S(1)}, bf16[4,16,2560]{2,1,0:T(8,128)(2,1)S(1)}, u32[]{:S(2)}, u32[]{:S(2)}) collective-permute-start(bf16[4,16,2560]{2,1,0:T(8,128)(2,1)S(1)} %pad_maximum_fusion.rest_0_), channel_id=1, source_target_pairs={{0,24},{1,25},{2,26},{3,27},{4,28},{5,29},{6,30},{7,31},{8,16},{9,... | collective-permute-start | bytes 983048 | tf_op jit(solution)/shard_map/ppermute | solution.py:718
  30.1 0.5 collective-permute-start.13
  30.7 0.5 collective-permute-start.12
  31.2 14.6 %self_forward.1 = (bf16[512,1664]{1,0:T(8,128)(2,1)S(1)}, f32[24,512]{1,0:T(8,128)S(1)}, bf16[1024,512]{1,0:T(8,128)(2,1)S(1)}, bf16[1024,512]{1,0:T(8,128)(2,1)...) custom-call(s32[1]{0:T(128)} %bitcast.place, ...), custom_call_target="tpu_custom_call" | custom-call | flops 6979321856 | bytes 2752512 | tf_op jit(solution)/shard_map/self_forward/pallas_call | solution.py:685
  45.9 0.5 collective-permute-start.16
  47.0 0.9 collective-permute-start.21
  48.9 6.8 %cross_project.1 = (bf16[512,2560]{1,0:T(8,128)(2,1)S(1)}, f32[1024,512]{1,0:T(8,128)S(1)}, f32[1024,1]{1,0:T(8,128)S(1)}, bf16[1024,512]{1,0:T(8,128)(2,1)S(1)}...) custom-call(s32[1]{0:T(128)} %bitcast.place, bf16[1024,512]{1,0:T(8,128)(2,1)S(1)} %copy-done.17, ...), custom_call_target="tpu_custom_call" | custom-call | flops 2147483648 | bytes 5816320 | tf_op jit(solution)/shard_map/cross_project/pallas_call | solution.py:685
  55.7 5.3 %collective-permute-done.21.rest_1_ = bf16[4,8,16,512]{3,2,1,0:T(8,128)(2,1)S(1)} collective-permute-done((bf16[4,8,16,512]{3,2,1,0:T(8,128)(2,1)S(1)}, bf16[4,8,16,512]{3,2,1,0:T(8,128)(2,1)S(1)}, u32[]{:S(2)}, u32[]{:S(2)}) %collective-permute-start.21) | collective-permute-done | bytes 524320 | tf_op jit(solution)/shard_map/ppermute | solution.py:718
  61.0 0.9 collective-permute-start.23
  62.1 9.6 %cross_attend.1 = (bf16[1024,512]{1,0:T(8,128)(2,1)S(1)}, f32[20,1024]{1,0:T(8,128)S(1)}) custom-call(s32[11]{0:T(128)S(1)} %convert_reduce_fusion.1.row_starts, s32[11]{0:T(128)S(1)} %convert_reduce_fusion.col_starts, bf16[1024,512]{1,0:T(8,128)(2,1)S(1)} %get-tuple-element.141.queries, bf16[1024,512]{1,0:T(8,128)(2,1)S(1)} %get-tuple-element.142.keys, ...), custom_call_target="tpu_custom_call" | custom-call | flops 5368709120 | bytes 3145728 | tf_op jit(solution)/shard_map/cross_attend/pallas_call | solution.py:685
  72.3 1.8 collective-permute-done.23.rest_3_
  74.1 1.4 cross_finish.1
  76.0 22.5 %ffn.1 = (bf16[1024,512]{1,0:T(8,128)(2,1)}, f32[1024,512]{1,0:T(8,128)S(1)}, bf16[1024,512]{1,0:T(8,128)(2,1)S(1)}, f32[8,512]{1,0:T(8,128)S(1)}, f32[8,512]{1,...) custom-call(s32[1]{0:T(128)} %bitcast.place, ...), custom_call_target="tpu_custom_call" | custom-call | flops 11274289152 | bytes 7393280 | tf_op jit(solution)/shard_map/ffn/pallas_call | solution.py:685
  98.7 15.0 %cross_backward.1 = (bf16[1024,512]{1,0:T(8,128)(2,1)S(1)}, bf16[1024,512]{1,0:T(8,128)(2,1)S(1)}, bf16[1024,512]{1,0:T(8,128)(2,1)S(1)}) custom-call(s32[11]{0:T(128)S(1)} %convert_reduce_fusion.1.row_starts, s32[11]{0:T(128)S(1)} %convert_reduce_fusion.col_starts, bf16[1024,512]{1,0:T(8,128)(2,1)S(1)} %get-tuple-element.141.queries, ...), custom_call_target="tpu_custom_call" | custom-call | flops 13421772800 | bytes 6897664 | tf_op jit(solution)/shard_map/cross_backward/pallas_call | solution.py:685
  114.7 6.5 %cross_grads.1 = (f32[1024,512]{1,0:T(8,128)S(1)}, bf16[1024,512]{1,0:T(8,128)(2,1)S(1)}, bf16[1024,512]{1,0:T(8,128)(2,1)S(1)}, f32[8,512]{1,0:T(8,128)S(1)}, f...) custom-call(s32[1]{0:T(128)} %bitcast.place, ...), custom_call_target="tpu_custom_call" | custom-call | flops 4294967296 | bytes 13160448 | tf_op jit(solution)/shard_map/cross_grads/pallas_call | solution.py:685
  121.2 6.5 %collective-permute-done.29.got_first = bf16[2,4,16,2048]{3,2,1,0:T(8,128)(2,1)S(1)} collective-permute-done((bf16[2,4,16,2048]{3,2,1,0:T(8,128)(2,1)S(1)}, bf16[2,4,16,2048]{3,2,1,0:T(8,128)(2,1)S(1)}, u32[]{:S(2)}, u32[]{:S(2)}) %collective-permute-start.29) | collective-permute-done | bytes 524320 | tf_op jit(solution)/shard_map/ppermute | solution.py:718
  127.7 1.4 collective-permute-done.30.got_second
  129.7 1.5 collective-permute-start.33
  131.2 0.8 collective-permute-done.31.received
  132.6 1.5 collective-permute-start.35
  134.1 1.7 collective-permute-start.36
  135.8 16.9 %self_backward.1 = (bf16[1024,512]{1,0:T(8,128)(2,1)S(1)}, bf16[1024,512]{1,0:T(8,128)(2,1)S(1)}, bf16[1024,512]{1,0:T(8,128)(2,1)S(1)}, bf16[16,16,2176]{2,1,0:T(8,128)(2,1)S(1)}, bf16[16,16,2176]{2,1,0:T(8,128)(2,1)S(1)}) custom-call(s32[1]{0:T(128)} %bitcast.place, s32[11]{0:T(128)S(1)} %convert_reduce_fusion.1.row_starts, ...), custom_call_target="tpu_custom_call" | custom-call | flops 15569256448 | bytes 7471104 | tf_op jit(solution)/shard_map/self_backward/pallas_call | solution.py:685
  153.1 2.3 %collective-permute-start.37 = (bf16[2,16,6144]{2,1,0:T(8,128)(2,1)S(1)}, bf16[2,16,6144]{2,1,0:T(8,128)(2,1)S(1)}, u32[]{:S(2)}, u32[]{:S(2)}) collective-permute-start(bf16[2,16,6144]{2,1,0:T(8,128)(2,1)S(1)} %get-tuple-element.197), channel_id=1, source_target_pairs={{0,4},{1,5},{2,6},{3,7},{4,0},{5,1},{6,2},{7,3},{8,12},{9,13},{10,... | collective-permute-start | bytes 1179656 | tf_op jit(solution)/shard_map/ppermute | solution.py:718
  155.4 3.3 %tokens_grad.1 = f32[1024,512]{1,0:T(8,128)} custom-call(bf16[1024,512]{1,0:T(8,128)(2,1)S(1)} %get-tuple-element.198.dq, bf16[1024,512]{1,0:T(8,128)(2,1)S(1)} %get-tuple-element.199.dk, bf16[1024,512]{1,0:T(8,128)(2,1)S(1)} %get-tuple-element.200.dv, f32[1024,512]{1,0:T(8,128)S(1)} %get-tuple-element.201.first_sum, ...), custom_call_target="tpu_custom_call" | custom-call | flops 1610612736 | bytes 6946816 | tf_op jit(solution)/shard_map/tokens_grad/pallas_call | solution.py:685
  159.2 1.2 collective-permute-start.39
  160.7 2.0 %collective-permute-start.41 = (bf16[4,16,2176]{2,1,0:T(8,128)(2,1)S(1)}, bf16[4,16,2176]{2,1,0:T(8,128)(2,1)S(1)}, u32[]{:S(2)}, u32[]{:S(2)}) collective-permute-start(bf16[4,16,2176]{2,1,0:T(8,128)(2,1)S(1)} %get-tuple-element.211), channel_id=1, source_target_pairs={{0,24},{1,25},{2,26},{3,27},{4,28},{5,29},{6,30},{7,31},{8,16},{9,... | collective-permute-start | bytes 835592 | tf_op jit(solution)/shard_map/ppermute | solution.py:718
  162.7 6.0 %collective-permute-done.39.rest_0_ = bf16[4,16,2176]{2,1,0:T(8,128)(2,1)S(1)} collective-permute-done((bf16[4,16,2176]{2,1,0:T(8,128)(2,1)S(1)}, bf16[4,16,2176]{2,1,0:T(8,128)(2,1)S(1)}, u32[]{:S(2)}, u32[]{:S(2)}) %collective-permute-start.39) | collective-permute-done | bytes 278560 | tf_op jit(solution)/shard_map/ppermute | solution.py:718
  168.8 5.8 %collective-permute-done.40.rest_1_ = bf16[4,16,2176]{2,1,0:T(8,128)(2,1)S(1)} collective-permute-done((bf16[4,16,2176]{2,1,0:T(8,128)(2,1)S(1)}, bf16[4,16,2176]{2,1,0:T(8,128)(2,1)S(1)}, u32[]{:S(2)}, u32[]{:S(2)}) %collective-permute-start.40) | collective-permute-done | bytes 278560 | tf_op jit(solution)/shard_map/ppermute | solution.py:718
  174.9 2.0 %collective-permute-start.43 = (bf16[16,2176]{1,0:T(8,128)(2,1)S(1)}, bf16[16,2176]{1,0:T(8,128)(2,1)S(1)}, u32[]{:S(2)}, u32[]{:S(2)}) collective-permute-start(bf16[16,2176]{1,0:T(8,128)(2,1)S(1)} %get-tuple-element.212), channel_id=1, source_target_pairs={{0,2},{1,3},{2,0},{3,1},{4,6},{5,7},{6,4},{7,5},{8,10},{9,11},{10,... | collective-permute-start | bytes 208904 | tf_op jit(solution)/shard_map/ppermute | solution.py:718
  177.2 2.2 %collective-permute-start.45 = (bf16[16,2176]{1,0:T(8,128)(2,1)S(1)}, bf16[16,2176]{1,0:T(8,128)(2,1)S(1)}, u32[]{:S(2)}, u32[]{:S(2)}) collective-permute-start(bf16[16,2176]{1,0:T(8,128)(2,1)S(1)} %get-tuple-element.214), channel_id=1, source_target_pairs={{0,6},{1,7},{2,4},{3,5},{4,2},{5,3},{6,0},{7,1},{8,14},{9,15},{10,... | collective-permute-start | bytes 208904 | tf_op jit(solution)/shard_map/ppermute | solution.py:718
  179.4 4.3 %collective-permute-done.42.got = bf16[16,6144]{1,0:T(8,128)(2,1)S(1)} collective-permute-done((bf16[16,6144]{1,0:T(8,128)(2,1)S(1)}, bf16[16,6144]{1,0:T(8,128)(2,1)S(1)}, u32[]{:S(2)}, u32[]{:S(2)}) %collective-permute-start.42) | collective-permute-done | bytes 196640 | tf_op jit(solution)/shard_map/ppermute | solution.py:718
  183.7 1.1 ffn_update.1
  185.3 1.1 final_update.1
  (133 shorter events, 8.9 us)
Async XLA Ops:
  0.7 30.5 %copy-start.17 = (bf16[1024,512]{1,0:T(8,128)(2,1)S(1)}, bf16[1024,512]{1,0:T(8,128)(2,1)}, u32[]{:S(2)}) copy-start(bf16[1024,512]{1,0:T(8,128)(2,1)} %tokens.4) | copy-start | bytes 3145732
  2.4 8.4 %collective-permute-start.1 = (bf16[16,1664]{1,0:T(8,128)(2,1)S(1)}, bf16[16,1664]{1,0:T(8,128)(2,1)S(1)}, u32[]{:S(2)}, u32[]{:S(2)}) collective-permute-start(bf16[16,1664]{1,0:T(8,128)(2,1)S(1)} %fusion.1), channel_id=1, source_target_pairs={{0,4},{1,5},{2,6},{3,7},{4,0},{5,1},{6,2},{7,3},{8,12},{9,13},{10,... | collective-permute-start | bytes 159752 | tf_op jit(solution)/shard_map/ppermute | solution.py:718
  6.5 4.3 %collective-permute-start = (bf16[16,1664]{1,0:T(8,128)(2,1)S(1)}, bf16[16,1664]{1,0:T(8,128)(2,1)S(1)}, u32[]{:S(2)}, u32[]{:S(2)}) collective-permute-start(bf16[16,1664]{1,0:T(8,128)(2,1)S(1)} %fusion.1), channel_id=1, source_target_pairs={{0,2},{1,3},{2,0},{3,1},{4,6},{5,7},{6,4},{7,5},{8,10},{9,11},{10,... | collective-permute-start | bytes 159752 | tf_op jit(solution)/shard_map/ppermute | solution.py:718
  8.1 5.9 %collective-permute-start.2 = (bf16[16,1664]{1,0:T(8,128)(2,1)S(1)}, bf16[16,1664]{1,0:T(8,128)(2,1)S(1)}, u32[]{:S(2)}, u32[]{:S(2)}) collective-permute-start(bf16[16,1664]{1,0:T(8,128)(2,1)S(1)} %fusion.1), channel_id=1, source_target_pairs={{0,6},{1,7},{2,4},{3,5},{4,2},{5,3},{6,0},{7,1},{8,14},{9,15},{10,... | collective-permute-start | bytes 159752 | tf_op jit(solution)/shard_map/ppermute | solution.py:718
  14.1 5.7 %collective-permute-start.3 = (bf16[1,16,2560]{2,1,0:T(8,128)(2,1)S(1)}, bf16[1,16,2560]{2,1,0:T(8,128)(2,1)S(1)}, u32[]{:S(2)}, u32[]{:S(2)}) collective-permute-start(bf16[1,16,2560]{2,1,0:T(8,128)(2,1)S(1)} %bitcast.58), channel_id=1, source_target_pairs={{0,2},{1,3},{2,0},{3,1},{4,6},{5,7},{6,4},{7,5},{8,10},{9,11},{10,... | collective-permute-start | bytes 245768 | tf_op jit(solution)/shard_map/ppermute | solution.py:718
  14.2 10.1 %collective-permute-start.7 = (bf16[4,16,1664]{2,1,0:T(8,128)(2,1)S(1)}, bf16[4,16,1664]{2,1,0:T(8,128)(2,1)S(1)}, u32[]{:S(2)}, u32[]{:S(2)}) collective-permute-start(bf16[4,16,1664]{2,1,0:T(8,128)(2,1)S(1)} %pad_maximum_fusion.2.rest_0_), channel_id=1, source_target_pairs={{0,24},{1,25},{2,26},{3,27},{4,28},{5,29},{6,30},{7,31},{8,16},{9,... | collective-permute-start | bytes 638984 | tf_op jit(solution)/shard_map/ppermute | solution.py:718
  16.7 8.4 %collective-permute-start.6 = (bf16[4,16,1664]{2,1,0:T(8,128)(2,1)S(1)}, bf16[4,16,1664]{2,1,0:T(8,128)(2,1)S(1)}, u32[]{:S(2)}, u32[]{:S(2)}) collective-permute-start(bf16[4,16,1664]{2,1,0:T(8,128)(2,1)S(1)} %pad_maximum_fusion.2.rest_0_), channel_id=1, source_target_pairs={{0,16},{1,17},{2,18},{3,19},{4,20},{5,21},{6,22},{7,23},{8,24},{9,... | collective-permute-start | bytes 638984 | tf_op jit(solution)/shard_map/ppermute | solution.py:718
  17.2 8.0 %collective-permute-start.5 = (bf16[4,16,1664]{2,1,0:T(8,128)(2,1)S(1)}, bf16[4,16,1664]{2,1,0:T(8,128)(2,1)S(1)}, u32[]{:S(2)}, u32[]{:S(2)}) collective-permute-start(bf16[4,16,1664]{2,1,0:T(8,128)(2,1)S(1)} %pad_maximum_fusion.2.rest_0_), channel_id=1, source_target_pairs={{0,8},{1,9},{2,10},{3,11},{4,12},{5,13},{6,14},{7,15},{8,0},{9,1},... | collective-permute-start | bytes 638984 | tf_op jit(solution)/shard_map/ppermute | solution.py:718
  17.8 6.5 %collective-permute-start.19 = (bf16[1,8,16,512]{3,2,1,0:T(8,128)(2,1)S(1)}, bf16[1,8,16,512]{3,2,1,0:T(8,128)(2,1)S(1)}, u32[]{:S(2)}, u32[]{:S(2)}) collective-permute-start(bf16[1,8,16,512]{3,2,1,0:T(8,128)(2,1)S(1)} %bitcast.56), channel_id=1, source_target_pairs={{0,2},{1,3},{2,0},{3,1},{4,6},{5,7},{6,4},{7,5},{8,10},{9,11},{10,... | collective-permute-start | bytes 393224 | tf_op jit(solution)/shard_map/ppermute | solution.py:718
  19.8 7.5 %collective-permute-start.4 = (bf16[2,16,2560]{2,1,0:T(8,128)(2,1)S(1)}, bf16[2,16,2560]{2,1,0:T(8,128)(2,1)S(1)}, u32[]{:S(2)}, u32[]{:S(2)}) collective-permute-start(bf16[2,16,2560]{2,1,0:T(8,128)(2,1)S(1)} %pad_maximum_fusion.3), channel_id=1, source_target_pairs={{0,4},{1,5},{2,6},{3,7},{4,0},{5,1},{6,2},{7,3},{8,12},{9,13},{10,... | collective-permute-start | bytes 491528 | tf_op jit(solution)/shard_map/ppermute | solution.py:718
  24.3 3.3 %collective-permute-start.8 = (bf16[4,16,1664]{2,1,0:T(8,128)(2,1)S(1)}, bf16[4,16,1664]{2,1,0:T(8,128)(2,1)S(1)}, u32[]{:S(2)}, u32[]{:S(2)}) collective-permute-start(bf16[4,16,1664]{2,1,0:T(8,128)(2,1)S(1)} %pad_maximum_fusion.2.rest_0_), channel_id=1, source_target_pairs={{0,1},{1,0},{2,3},{3,2},{4,5},{5,4},{6,7},{7,6},{8,9},{9,8},{10,11... | collective-permute-start | bytes 638984 | tf_op jit(solution)/shard_map/ppermute | solution.py:718
  24.3 5.8 %collective-permute-start.11 = (bf16[4,16,1664]{2,1,0:T(8,128)(2,1)S(1)}, bf16[4,16,1664]{2,1,0:T(8,128)(2,1)S(1)}, u32[]{:S(2)}, u32[]{:S(2)}) collective-permute-start(bf16[4,16,1664]{2,1,0:T(8,128)(2,1)S(1)} %collective-permute-done.7.rest_3_), channel_id=1, source_target_pairs={{0,1},{1,0},{2,3},{3,2},{4,5},{5,4},{6,7},{7,6},{8,9},{9,8},{10,11... | collective-permute-start | bytes 638984 | tf_op jit(solution)/shard_map/ppermute | solution.py:718
  25.1 5.5 %collective-permute-start.10 = (bf16[4,16,1664]{2,1,0:T(8,128)(2,1)S(1)}, bf16[4,16,1664]{2,1,0:T(8,128)(2,1)S(1)}, u32[]{:S(2)}, u32[]{:S(2)}) collective-permute-start(bf16[4,16,1664]{2,1,0:T(8,128)(2,1)S(1)} %collective-permute-done.6.rest_2_), channel_id=1, source_target_pairs={{0,1},{1,0},{2,3},{3,2},{4,5},{5,4},{6,7},{7,6},{8,9},{9,8},{10,11... | collective-permute-start | bytes 638984 | tf_op jit(solution)/shard_map/ppermute | solution.py:718
  25.2 6.0 %collective-permute-start.9 = (bf16[4,16,1664]{2,1,0:T(8,128)(2,1)S(1)}, bf16[4,16,1664]{2,1,0:T(8,128)(2,1)S(1)}, u32[]{:S(2)}, u32[]{:S(2)}) collective-permute-start(bf16[4,16,1664]{2,1,0:T(8,128)(2,1)S(1)} %collective-permute-done.5.rest_1_), channel_id=1, source_target_pairs={{0,1},{1,0},{2,3},{3,2},{4,5},{5,4},{6,7},{7,6},{8,9},{9,8},{10,11... | collective-permute-start | bytes 638984 | tf_op jit(solution)/shard_map/ppermute | solution.py:718
  27.3 19.7 %collective-permute-start.20 = (bf16[2,8,16,512]{3,2,1,0:T(8,128)(2,1)S(1)}, bf16[2,8,16,512]{3,2,1,0:T(8,128)(2,1)S(1)}, u32[]{:S(2)}, u32[]{:S(2)}) collective-permute-start(bf16[2,8,16,512]{3,2,1,0:T(8,128)(2,1)S(1)} %pad_maximum_fusion.1), channel_id=1, source_target_pairs={{0,4},{1,5},{2,6},{3,7},{4,0},{5,1},{6,2},{7,3},{8,12},{9,13},{10,... | collective-permute-start | bytes 786440 | tf_op jit(solution)/shard_map/ppermute | solution.py:718
  27.6 18.3 %collective-permute-start.14 = (bf16[4,16,2560]{2,1,0:T(8,128)(2,1)S(1)}, bf16[4,16,2560]{2,1,0:T(8,128)(2,1)S(1)}, u32[]{:S(2)}, u32[]{:S(2)}) collective-permute-start(bf16[4,16,2560]{2,1,0:T(8,128)(2,1)S(1)} %pad_maximum_fusion.rest_0_), channel_id=1, source_target_pairs={{0,24},{1,25},{2,26},{3,27},{4,28},{5,29},{6,30},{7,31},{8,16},{9,... | collective-permute-start | bytes 983048 | tf_op jit(solution)/shard_map/ppermute | solution.py:718
  30.1 15.8 %collective-permute-start.13 = (bf16[4,16,2560]{2,1,0:T(8,128)(2,1)S(1)}, bf16[4,16,2560]{2,1,0:T(8,128)(2,1)S(1)}, u32[]{:S(2)}, u32[]{:S(2)}) collective-permute-start(bf16[4,16,2560]{2,1,0:T(8,128)(2,1)S(1)} %pad_maximum_fusion.rest_0_), channel_id=1, source_target_pairs={{0,16},{1,17},{2,18},{3,19},{4,20},{5,21},{6,22},{7,23},{8,24},{9,... | collective-permute-start | bytes 983048 | tf_op jit(solution)/shard_map/ppermute | solution.py:718
  30.7 15.3 %collective-permute-start.12 = (bf16[4,16,2560]{2,1,0:T(8,128)(2,1)S(1)}, bf16[4,16,2560]{2,1,0:T(8,128)(2,1)S(1)}, u32[]{:S(2)}, u32[]{:S(2)}) collective-permute-start(bf16[4,16,2560]{2,1,0:T(8,128)(2,1)S(1)} %pad_maximum_fusion.rest_0_), channel_id=1, source_target_pairs={{0,8},{1,9},{2,10},{3,11},{4,12},{5,13},{6,14},{7,15},{8,0},{9,1},... | collective-permute-start | bytes 983048 | tf_op jit(solution)/shard_map/ppermute | solution.py:718
  45.8 2.1 %collective-permute-start.15 = (bf16[4,16,2560]{2,1,0:T(8,128)(2,1)S(1)}, bf16[4,16,2560]{2,1,0:T(8,128)(2,1)S(1)}, u32[]{:S(2)}, u32[]{:S(2)}) collective-permute-start(bf16[4,16,2560]{2,1,0:T(8,128)(2,1)S(1)} %pad_maximum_fusion.rest_0_), channel_id=1, source_target_pairs={{0,1},{1,0},{2,3},{3,2},{4,5},{5,4},{6,7},{7,6},{8,9},{9,8},{10,11... | collective-permute-start | bytes 983048 | tf_op jit(solution)/shard_map/ppermute | solution.py:718
  45.9 2.5 %collective-permute-start.16 = (bf16[4,16,2560]{2,1,0:T(8,128)(2,1)S(1)}, bf16[4,16,2560]{2,1,0:T(8,128)(2,1)S(1)}, u32[]{:S(2)}, u32[]{:S(2)}) collective-permute-start(bf16[4,16,2560]{2,1,0:T(8,128)(2,1)S(1)} %collective-permute-done.12.rest_1_), channel_id=1, source_target_pairs={{0,1},{1,0},{2,3},{3,2},{4,5},{5,4},{6,7},{7,6},{8,9},{9,8},{10,11... | collective-permute-start | bytes 983048 | tf_op jit(solution)/shard_map/ppermute | solution.py:718
  46.5 2.0 %collective-permute-start.17 = (bf16[4,16,2560]{2,1,0:T(8,128)(2,1)S(1)}, bf16[4,16,2560]{2,1,0:T(8,128)(2,1)S(1)}, u32[]{:S(2)}, u32[]{:S(2)}) collective-permute-start(bf16[4,16,2560]{2,1,0:T(8,128)(2,1)S(1)} %collective-permute-done.13.rest_2_), channel_id=1, source_target_pairs={{0,1},{1,0},{2,3},{3,2},{4,5},{5,4},{6,7},{7,6},{8,9},{9,8},{10,11... | collective-permute-start | bytes 983048 | tf_op jit(solution)/shard_map/ppermute | solution.py:718
  46.6 2.4 %collective-permute-start.18 = (bf16[4,16,2560]{2,1,0:T(8,128)(2,1)S(1)}, bf16[4,16,2560]{2,1,0:T(8,128)(2,1)S(1)}, u32[]{:S(2)}, u32[]{:S(2)}) collective-permute-start(bf16[4,16,2560]{2,1,0:T(8,128)(2,1)S(1)} %collective-permute-done.14.rest_3_), channel_id=1, source_target_pairs={{0,1},{1,0},{2,3},{3,2},{4,5},{5,4},{6,7},{7,6},{8,9},{9,8},{10,11... | collective-permute-start | bytes 983048 | tf_op jit(solution)/shard_map/ppermute | solution.py:718
  47.0 14.0 %collective-permute-start.21 = (bf16[4,8,16,512]{3,2,1,0:T(8,128)(2,1)S(1)}, bf16[4,8,16,512]{3,2,1,0:T(8,128)(2,1)S(1)}, u32[]{:S(2)}, u32[]{:S(2)}) collective-permute-start(bf16[4,8,16,512]{3,2,1,0:T(8,128)(2,1)S(1)} %constant_dynamic-update-slice_fusion.rest_0_), channel_id=1, source_target_pairs={{0,8},{1,9},{2,10},{3,11},{4,12},{5,13},{6,14},{7,15},{8,0},{9,1},... | collective-permute-start | bytes 1572872 | tf_op jit(solution)/shard_map/ppermute | solution.py:718
  48.0 23.9 %collective-permute-start.22 = (bf16[4,8,16,512]{3,2,1,0:T(8,128)(2,1)S(1)}, bf16[4,8,16,512]{3,2,1,0:T(8,128)(2,1)S(1)}, u32[]{:S(2)}, u32[]{:S(2)}) collective-permute-start(bf16[4,8,16,512]{3,2,1,0:T(8,128)(2,1)S(1)} %constant_dynamic-update-slice_fusion.rest_0_), channel_id=1, source_target_pairs={{0,16},{1,17},{2,18},{3,19},{4,20},{5,21},{6,22},{7,23},{8,24},{9,... | collective-permute-start | bytes 1572872 | tf_op jit(solution)/shard_map/ppermute | solution.py:718
  61.0 13.1 %collective-permute-start.23 = (bf16[4,8,16,512]{3,2,1,0:T(8,128)(2,1)S(1)}, bf16[4,8,16,512]{3,2,1,0:T(8,128)(2,1)S(1)}, u32[]{:S(2)}, u32[]{:S(2)}) collective-permute-start(bf16[4,8,16,512]{3,2,1,0:T(8,128)(2,1)S(1)} %collective-permute-done.21.rest_1_), channel_id=1, source_target_pairs={{0,16},{1,17},{2,18},{3,19},{4,20},{5,21},{6,22},{7,23},{8,24},{9,... | collective-permute-start | bytes 1572872 | tf_op jit(solution)/shard_map/ppermute | solution.py:718
  62.0 13.4 %collective-permute-start.24 = (bf16[4,8,16,512]{3,2,1,0:T(8,128)(2,1)S(1)}, bf16[4,8,16,512]{3,2,1,0:T(8,128)(2,1)S(1)}, u32[]{:S(2)}, u32[]{:S(2)}) collective-permute-start(bf16[4,8,16,512]{3,2,1,0:T(8,128)(2,1)S(1)} %constant_dynamic-update-slice_fusion.rest_0_), channel_id=1, source_target_pairs={{0,1},{1,0},{2,3},{3,2},{4,5},{5,4},{6,7},{7,6},{8,9},{9,8},{10,11... | collective-permute-start | bytes 1572872 | tf_op jit(solution)/shard_map/ppermute | solution.py:718
  71.7 3.8 %collective-permute-start.25 = (bf16[4,8,16,512]{3,2,1,0:T(8,128)(2,1)S(1)}, bf16[4,8,16,512]{3,2,1,0:T(8,128)(2,1)S(1)}, u32[]{:S(2)}, u32[]{:S(2)}) collective-permute-start(bf16[4,8,16,512]{3,2,1,0:T(8,128)(2,1)S(1)} %collective-permute-done.21.rest_1_), channel_id=1, source_target_pairs={{0,1},{1,0},{2,3},{3,2},{4,5},{5,4},{6,7},{7,6},{8,9},{9,8},{10,11... | collective-permute-start | bytes 1572872 | tf_op jit(solution)/shard_map/ppermute | solution.py:718
  71.8 3.6 %collective-permute-start.26 = (bf16[4,8,16,512]{3,2,1,0:T(8,128)(2,1)S(1)}, bf16[4,8,16,512]{3,2,1,0:T(8,128)(2,1)S(1)}, u32[]{:S(2)}, u32[]{:S(2)}) collective-permute-start(bf16[4,8,16,512]{3,2,1,0:T(8,128)(2,1)S(1)} %collective-permute-done.22.rest_2_), channel_id=1, source_target_pairs={{0,1},{1,0},{2,3},{3,2},{4,5},{5,4},{6,7},{7,6},{8,9},{9,8},{10,11... | collective-permute-start | bytes 1572872 | tf_op jit(solution)/shard_map/ppermute | solution.py:718
  74.1 1.9 %collective-permute-start.27 = (bf16[4,8,16,512]{3,2,1,0:T(8,128)(2,1)S(1)}, bf16[4,8,16,512]{3,2,1,0:T(8,128)(2,1)S(1)}, u32[]{:S(2)}, u32[]{:S(2)}) collective-permute-start(bf16[4,8,16,512]{3,2,1,0:T(8,128)(2,1)S(1)} %collective-permute-done.23.rest_3_), channel_id=1, source_target_pairs={{0,1},{1,0},{2,3},{3,2},{4,5},{5,4},{6,7},{7,6},{8,9},{9,8},{10,11... | collective-permute-start | bytes 1572872 | tf_op jit(solution)/shard_map/ppermute | solution.py:718
  98.5 15.3 %collective-permute-start.28 = (bf16[16,16,4096]{2,1,0:T(8,128)(2,1)S(1)}, bf16[16,16,4096]{2,1,0:T(8,128)(2,1)S(1)}, u32[]{:S(2)}, u32[]{:S(2)}) collective-permute-start(bf16[16,16,4096]{2,1,0:T(8,128)(2,1)S(1)} %get-tuple-element.160), channel_id=1, source_target_pairs={{0,1},{1,0},{2,3},{3,2},{4,5},{5,4},{6,7},{7,6},{8,9},{9,8},{10,11... | collective-permute-start | bytes 6291464 | tf_op jit(solution)/shard_map/ppermute | solution.py:718
  114.2 13.5 %collective-permute-start.29 = (bf16[2,4,16,2048]{3,2,1,0:T(8,128)(2,1)S(1)}, bf16[2,4,16,2048]{3,2,1,0:T(8,128)(2,1)S(1)}, u32[]{:S(2)}, u32[]{:S(2)}) collective-permute-start(bf16[2,4,16,2048]{3,2,1,0:T(8,128)(2,1)S(1)} %get-tuple-element.166), channel_id=1, source_target_pairs={{0,16},{1,17},{2,18},{3,19},{4,20},{5,21},{6,22},{7,23},{8,24},{9,... | collective-permute-start | bytes 1572872 | tf_op jit(solution)/shard_map/ppermute | solution.py:718
  114.7 14.5 %collective-permute-start.30 = (bf16[2,4,16,2048]{3,2,1,0:T(8,128)(2,1)S(1)}, bf16[2,4,16,2048]{3,2,1,0:T(8,128)(2,1)S(1)}, u32[]{:S(2)}, u32[]{:S(2)}) collective-permute-start(bf16[2,4,16,2048]{3,2,1,0:T(8,128)(2,1)S(1)} %get-tuple-element.167), channel_id=1, source_target_pairs={{0,8},{1,9},{2,10},{3,11},{4,12},{5,13},{6,14},{7,15},{8,0},{9,1},... | collective-permute-start | bytes 1572872 | tf_op jit(solution)/shard_map/ppermute | solution.py:718
  129.3 2.7 %collective-permute-start.31 = (bf16[16,16,2048]{2,1,0:T(8,128)(2,1)S(1)}, bf16[16,16,2048]{2,1,0:T(8,128)(2,1)S(1)}, u32[]{:S(2)}, u32[]{:S(2)}) collective-permute-start(bf16[16,16,2048]{2,1,0:T(8,128)(2,1)S(1)} %get-tuple-element.181), channel_id=1, source_target_pairs={{0,1},{1,0},{2,3},{3,2},{4,5},{5,4},{6,7},{7,6},{8,9},{9,8},{10,11... | collective-permute-start | bytes 3145736 | tf_op jit(solution)/shard_map/ppermute | solution.py:718
  129.4 23.4 %collective-permute-start.32 = (bf16[4,16,2048]{2,1,0:T(8,128)(2,1)S(1)}, bf16[4,16,2048]{2,1,0:T(8,128)(2,1)S(1)}, u32[]{:S(2)}, u32[]{:S(2)}) collective-permute-start(bf16[4,16,2048]{2,1,0:T(8,128)(2,1)S(1)} %get-tuple-element.179), channel_id=1, source_target_pairs={{0,8},{1,9},{2,10},{3,11},{4,12},{5,13},{6,14},{7,15},{8,0},{9,1},... | collective-permute-start | bytes 786440 | tf_op jit(solution)/shard_map/ppermute | solution.py:718
  129.7 23.0 %collective-permute-start.33 = (bf16[4,16,2048]{2,1,0:T(8,128)(2,1)S(1)}, bf16[4,16,2048]{2,1,0:T(8,128)(2,1)S(1)}, u32[]{:S(2)}, u32[]{:S(2)}) collective-permute-start(bf16[4,16,2048]{2,1,0:T(8,128)(2,1)S(1)} %get-tuple-element.180), channel_id=1, source_target_pairs={{0,16},{1,17},{2,18},{3,19},{4,20},{5,21},{6,22},{7,23},{8,24},{9,... | collective-permute-start | bytes 786440 | tf_op jit(solution)/shard_map/ppermute | solution.py:718
  132.3 20.5 %collective-permute-start.34 = (bf16[4,16,2048]{2,1,0:T(8,128)(2,1)S(1)}, bf16[4,16,2048]{2,1,0:T(8,128)(2,1)S(1)}, u32[]{:S(2)}, u32[]{:S(2)}) collective-permute-start(bf16[4,16,2048]{2,1,0:T(8,128)(2,1)S(1)} %get-tuple-element.182), channel_id=1, source_target_pairs={{0,8},{1,9},{2,10},{3,11},{4,12},{5,13},{6,14},{7,15},{8,0},{9,1},... | collective-permute-start | bytes 786440 | tf_op jit(solution)/shard_map/ppermute | solution.py:718
  132.6 20.2 %collective-permute-start.35 = (bf16[4,16,2048]{2,1,0:T(8,128)(2,1)S(1)}, bf16[4,16,2048]{2,1,0:T(8,128)(2,1)S(1)}, u32[]{:S(2)}, u32[]{:S(2)}) collective-permute-start(bf16[4,16,2048]{2,1,0:T(8,128)(2,1)S(1)} %get-tuple-element.183), channel_id=1, source_target_pairs={{0,16},{1,17},{2,18},{3,19},{4,20},{5,21},{6,22},{7,23},{8,24},{9,... | collective-permute-start | bytes 786440 | tf_op jit(solution)/shard_map/ppermute | solution.py:718
  134.1 18.7 %collective-permute-start.36 = (bf16[4,16,2048]{2,1,0:T(8,128)(2,1)S(1)}, bf16[4,16,2048]{2,1,0:T(8,128)(2,1)S(1)}, u32[]{:S(2)}, u32[]{:S(2)}) collective-permute-start(bf16[4,16,2048]{2,1,0:T(8,128)(2,1)S(1)} %get-tuple-element.184), channel_id=1, source_target_pairs={{0,24},{1,25},{2,26},{3,27},{4,28},{5,29},{6,30},{7,31},{8,16},{9,... | collective-permute-start | bytes 786440 | tf_op jit(solution)/shard_map/ppermute | solution.py:718
  153.0 5.7 %collective-permute-start.38 = (bf16[16,16,2176]{2,1,0:T(8,128)(2,1)S(1)}, bf16[16,16,2176]{2,1,0:T(8,128)(2,1)S(1)}, u32[]{:S(2)}, u32[]{:S(2)}) collective-permute-start(bf16[16,16,2176]{2,1,0:T(8,128)(2,1)S(1)} %get-tuple-element.206), channel_id=1, source_target_pairs={{0,1},{1,0},{2,3},{3,2},{4,5},{5,4},{6,7},{7,6},{8,9},{9,8},{10,11... | collective-permute-start | bytes 3342344 | tf_op jit(solution)/shard_map/ppermute | solution.py:718
  153.1 21.6 %collective-permute-start.37 = (bf16[2,16,6144]{2,1,0:T(8,128)(2,1)S(1)}, bf16[2,16,6144]{2,1,0:T(8,128)(2,1)S(1)}, u32[]{:S(2)}, u32[]{:S(2)}) collective-permute-start(bf16[2,16,6144]{2,1,0:T(8,128)(2,1)S(1)} %get-tuple-element.197), channel_id=1, source_target_pairs={{0,4},{1,5},{2,6},{3,7},{4,0},{5,1},{6,2},{7,3},{8,12},{9,13},{10,... | collective-permute-start | bytes 1179656 | tf_op jit(solution)/shard_map/ppermute | solution.py:718
  159.1 26.1 %copy-start = (f32[6,16,512]{2,1,0:T(8,128)S(1)}, f32[6,16,512]{2,1,0:T(8,128)}, u32[]{:S(2)}) copy-start(f32[6,16,512]{2,1,0:T(8,128)} %rest_3_.2) | copy-start | bytes 589828
  159.2 9.6 %collective-permute-start.39 = (bf16[4,16,2176]{2,1,0:T(8,128)(2,1)S(1)}, bf16[4,16,2176]{2,1,0:T(8,128)(2,1)S(1)}, u32[]{:S(2)}, u32[]{:S(2)}) collective-permute-start(bf16[4,16,2176]{2,1,0:T(8,128)(2,1)S(1)} %get-tuple-element.209), channel_id=1, source_target_pairs={{0,8},{1,9},{2,10},{3,11},{4,12},{5,13},{6,14},{7,15},{8,0},{9,1},... | collective-permute-start | bytes 835592 | tf_op jit(solution)/shard_map/ppermute | solution.py:718
  160.4 14.1 %collective-permute-start.40 = (bf16[4,16,2176]{2,1,0:T(8,128)(2,1)S(1)}, bf16[4,16,2176]{2,1,0:T(8,128)(2,1)S(1)}, u32[]{:S(2)}, u32[]{:S(2)}) collective-permute-start(bf16[4,16,2176]{2,1,0:T(8,128)(2,1)S(1)} %get-tuple-element.210), channel_id=1, source_target_pairs={{0,16},{1,17},{2,18},{3,19},{4,20},{5,21},{6,22},{7,23},{8,24},{9,... | collective-permute-start | bytes 835592 | tf_op jit(solution)/shard_map/ppermute | solution.py:718
  160.7 13.9 %collective-permute-start.41 = (bf16[4,16,2176]{2,1,0:T(8,128)(2,1)S(1)}, bf16[4,16,2176]{2,1,0:T(8,128)(2,1)S(1)}, u32[]{:S(2)}, u32[]{:S(2)}) collective-permute-start(bf16[4,16,2176]{2,1,0:T(8,128)(2,1)S(1)} %get-tuple-element.211), channel_id=1, source_target_pairs={{0,24},{1,25},{2,26},{3,27},{4,28},{5,29},{6,30},{7,31},{8,16},{9,... | collective-permute-start | bytes 835592 | tf_op jit(solution)/shard_map/ppermute | solution.py:718
  174.8 8.9 %collective-permute-start.42 = (bf16[16,6144]{1,0:T(8,128)(2,1)S(1)}, bf16[16,6144]{1,0:T(8,128)(2,1)S(1)}, u32[]{:S(2)}, u32[]{:S(2)}) collective-permute-start(bf16[16,6144]{1,0:T(8,128)(2,1)S(1)} %get-tuple-element.217), channel_id=1, source_target_pairs={{0,2},{1,3},{2,0},{3,1},{4,6},{5,7},{6,4},{7,5},{8,10},{9,11},{10,... | collective-permute-start | bytes 589832 | tf_op jit(solution)/shard_map/ppermute | solution.py:718
  174.9 10.3 %collective-permute-start.43 = (bf16[16,2176]{1,0:T(8,128)(2,1)S(1)}, bf16[16,2176]{1,0:T(8,128)(2,1)S(1)}, u32[]{:S(2)}, u32[]{:S(2)}) collective-permute-start(bf16[16,2176]{1,0:T(8,128)(2,1)S(1)} %get-tuple-element.212), channel_id=1, source_target_pairs={{0,2},{1,3},{2,0},{3,1},{4,6},{5,7},{6,4},{7,5},{8,10},{9,11},{10,... | collective-permute-start | bytes 208904 | tf_op jit(solution)/shard_map/ppermute | solution.py:718
  176.9 8.3 %collective-permute-start.44 = (bf16[16,2176]{1,0:T(8,128)(2,1)S(1)}, bf16[16,2176]{1,0:T(8,128)(2,1)S(1)}, u32[]{:S(2)}, u32[]{:S(2)}) collective-permute-start(bf16[16,2176]{1,0:T(8,128)(2,1)S(1)} %get-tuple-element.213), channel_id=1, source_target_pairs={{0,4},{1,5},{2,6},{3,7},{4,0},{5,1},{6,2},{7,3},{8,12},{9,13},{10,... | collective-permute-start | bytes 208904 | tf_op jit(solution)/shard_map/ppermute | solution.py:718
  177.2 8.0 %collective-permute-start.45 = (bf16[16,2176]{1,0:T(8,128)(2,1)S(1)}, bf16[16,2176]{1,0:T(8,128)(2,1)S(1)}, u32[]{:S(2)}, u32[]{:S(2)}) collective-permute-start(bf16[16,2176]{1,0:T(8,128)(2,1)S(1)} %get-tuple-element.214), channel_id=1, source_target_pairs={{0,6},{1,7},{2,4},{3,5},{4,2},{5,3},{6,0},{7,1},{8,14},{9,15},{10,... | collective-permute-start | bytes 208904 | tf_op jit(solution)/shard_map/ppermute | solution.py:718
  (22 other events, 447.1 us)

commit v2 on v1

--- a/solution.py
+++ b/solution.py
@@ -255,7 +255,7 @@
             dot_nn(block, weights[:, 2 * model : 3 * model]) + vectors[1:2, :]
         ).astype(LOW)
 
-    row_steps(tokens.shape[0], project)
+    row_steps(tokens.shape[0], project, 512)
     attend_forward(row_starts, row_starts, queries, keys, values, mixed, sums)
 
 
@@ -471,7 +471,7 @@
         sums[4:5, :] += column_sum(low)
         grad_mixed[rows, :] = dot_nt(low, weights[:, :model]).astype(LOW)
 
-    row_steps(dq.shape[0], finish)
+    row_steps(dq.shape[0], finish, 512)
     core = place[0] % 2
     first_low = (unit_one[...] * (1.0 + vectors[7:8, :]) + vectors[10:11, :]).astype(LOW)
     pairs = ((first_low, dq), (encoded, dk), (encoded, dv), (cross_mixed, grad_out))

time: 187 us -> 186 us (level)
  starting transfers between devices: 37.2 us -> 42.7 us
  Pallas kernels: 100 us -> 96.8 us
  waiting for transfers between devices: 42.4 us -> 40 us
    ppermute x46, starting transfers between devices: 37.2 us -> 42.7 us  [exchange(): return lax.ppermute(values, AXES, [(i, i ^ offset) for i in range(count)])]
    pallas_call x18, Pallas kernels: 100 us -> 96.8 us  [call(): pl.pallas_call(kernel, out_shape=shapes, in_specs=specs, out_specs=[pl.Bl...]
    ppermute x46, waiting for transfers between devices: 42.4 us -> 40 us  [exchange(): return lax.ppermute(values, AXES, [(i, i ^ offset) for i in range(count)])]
  transfers between devices with their start and end apart: 46 -> 46, of which waited for: 16 -> 16; matrix products, arithmetic and copies ran while one was open for 2% -> 2% of each run, Pallas kernels for 41% -> 39%
where the time goes in v2:
time: 186 us
  Pallas kernels  96.8 us (52%)
  starting transfers between devices  42.7 us (23%)
  waiting for transfers between devices  40 us (22%)
  other arithmetic  4.8 us (3%)
    pallas_call x18, Pallas kernels, call(): pl.pallas_call(kernel, out_shape=shapes, in_specs=specs, out_specs=[pl.Bl...  96.8 us
    ppermute x46, starting transfers between devices, exchange(): return lax.ppermute(values, AXES, [(i, i ^ offset) for i in range(count)])  42.7 us
    ppermute x46, waiting for transfers between devices, exchange(): return lax.ppermute(values, AXES, [(i, i ^ offset) for i in range(count)])  40 us
  transfers between devices with their start and end apart: 46, of which 16 were waited for; matrix products, arithmetic and copies ran while one was open for 2% of the time, Pallas kernels for 39%

profile of v2, /device:TPU:0, one launch (start us, length us, event | category | flops | bytes accessed | tf_op | source)
XLA Modules:
  0.0 186.0 jit_solution(16090314328787085455)
XLA Ops:
  0.7 0.8 convert_bitcast_fusion
  1.5 0.9 convert_element_type.25
  2.4 4.1 %collective-permute-start.1 = (bf16[16,1664]{1,0:T(8,128)(2,1)S(1)}, bf16[16,1664]{1,0:T(8,128)(2,1)S(1)}, u32[]{:S(2)}, u32[]{:S(2)}) collective-permute-start(bf16[16,1664]{1,0:T(8,128)(2,1)S(1)} %fusion.1), channel_id=1, source_target_pairs={{0,4},{1,5},{2,6},{3,7},{4,0},{5,1},{6,2},{7,3},{8,12},{9,13},{10,... | collective-permute-start | bytes 159752 | tf_op jit(solution)/shard_map/ppermute | solution.py:718
  6.5 1.6 collective-permute-start
  8.1 0.8 convert_element_type.24
  9.0 0.9 convert_element_type.28
  10.0 0.9 convert_element_type.29
  10.9 3.2 %collective-permute-done.2 = bf16[16,1664]{1,0:T(8,128)(2,1)S(1)} collective-permute-done((bf16[16,1664]{1,0:T(8,128)(2,1)S(1)}, bf16[16,1664]{1,0:T(8,128)(2,1)S(1)}, u32[]{:S(2)}, u32[]{:S(2)}) %collective-permute-start.2) | collective-permute-done | bytes 53280 | tf_op jit(solution)/shard_map/ppermute | solution.py:718
  14.2 2.5 %collective-permute-start.7 = (bf16[4,16,1664]{2,1,0:T(8,128)(2,1)S(1)}, bf16[4,16,1664]{2,1,0:T(8,128)(2,1)S(1)}, u32[]{:S(2)}, u32[]{:S(2)}) collective-permute-start(bf16[4,16,1664]{2,1,0:T(8,128)(2,1)S(1)} %pad_maximum_fusion.2.rest_0_), channel_id=1, source_target_pairs={{0,24},{1,25},{2,26},{3,27},{4,28},{5,29},{6,30},{7,31},{8,16},{9,... | collective-permute-start | bytes 638984 | tf_op jit(solution)/shard_map/ppermute | solution.py:718
  17.8 2.0 %collective-permute-start.19 = (bf16[1,8,16,512]{3,2,1,0:T(8,128)(2,1)S(1)}, bf16[1,8,16,512]{3,2,1,0:T(8,128)(2,1)S(1)}, u32[]{:S(2)}, u32[]{:S(2)}) collective-permute-start(bf16[1,8,16,512]{3,2,1,0:T(8,128)(2,1)S(1)} %bitcast.56), channel_id=1, source_target_pairs={{0,2},{1,3},{2,0},{3,1},{4,6},{5,7},{6,4},{7,5},{8,10},{9,11},{10,... | collective-permute-start | bytes 393224 | tf_op jit(solution)/shard_map/ppermute | solution.py:718
  20.4 3.9 %collective-permute-done.19 = bf16[1,8,16,512]{3,2,1,0:T(8,128)(2,1)S(1)} collective-permute-done((bf16[1,8,16,512]{3,2,1,0:T(8,128)(2,1)S(1)}, bf16[1,8,16,512]{3,2,1,0:T(8,128)(2,1)S(1)}, u32[]{:S(2)}, u32[]{:S(2)}) %collective-permute-start.19) | collective-permute-done | bytes 131104 | tf_op jit(solution)/shard_map/ppermute | solution.py:718
  25.6 1.6 collective-permute-done.4
  27.6 2.5 %collective-permute-start.14 = (bf16[4,16,2560]{2,1,0:T(8,128)(2,1)S(1)}, bf16[4,16,2560]{2,1,0:T(8,128)(2,1)S(1)}, u32[]{:S(2)}, u32[]{:S(2)}) collective-permute-start(bf16[4,16,2560]{2,1,0:T(8,128)(2,1)S(1)} %pad_maximum_fusion.rest_0_), channel_id=1, source_target_pairs={{0,24},{1,25},{2,26},{3,27},{4,28},{5,29},{6,30},{7,31},{8,16},{9,... | collective-permute-start | bytes 983048 | tf_op jit(solution)/shard_map/ppermute | solution.py:718
  31.2 13.7 %self_forward.1 = (bf16[512,1664]{1,0:T(8,128)(2,1)S(1)}, f32[24,512]{1,0:T(8,128)S(1)}, bf16[1024,512]{1,0:T(8,128)(2,1)S(1)}, bf16[1024,512]{1,0:T(8,128)(2,1)...) custom-call(s32[1]{0:T(128)} %bitcast.place, ...), custom_call_target="tpu_custom_call" | custom-call | flops 6979321856 | bytes 2752512 | tf_op jit(solution)/shard_map/self_forward/pallas_call | solution.py:685
  46.1 2.1 %collective-permute-start.21 = (bf16[4,8,16,512]{3,2,1,0:T(8,128)(2,1)S(1)}, bf16[4,8,16,512]{3,2,1,0:T(8,128)(2,1)S(1)}, u32[]{:S(2)}, u32[]{:S(2)}) collective-permute-start(bf16[4,8,16,512]{3,2,1,0:T(8,128)(2,1)S(1)} %constant_dynamic-update-slice_fusion.rest_0_), channel_id=1, source_target_pairs={{0,8},{1,9},{2,10},{3,11},{4,12},{5,13},{6,14},{7,15},{8,0},{9,1},... | collective-permute-start | bytes 1572872 | tf_op jit(solution)/shard_map/ppermute | solution.py:718
  48.2 1.0 collective-permute-start.22
  49.2 6.8 %cross_project.1 = (bf16[512,2560]{1,0:T(8,128)(2,1)S(1)}, f32[1024,512]{1,0:T(8,128)S(1)}, f32[1024,1]{1,0:T(8,128)S(1)}, bf16[1024,512]{1,0:T(8,128)(2,1)S(1)}...) custom-call(s32[1]{0:T(128)} %bitcast.place, bf16[1024,512]{1,0:T(8,128)(2,1)S(1)} %copy-done.17, ...), custom_call_target="tpu_custom_call" | custom-call | flops 2147483648 | bytes 5816320 | tf_op jit(solution)/shard_map/cross_project/pallas_call | solution.py:685
  56.0 4.3 %collective-permute-done.21.rest_1_ = bf16[4,8,16,512]{3,2,1,0:T(8,128)(2,1)S(1)} collective-permute-done((bf16[4,8,16,512]{3,2,1,0:T(8,128)(2,1)S(1)}, bf16[4,8,16,512]{3,2,1,0:T(8,128)(2,1)S(1)}, u32[]{:S(2)}, u32[]{:S(2)}) %collective-permute-start.21) | collective-permute-done | bytes 524320 | tf_op jit(solution)/shard_map/ppermute | solution.py:718
  60.3 1.0 collective-permute-start.23
  61.5 9.2 %cross_attend.1 = (bf16[1024,512]{1,0:T(8,128)(2,1)S(1)}, f32[20,1024]{1,0:T(8,128)S(1)}) custom-call(s32[11]{0:T(128)S(1)} %convert_reduce_fusion.1.row_starts, s32[11]{0:T(128)S(1)} %convert_reduce_fusion.col_starts, bf16[1024,512]{1,0:T(8,128)(2,1)S(1)} %get-tuple-element.141.queries, bf16[1024,512]{1,0:T(8,128)(2,1)S(1)} %get-tuple-element.142.keys, ...), custom_call_target="tpu_custom_call" | custom-call | flops 5368709120 | bytes 3145728 | tf_op jit(solution)/shard_map/cross_attend/pallas_call | solution.py:685
  71.3 2.4 %collective-permute-done.23.rest_3_ = bf16[4,8,16,512]{3,2,1,0:T(8,128)(2,1)S(1)} collective-permute-done((bf16[4,8,16,512]{3,2,1,0:T(8,128)(2,1)S(1)}, bf16[4,8,16,512]{3,2,1,0:T(8,128)(2,1)S(1)}, u32[]{:S(2)}, u32[]{:S(2)}) %collective-permute-start.23) | collective-permute-done | bytes 524320 | tf_op jit(solution)/shard_map/ppermute | solution.py:718
  73.7 1.4 cross_finish.1
  75.6 22.5 %ffn.1 = (bf16[1024,512]{1,0:T(8,128)(2,1)}, f32[1024,512]{1,0:T(8,128)S(1)}, bf16[1024,512]{1,0:T(8,128)(2,1)S(1)}, f32[8,512]{1,0:T(8,128)S(1)}, f32[8,512]{1,...) custom-call(s32[1]{0:T(128)} %bitcast.place, ...), custom_call_target="tpu_custom_call" | custom-call | flops 11274289152 | bytes 7393280 | tf_op jit(solution)/shard_map/ffn/pallas_call | solution.py:685
  98.4 14.3 %cross_backward.1 = (bf16[1024,512]{1,0:T(8,128)(2,1)S(1)}, bf16[1024,512]{1,0:T(8,128)(2,1)S(1)}, bf16[1024,512]{1,0:T(8,128)(2,1)S(1)}) custom-call(s32[11]{0:T(128)S(1)} %convert_reduce_fusion.1.row_starts, s32[11]{0:T(128)S(1)} %convert_reduce_fusion.col_starts, bf16[1024,512]{1,0:T(8,128)(2,1)S(1)} %get-tuple-element.141.queries, ...), custom_call_target="tpu_custom_call" | custom-call | flops 13421772800 | bytes 6897664 | tf_op jit(solution)/shard_map/cross_backward/pallas_call | solution.py:685
  113.3 1.7 collective-permute-start.30
  115.0 6.0 %cross_grads.1 = (f32[1024,512]{1,0:T(8,128)S(1)}, bf16[1024,512]{1,0:T(8,128)(2,1)S(1)}, bf16[1024,512]{1,0:T(8,128)(2,1)S(1)}, f32[8,512]{1,0:T(8,128)S(1)}, f...) custom-call(s32[1]{0:T(128)} %bitcast.place, ...), custom_call_target="tpu_custom_call" | custom-call | flops 4294967296 | bytes 13160448 | tf_op jit(solution)/shard_map/cross_grads/pallas_call | solution.py:685
  121.0 5.8 %collective-permute-done.29.got_first = bf16[2,4,16,2048]{3,2,1,0:T(8,128)(2,1)S(1)} collective-permute-done((bf16[2,4,16,2048]{3,2,1,0:T(8,128)(2,1)S(1)}, bf16[2,4,16,2048]{3,2,1,0:T(8,128)(2,1)S(1)}, u32[]{:S(2)}, u32[]{:S(2)}) %collective-permute-start.29) | collective-permute-done | bytes 524320 | tf_op jit(solution)/shard_map/ppermute | solution.py:718
  126.8 1.0 collective-permute-done.30.got_second
  128.2 1.7 collective-permute-start.32
  129.9 1.2 collective-permute-start.33
  131.3 1.2 collective-permute-start.34
  132.6 1.4 collective-permute-start.35
  134.0 0.9 collective-permute-start.36
  134.9 15.9 %self_backward.1 = (bf16[1024,512]{1,0:T(8,128)(2,1)S(1)}, bf16[1024,512]{1,0:T(8,128)(2,1)S(1)}, bf16[1024,512]{1,0:T(8,128)(2,1)S(1)}, bf16[16,16,2176]{2,1,0:T(8,128)(2,1)S(1)}, bf16[16,16,2176]{2,1,0:T(8,128)(2,1)S(1)}) custom-call(s32[1]{0:T(128)} %bitcast.place, s32[11]{0:T(128)S(1)} %convert_reduce_fusion.1.row_starts, ...), custom_call_target="tpu_custom_call" | custom-call | flops 15569256448 | bytes 7471104 | tf_op jit(solution)/shard_map/self_backward/pallas_call | solution.py:685
  151.1 2.1 %collective-permute-start.37 = (bf16[2,16,6144]{2,1,0:T(8,128)(2,1)S(1)}, bf16[2,16,6144]{2,1,0:T(8,128)(2,1)S(1)}, u32[]{:S(2)}, u32[]{:S(2)}) collective-permute-start(bf16[2,16,6144]{2,1,0:T(8,128)(2,1)S(1)} %get-tuple-element.197), channel_id=1, source_target_pairs={{0,4},{1,5},{2,6},{3,7},{4,0},{5,1},{6,2},{7,3},{8,12},{9,13},{10,... | collective-permute-start | bytes 1179656 | tf_op jit(solution)/shard_map/ppermute | solution.py:718
  153.2 3.3 %tokens_grad.1 = f32[1024,512]{1,0:T(8,128)} custom-call(bf16[1024,512]{1,0:T(8,128)(2,1)S(1)} %get-tuple-element.198.dq, bf16[1024,512]{1,0:T(8,128)(2,1)S(1)} %get-tuple-element.199.dk, bf16[1024,512]{1,0:T(8,128)(2,1)S(1)} %get-tuple-element.200.dv, f32[1024,512]{1,0:T(8,128)S(1)} %get-tuple-element.201.first_sum, ...), custom_call_target="tpu_custom_call" | custom-call | flops 1610612736 | bytes 6946816 | tf_op jit(solution)/shard_map/tokens_grad/pallas_call | solution.py:685
  157.7 1.4 collective-permute-start.40
  159.1 1.4 collective-permute-start.41
  160.5 6.0 %collective-permute-done.39.rest_0_ = bf16[4,16,2176]{2,1,0:T(8,128)(2,1)S(1)} collective-permute-done((bf16[4,16,2176]{2,1,0:T(8,128)(2,1)S(1)}, bf16[4,16,2176]{2,1,0:T(8,128)(2,1)S(1)}, u32[]{:S(2)}, u32[]{:S(2)}) %collective-permute-start.39) | collective-permute-done | bytes 278560 | tf_op jit(solution)/shard_map/ppermute | solution.py:718
  166.5 4.6 %collective-permute-done.40.rest_1_ = bf16[4,16,2176]{2,1,0:T(8,128)(2,1)S(1)} collective-permute-done((bf16[4,16,2176]{2,1,0:T(8,128)(2,1)S(1)}, bf16[4,16,2176]{2,1,0:T(8,128)(2,1)S(1)}, u32[]{:S(2)}, u32[]{:S(2)}) %collective-permute-start.40) | collective-permute-done | bytes 278560 | tf_op jit(solution)/shard_map/ppermute | solution.py:718
  171.1 1.3 collective-permute-done.41.rest_2_
  172.6 1.4 collective-permute-start.42
  174.7 2.2 %collective-permute-start.44 = (bf16[16,2176]{1,0:T(8,128)(2,1)S(1)}, bf16[16,2176]{1,0:T(8,128)(2,1)S(1)}, u32[]{:S(2)}, u32[]{:S(2)}) collective-permute-start(bf16[16,2176]{1,0:T(8,128)(2,1)S(1)} %get-tuple-element.213), channel_id=1, source_target_pairs={{0,4},{1,5},{2,6},{3,7},{4,0},{5,1},{6,2},{7,3},{8,12},{9,13},{10,... | collective-permute-start | bytes 208904 | tf_op jit(solution)/shard_map/ppermute | solution.py:718
  176.9 1.5 collective-permute-start.45
  178.4 2.6 %collective-permute-done.42.got = bf16[16,6144]{1,0:T(8,128)(2,1)S(1)} collective-permute-done((bf16[16,6144]{1,0:T(8,128)(2,1)S(1)}, bf16[16,6144]{1,0:T(8,128)(2,1)S(1)}, u32[]{:S(2)}, u32[]{:S(2)}) %collective-permute-start.42) | collective-permute-done | bytes 196640 | tf_op jit(solution)/shard_map/ppermute | solution.py:718
  181.1 1.1 ffn_update.1
  182.5 2.2 %collective-permute-done.45.rest_2_ = bf16[16,2176]{1,0:T(8,128)(2,1)S(1)} collective-permute-done((bf16[16,2176]{1,0:T(8,128)(2,1)S(1)}, bf16[16,2176]{1,0:T(8,128)(2,1)S(1)}, u32[]{:S(2)}, u32[]{:S(2)}) %collective-permute-start.45) | collective-permute-done | bytes 69664 | tf_op jit(solution)/shard_map/ppermute | solution.py:718
  184.7 1.1 final_update.1
  (133 shorter events, 11.1 us)
Async XLA Ops:
  0.7 30.5 %copy-start.17 = (bf16[1024,512]{1,0:T(8,128)(2,1)S(1)}, bf16[1024,512]{1,0:T(8,128)(2,1)}, u32[]{:S(2)}) copy-start(bf16[1024,512]{1,0:T(8,128)(2,1)} %tokens.4) | copy-start | bytes 3145732
  2.4 8.4 %collective-permute-start.1 = (bf16[16,1664]{1,0:T(8,128)(2,1)S(1)}, bf16[16,1664]{1,0:T(8,128)(2,1)S(1)}, u32[]{:S(2)}, u32[]{:S(2)}) collective-permute-start(bf16[16,1664]{1,0:T(8,128)(2,1)S(1)} %fusion.1), channel_id=1, source_target_pairs={{0,4},{1,5},{2,6},{3,7},{4,0},{5,1},{6,2},{7,3},{8,12},{9,13},{10,... | collective-permute-start | bytes 159752 | tf_op jit(solution)/shard_map/ppermute | solution.py:718
  6.5 4.3 %collective-permute-start = (bf16[16,1664]{1,0:T(8,128)(2,1)S(1)}, bf16[16,1664]{1,0:T(8,128)(2,1)S(1)}, u32[]{:S(2)}, u32[]{:S(2)}) collective-permute-start(bf16[16,1664]{1,0:T(8,128)(2,1)S(1)} %fusion.1), channel_id=1, source_target_pairs={{0,2},{1,3},{2,0},{3,1},{4,6},{5,7},{6,4},{7,5},{8,10},{9,11},{10,... | collective-permute-start | bytes 159752 | tf_op jit(solution)/shard_map/ppermute | solution.py:718
  8.1 5.9 %collective-permute-start.2 = (bf16[16,1664]{1,0:T(8,128)(2,1)S(1)}, bf16[16,1664]{1,0:T(8,128)(2,1)S(1)}, u32[]{:S(2)}, u32[]{:S(2)}) collective-permute-start(bf16[16,1664]{1,0:T(8,128)(2,1)S(1)} %fusion.1), channel_id=1, source_target_pairs={{0,6},{1,7},{2,4},{3,5},{4,2},{5,3},{6,0},{7,1},{8,14},{9,15},{10,... | collective-permute-start | bytes 159752 | tf_op jit(solution)/shard_map/ppermute | solution.py:718
  14.1 5.7 %collective-permute-start.3 = (bf16[1,16,2560]{2,1,0:T(8,128)(2,1)S(1)}, bf16[1,16,2560]{2,1,0:T(8,128)(2,1)S(1)}, u32[]{:S(2)}, u32[]{:S(2)}) collective-permute-start(bf16[1,16,2560]{2,1,0:T(8,128)(2,1)S(1)} %bitcast.58), channel_id=1, source_target_pairs={{0,2},{1,3},{2,0},{3,1},{4,6},{5,7},{6,4},{7,5},{8,10},{9,11},{10,... | collective-permute-start | bytes 245768 | tf_op jit(solution)/shard_map/ppermute | solution.py:718
  14.2 10.1 %collective-permute-start.7 = (bf16[4,16,1664]{2,1,0:T(8,128)(2,1)S(1)}, bf16[4,16,1664]{2,1,0:T(8,128)(2,1)S(1)}, u32[]{:S(2)}, u32[]{:S(2)}) collective-permute-start(bf16[4,16,1664]{2,1,0:T(8,128)(2,1)S(1)} %pad_maximum_fusion.2.rest_0_), channel_id=1, source_target_pairs={{0,24},{1,25},{2,26},{3,27},{4,28},{5,29},{6,30},{7,31},{8,16},{9,... | collective-permute-start | bytes 638984 | tf_op jit(solution)/shard_map/ppermute | solution.py:718
  16.7 8.4 %collective-permute-start.6 = (bf16[4,16,1664]{2,1,0:T(8,128)(2,1)S(1)}, bf16[4,16,1664]{2,1,0:T(8,128)(2,1)S(1)}, u32[]{:S(2)}, u32[]{:S(2)}) collective-permute-start(bf16[4,16,1664]{2,1,0:T(8,128)(2,1)S(1)} %pad_maximum_fusion.2.rest_0_), channel_id=1, source_target_pairs={{0,16},{1,17},{2,18},{3,19},{4,20},{5,21},{6,22},{7,23},{8,24},{9,... | collective-permute-start | bytes 638984 | tf_op jit(solution)/shard_map/ppermute | solution.py:718
  17.2 8.0 %collective-permute-start.5 = (bf16[4,16,1664]{2,1,0:T(8,128)(2,1)S(1)}, bf16[4,16,1664]{2,1,0:T(8,128)(2,1)S(1)}, u32[]{:S(2)}, u32[]{:S(2)}) collective-permute-start(bf16[4,16,1664]{2,1,0:T(8,128)(2,1)S(1)} %pad_maximum_fusion.2.rest_0_), channel_id=1, source_target_pairs={{0,8},{1,9},{2,10},{3,11},{4,12},{5,13},{6,14},{7,15},{8,0},{9,1},... | collective-permute-start | bytes 638984 | tf_op jit(solution)/shard_map/ppermute | solution.py:718
  17.8 6.5 %collective-permute-start.19 = (bf16[1,8,16,512]{3,2,1,0:T(8,128)(2,1)S(1)}, bf16[1,8,16,512]{3,2,1,0:T(8,128)(2,1)S(1)}, u32[]{:S(2)}, u32[]{:S(2)}) collective-permute-start(bf16[1,8,16,512]{3,2,1,0:T(8,128)(2,1)S(1)} %bitcast.56), channel_id=1, source_target_pairs={{0,2},{1,3},{2,0},{3,1},{4,6},{5,7},{6,4},{7,5},{8,10},{9,11},{10,... | collective-permute-start | bytes 393224 | tf_op jit(solution)/shard_map/ppermute | solution.py:718
  19.8 7.5 %collective-permute-start.4 = (bf16[2,16,2560]{2,1,0:T(8,128)(2,1)S(1)}, bf16[2,16,2560]{2,1,0:T(8,128)(2,1)S(1)}, u32[]{:S(2)}, u32[]{:S(2)}) collective-permute-start(bf16[2,16,2560]{2,1,0:T(8,128)(2,1)S(1)} %pad_maximum_fusion.3), channel_id=1, source_target_pairs={{0,4},{1,5},{2,6},{3,7},{4,0},{5,1},{6,2},{7,3},{8,12},{9,13},{10,... | collective-permute-start | bytes 491528 | tf_op jit(solution)/shard_map/ppermute | solution.py:718
  24.3 3.3 %collective-permute-start.8 = (bf16[4,16,1664]{2,1,0:T(8,128)(2,1)S(1)}, bf16[4,16,1664]{2,1,0:T(8,128)(2,1)S(1)}, u32[]{:S(2)}, u32[]{:S(2)}) collective-permute-start(bf16[4,16,1664]{2,1,0:T(8,128)(2,1)S(1)} %pad_maximum_fusion.2.rest_0_), channel_id=1, source_target_pairs={{0,1},{1,0},{2,3},{3,2},{4,5},{5,4},{6,7},{7,6},{8,9},{9,8},{10,11... | collective-permute-start | bytes 638984 | tf_op jit(solution)/shard_map/ppermute | solution.py:718
  24.3 5.8 %collective-permute-start.11 = (bf16[4,16,1664]{2,1,0:T(8,128)(2,1)S(1)}, bf16[4,16,1664]{2,1,0:T(8,128)(2,1)S(1)}, u32[]{:S(2)}, u32[]{:S(2)}) collective-permute-start(bf16[4,16,1664]{2,1,0:T(8,128)(2,1)S(1)} %collective-permute-done.7.rest_3_), channel_id=1, source_target_pairs={{0,1},{1,0},{2,3},{3,2},{4,5},{5,4},{6,7},{7,6},{8,9},{9,8},{10,11... | collective-permute-start | bytes 638984 | tf_op jit(solution)/shard_map/ppermute | solution.py:718
  25.1 5.5 %collective-permute-start.10 = (bf16[4,16,1664]{2,1,0:T(8,128)(2,1)S(1)}, bf16[4,16,1664]{2,1,0:T(8,128)(2,1)S(1)}, u32[]{:S(2)}, u32[]{:S(2)}) collective-permute-start(bf16[4,16,1664]{2,1,0:T(8,128)(2,1)S(1)} %collective-permute-done.6.rest_2_), channel_id=1, source_target_pairs={{0,1},{1,0},{2,3},{3,2},{4,5},{5,4},{6,7},{7,6},{8,9},{9,8},{10,11... | collective-permute-start | bytes 638984 | tf_op jit(solution)/shard_map/ppermute | solution.py:718
  25.2 6.0 %collective-permute-start.9 = (bf16[4,16,1664]{2,1,0:T(8,128)(2,1)S(1)}, bf16[4,16,1664]{2,1,0:T(8,128)(2,1)S(1)}, u32[]{:S(2)}, u32[]{:S(2)}) collective-permute-start(bf16[4,16,1664]{2,1,0:T(8,128)(2,1)S(1)} %collective-permute-done.5.rest_1_), channel_id=1, source_target_pairs={{0,1},{1,0},{2,3},{3,2},{4,5},{5,4},{6,7},{7,6},{8,9},{9,8},{10,11... | collective-permute-start | bytes 638984 | tf_op jit(solution)/shard_map/ppermute | solution.py:718
  27.3 18.7 %collective-permute-start.20 = (bf16[2,8,16,512]{3,2,1,0:T(8,128)(2,1)S(1)}, bf16[2,8,16,512]{3,2,1,0:T(8,128)(2,1)S(1)}, u32[]{:S(2)}, u32[]{:S(2)}) collective-permute-start(bf16[2,8,16,512]{3,2,1,0:T(8,128)(2,1)S(1)} %pad_maximum_fusion.1), channel_id=1, source_target_pairs={{0,4},{1,5},{2,6},{3,7},{4,0},{5,1},{6,2},{7,3},{8,12},{9,13},{10,... | collective-permute-start | bytes 786440 | tf_op jit(solution)/shard_map/ppermute | solution.py:718
  27.6 17.3 %collective-permute-start.14 = (bf16[4,16,2560]{2,1,0:T(8,128)(2,1)S(1)}, bf16[4,16,2560]{2,1,0:T(8,128)(2,1)S(1)}, u32[]{:S(2)}, u32[]{:S(2)}) collective-permute-start(bf16[4,16,2560]{2,1,0:T(8,128)(2,1)S(1)} %pad_maximum_fusion.rest_0_), channel_id=1, source_target_pairs={{0,24},{1,25},{2,26},{3,27},{4,28},{5,29},{6,30},{7,31},{8,16},{9,... | collective-permute-start | bytes 983048 | tf_op jit(solution)/shard_map/ppermute | solution.py:718
  30.1 14.8 %collective-permute-start.13 = (bf16[4,16,2560]{2,1,0:T(8,128)(2,1)S(1)}, bf16[4,16,2560]{2,1,0:T(8,128)(2,1)S(1)}, u32[]{:S(2)}, u32[]{:S(2)}) collective-permute-start(bf16[4,16,2560]{2,1,0:T(8,128)(2,1)S(1)} %pad_maximum_fusion.rest_0_), channel_id=1, source_target_pairs={{0,16},{1,17},{2,18},{3,19},{4,20},{5,21},{6,22},{7,23},{8,24},{9,... | collective-permute-start | bytes 983048 | tf_op jit(solution)/shard_map/ppermute | solution.py:718
  30.7 14.3 %collective-permute-start.12 = (bf16[4,16,2560]{2,1,0:T(8,128)(2,1)S(1)}, bf16[4,16,2560]{2,1,0:T(8,128)(2,1)S(1)}, u32[]{:S(2)}, u32[]{:S(2)}) collective-permute-start(bf16[4,16,2560]{2,1,0:T(8,128)(2,1)S(1)} %pad_maximum_fusion.rest_0_), channel_id=1, source_target_pairs={{0,8},{1,9},{2,10},{3,11},{4,12},{5,13},{6,14},{7,15},{8,0},{9,1},... | collective-permute-start | bytes 983048 | tf_op jit(solution)/shard_map/ppermute | solution.py:718
  44.9 3.3 %collective-permute-start.15 = (bf16[4,16,2560]{2,1,0:T(8,128)(2,1)S(1)}, bf16[4,16,2560]{2,1,0:T(8,128)(2,1)S(1)}, u32[]{:S(2)}, u32[]{:S(2)}) collective-permute-start(bf16[4,16,2560]{2,1,0:T(8,128)(2,1)S(1)} %pad_maximum_fusion.rest_0_), channel_id=1, source_target_pairs={{0,1},{1,0},{2,3},{3,2},{4,5},{5,4},{6,7},{7,6},{8,9},{9,8},{10,11... | collective-permute-start | bytes 983048 | tf_op jit(solution)/shard_map/ppermute | solution.py:718
  45.0 4.2 %collective-permute-start.16 = (bf16[4,16,2560]{2,1,0:T(8,128)(2,1)S(1)}, bf16[4,16,2560]{2,1,0:T(8,128)(2,1)S(1)}, u32[]{:S(2)}, u32[]{:S(2)}) collective-permute-start(bf16[4,16,2560]{2,1,0:T(8,128)(2,1)S(1)} %collective-permute-done.12.rest_1_), channel_id=1, source_target_pairs={{0,1},{1,0},{2,3},{3,2},{4,5},{5,4},{6,7},{7,6},{8,9},{9,8},{10,11... | collective-permute-start | bytes 983048 | tf_op jit(solution)/shard_map/ppermute | solution.py:718
  45.5 3.6 %collective-permute-start.17 = (bf16[4,16,2560]{2,1,0:T(8,128)(2,1)S(1)}, bf16[4,16,2560]{2,1,0:T(8,128)(2,1)S(1)}, u32[]{:S(2)}, u32[]{:S(2)}) collective-permute-start(bf16[4,16,2560]{2,1,0:T(8,128)(2,1)S(1)} %collective-permute-done.13.rest_2_), channel_id=1, source_target_pairs={{0,1},{1,0},{2,3},{3,2},{4,5},{5,4},{6,7},{7,6},{8,9},{9,8},{10,11... | collective-permute-start | bytes 983048 | tf_op jit(solution)/shard_map/ppermute | solution.py:718
  45.6 3.5 %collective-permute-start.18 = (bf16[4,16,2560]{2,1,0:T(8,128)(2,1)S(1)}, bf16[4,16,2560]{2,1,0:T(8,128)(2,1)S(1)}, u32[]{:S(2)}, u32[]{:S(2)}) collective-permute-start(bf16[4,16,2560]{2,1,0:T(8,128)(2,1)S(1)} %collective-permute-done.14.rest_3_), channel_id=1, source_target_pairs={{0,1},{1,0},{2,3},{3,2},{4,5},{5,4},{6,7},{7,6},{8,9},{9,8},{10,11... | collective-permute-start | bytes 983048 | tf_op jit(solution)/shard_map/ppermute | solution.py:718
  46.1 14.3 %collective-permute-start.21 = (bf16[4,8,16,512]{3,2,1,0:T(8,128)(2,1)S(1)}, bf16[4,8,16,512]{3,2,1,0:T(8,128)(2,1)S(1)}, u32[]{:S(2)}, u32[]{:S(2)}) collective-permute-start(bf16[4,8,16,512]{3,2,1,0:T(8,128)(2,1)S(1)} %constant_dynamic-update-slice_fusion.rest_0_), channel_id=1, source_target_pairs={{0,8},{1,9},{2,10},{3,11},{4,12},{5,13},{6,14},{7,15},{8,0},{9,1},... | collective-permute-start | bytes 1572872 | tf_op jit(solution)/shard_map/ppermute | solution.py:718
  48.2 22.8 %collective-permute-start.22 = (bf16[4,8,16,512]{3,2,1,0:T(8,128)(2,1)S(1)}, bf16[4,8,16,512]{3,2,1,0:T(8,128)(2,1)S(1)}, u32[]{:S(2)}, u32[]{:S(2)}) collective-permute-start(bf16[4,8,16,512]{3,2,1,0:T(8,128)(2,1)S(1)} %constant_dynamic-update-slice_fusion.rest_0_), channel_id=1, source_target_pairs={{0,16},{1,17},{2,18},{3,19},{4,20},{5,21},{6,22},{7,23},{8,24},{9,... | collective-permute-start | bytes 1572872 | tf_op jit(solution)/shard_map/ppermute | solution.py:718
  60.3 13.4 %collective-permute-start.23 = (bf16[4,8,16,512]{3,2,1,0:T(8,128)(2,1)S(1)}, bf16[4,8,16,512]{3,2,1,0:T(8,128)(2,1)S(1)}, u32[]{:S(2)}, u32[]{:S(2)}) collective-permute-start(bf16[4,8,16,512]{3,2,1,0:T(8,128)(2,1)S(1)} %collective-permute-done.21.rest_1_), channel_id=1, source_target_pairs={{0,16},{1,17},{2,18},{3,19},{4,20},{5,21},{6,22},{7,23},{8,24},{9,... | collective-permute-start | bytes 1572872 | tf_op jit(solution)/shard_map/ppermute | solution.py:718
  61.4 13.7 %collective-permute-start.24 = (bf16[4,8,16,512]{3,2,1,0:T(8,128)(2,1)S(1)}, bf16[4,8,16,512]{3,2,1,0:T(8,128)(2,1)S(1)}, u32[]{:S(2)}, u32[]{:S(2)}) collective-permute-start(bf16[4,8,16,512]{3,2,1,0:T(8,128)(2,1)S(1)} %constant_dynamic-update-slice_fusion.rest_0_), channel_id=1, source_target_pairs={{0,1},{1,0},{2,3},{3,2},{4,5},{5,4},{6,7},{7,6},{8,9},{9,8},{10,11... | collective-permute-start | bytes 1572872 | tf_op jit(solution)/shard_map/ppermute | solution.py:718
  70.7 4.4 %collective-permute-start.25 = (bf16[4,8,16,512]{3,2,1,0:T(8,128)(2,1)S(1)}, bf16[4,8,16,512]{3,2,1,0:T(8,128)(2,1)S(1)}, u32[]{:S(2)}, u32[]{:S(2)}) collective-permute-start(bf16[4,8,16,512]{3,2,1,0:T(8,128)(2,1)S(1)} %collective-permute-done.21.rest_1_), channel_id=1, source_target_pairs={{0,1},{1,0},{2,3},{3,2},{4,5},{5,4},{6,7},{7,6},{8,9},{9,8},{10,11... | collective-permute-start | bytes 1572872 | tf_op jit(solution)/shard_map/ppermute | solution.py:718
  71.0 4.2 %collective-permute-start.26 = (bf16[4,8,16,512]{3,2,1,0:T(8,128)(2,1)S(1)}, bf16[4,8,16,512]{3,2,1,0:T(8,128)(2,1)S(1)}, u32[]{:S(2)}, u32[]{:S(2)}) collective-permute-start(bf16[4,8,16,512]{3,2,1,0:T(8,128)(2,1)S(1)} %collective-permute-done.22.rest_2_), channel_id=1, source_target_pairs={{0,1},{1,0},{2,3},{3,2},{4,5},{5,4},{6,7},{7,6},{8,9},{9,8},{10,11... | collective-permute-start | bytes 1572872 | tf_op jit(solution)/shard_map/ppermute | solution.py:718
  73.7 1.9 %collective-permute-start.27 = (bf16[4,8,16,512]{3,2,1,0:T(8,128)(2,1)S(1)}, bf16[4,8,16,512]{3,2,1,0:T(8,128)(2,1)S(1)}, u32[]{:S(2)}, u32[]{:S(2)}) collective-permute-start(bf16[4,8,16,512]{3,2,1,0:T(8,128)(2,1)S(1)} %collective-permute-done.23.rest_3_), channel_id=1, source_target_pairs={{0,1},{1,0},{2,3},{3,2},{4,5},{5,4},{6,7},{7,6},{8,9},{9,8},{10,11... | collective-permute-start | bytes 1572872 | tf_op jit(solution)/shard_map/ppermute | solution.py:718
  98.2 14.5 %collective-permute-start.28 = (bf16[16,16,4096]{2,1,0:T(8,128)(2,1)S(1)}, bf16[16,16,4096]{2,1,0:T(8,128)(2,1)S(1)}, u32[]{:S(2)}, u32[]{:S(2)}) collective-permute-start(bf16[16,16,4096]{2,1,0:T(8,128)(2,1)S(1)} %get-tuple-element.160), channel_id=1, source_target_pairs={{0,1},{1,0},{2,3},{3,2},{4,5},{5,4},{6,7},{7,6},{8,9},{9,8},{10,11... | collective-permute-start | bytes 6291464 | tf_op jit(solution)/shard_map/ppermute | solution.py:718
  113.1 13.7 %collective-permute-start.29 = (bf16[2,4,16,2048]{3,2,1,0:T(8,128)(2,1)S(1)}, bf16[2,4,16,2048]{3,2,1,0:T(8,128)(2,1)S(1)}, u32[]{:S(2)}, u32[]{:S(2)}) collective-permute-start(bf16[2,4,16,2048]{3,2,1,0:T(8,128)(2,1)S(1)} %get-tuple-element.166), channel_id=1, source_target_pairs={{0,16},{1,17},{2,18},{3,19},{4,20},{5,21},{6,22},{7,23},{8,24},{9,... | collective-permute-start | bytes 1572872 | tf_op jit(solution)/shard_map/ppermute | solution.py:718
  113.3 14.5 %collective-permute-start.30 = (bf16[2,4,16,2048]{3,2,1,0:T(8,128)(2,1)S(1)}, bf16[2,4,16,2048]{3,2,1,0:T(8,128)(2,1)S(1)}, u32[]{:S(2)}, u32[]{:S(2)}) collective-permute-start(bf16[2,4,16,2048]{3,2,1,0:T(8,128)(2,1)S(1)} %get-tuple-element.167), channel_id=1, source_target_pairs={{0,8},{1,9},{2,10},{3,11},{4,12},{5,13},{6,14},{7,15},{8,0},{9,1},... | collective-permute-start | bytes 1572872 | tf_op jit(solution)/shard_map/ppermute | solution.py:718
  128.0 3.2 %collective-permute-start.31 = (bf16[16,16,2048]{2,1,0:T(8,128)(2,1)S(1)}, bf16[16,16,2048]{2,1,0:T(8,128)(2,1)S(1)}, u32[]{:S(2)}, u32[]{:S(2)}) collective-permute-start(bf16[16,16,2048]{2,1,0:T(8,128)(2,1)S(1)} %get-tuple-element.181), channel_id=1, source_target_pairs={{0,1},{1,0},{2,3},{3,2},{4,5},{5,4},{6,7},{7,6},{8,9},{9,8},{10,11... | collective-permute-start | bytes 3145736 | tf_op jit(solution)/shard_map/ppermute | solution.py:718
  128.2 22.6 %collective-permute-start.32 = (bf16[4,16,2048]{2,1,0:T(8,128)(2,1)S(1)}, bf16[4,16,2048]{2,1,0:T(8,128)(2,1)S(1)}, u32[]{:S(2)}, u32[]{:S(2)}) collective-permute-start(bf16[4,16,2048]{2,1,0:T(8,128)(2,1)S(1)} %get-tuple-element.179), channel_id=1, source_target_pairs={{0,8},{1,9},{2,10},{3,11},{4,12},{5,13},{6,14},{7,15},{8,0},{9,1},... | collective-permute-start | bytes 786440 | tf_op jit(solution)/shard_map/ppermute | solution.py:718
  129.9 20.9 %collective-permute-start.33 = (bf16[4,16,2048]{2,1,0:T(8,128)(2,1)S(1)}, bf16[4,16,2048]{2,1,0:T(8,128)(2,1)S(1)}, u32[]{:S(2)}, u32[]{:S(2)}) collective-permute-start(bf16[4,16,2048]{2,1,0:T(8,128)(2,1)S(1)} %get-tuple-element.180), channel_id=1, source_target_pairs={{0,16},{1,17},{2,18},{3,19},{4,20},{5,21},{6,22},{7,23},{8,24},{9,... | collective-permute-start | bytes 786440 | tf_op jit(solution)/shard_map/ppermute | solution.py:718
  131.3 19.5 %collective-permute-start.34 = (bf16[4,16,2048]{2,1,0:T(8,128)(2,1)S(1)}, bf16[4,16,2048]{2,1,0:T(8,128)(2,1)S(1)}, u32[]{:S(2)}, u32[]{:S(2)}) collective-permute-start(bf16[4,16,2048]{2,1,0:T(8,128)(2,1)S(1)} %get-tuple-element.182), channel_id=1, source_target_pairs={{0,8},{1,9},{2,10},{3,11},{4,12},{5,13},{6,14},{7,15},{8,0},{9,1},... | collective-permute-start | bytes 786440 | tf_op jit(solution)/shard_map/ppermute | solution.py:718
  132.6 18.2 %collective-permute-start.35 = (bf16[4,16,2048]{2,1,0:T(8,128)(2,1)S(1)}, bf16[4,16,2048]{2,1,0:T(8,128)(2,1)S(1)}, u32[]{:S(2)}, u32[]{:S(2)}) collective-permute-start(bf16[4,16,2048]{2,1,0:T(8,128)(2,1)S(1)} %get-tuple-element.183), channel_id=1, source_target_pairs={{0,16},{1,17},{2,18},{3,19},{4,20},{5,21},{6,22},{7,23},{8,24},{9,... | collective-permute-start | bytes 786440 | tf_op jit(solution)/shard_map/ppermute | solution.py:718
  134.0 16.8 %collective-permute-start.36 = (bf16[4,16,2048]{2,1,0:T(8,128)(2,1)S(1)}, bf16[4,16,2048]{2,1,0:T(8,128)(2,1)S(1)}, u32[]{:S(2)}, u32[]{:S(2)}) collective-permute-start(bf16[4,16,2048]{2,1,0:T(8,128)(2,1)S(1)} %get-tuple-element.184), channel_id=1, source_target_pairs={{0,24},{1,25},{2,26},{3,27},{4,28},{5,29},{6,30},{7,31},{8,16},{9,... | collective-permute-start | bytes 786440 | tf_op jit(solution)/shard_map/ppermute | solution.py:718
  151.1 5.5 %collective-permute-start.38 = (bf16[16,16,2176]{2,1,0:T(8,128)(2,1)S(1)}, bf16[16,16,2176]{2,1,0:T(8,128)(2,1)S(1)}, u32[]{:S(2)}, u32[]{:S(2)}) collective-permute-start(bf16[16,16,2176]{2,1,0:T(8,128)(2,1)S(1)} %get-tuple-element.206), channel_id=1, source_target_pairs={{0,1},{1,0},{2,3},{3,2},{4,5},{5,4},{6,7},{7,6},{8,9},{9,8},{10,11... | collective-permute-start | bytes 3342344 | tf_op jit(solution)/shard_map/ppermute | solution.py:718
  151.1 21.4 %collective-permute-start.37 = (bf16[2,16,6144]{2,1,0:T(8,128)(2,1)S(1)}, bf16[2,16,6144]{2,1,0:T(8,128)(2,1)S(1)}, u32[]{:S(2)}, u32[]{:S(2)}) collective-permute-start(bf16[2,16,6144]{2,1,0:T(8,128)(2,1)S(1)} %get-tuple-element.197), channel_id=1, source_target_pairs={{0,4},{1,5},{2,6},{3,7},{4,0},{5,1},{6,2},{7,3},{8,12},{9,13},{10,... | collective-permute-start | bytes 1179656 | tf_op jit(solution)/shard_map/ppermute | solution.py:718
  156.9 27.8 %copy-start = (f32[6,16,512]{2,1,0:T(8,128)S(1)}, f32[6,16,512]{2,1,0:T(8,128)}, u32[]{:S(2)}) copy-start(f32[6,16,512]{2,1,0:T(8,128)} %rest_3_.2) | copy-start | bytes 589828
  157.0 9.6 %collective-permute-start.39 = (bf16[4,16,2176]{2,1,0:T(8,128)(2,1)S(1)}, bf16[4,16,2176]{2,1,0:T(8,128)(2,1)S(1)}, u32[]{:S(2)}, u32[]{:S(2)}) collective-permute-start(bf16[4,16,2176]{2,1,0:T(8,128)(2,1)S(1)} %get-tuple-element.209), channel_id=1, source_target_pairs={{0,8},{1,9},{2,10},{3,11},{4,12},{5,13},{6,14},{7,15},{8,0},{9,1},... | collective-permute-start | bytes 835592 | tf_op jit(solution)/shard_map/ppermute | solution.py:718
  157.7 13.4 %collective-permute-start.40 = (bf16[4,16,2176]{2,1,0:T(8,128)(2,1)S(1)}, bf16[4,16,2176]{2,1,0:T(8,128)(2,1)S(1)}, u32[]{:S(2)}, u32[]{:S(2)}) collective-permute-start(bf16[4,16,2176]{2,1,0:T(8,128)(2,1)S(1)} %get-tuple-element.210), channel_id=1, source_target_pairs={{0,16},{1,17},{2,18},{3,19},{4,20},{5,21},{6,22},{7,23},{8,24},{9,... | collective-permute-start | bytes 835592 | tf_op jit(solution)/shard_map/ppermute | solution.py:718
  159.1 13.2 %collective-permute-start.41 = (bf16[4,16,2176]{2,1,0:T(8,128)(2,1)S(1)}, bf16[4,16,2176]{2,1,0:T(8,128)(2,1)S(1)}, u32[]{:S(2)}, u32[]{:S(2)}) collective-permute-start(bf16[4,16,2176]{2,1,0:T(8,128)(2,1)S(1)} %get-tuple-element.211), channel_id=1, source_target_pairs={{0,24},{1,25},{2,26},{3,27},{4,28},{5,29},{6,30},{7,31},{8,16},{9,... | collective-permute-start | bytes 835592 | tf_op jit(solution)/shard_map/ppermute | solution.py:718
  172.6 8.4 %collective-permute-start.42 = (bf16[16,6144]{1,0:T(8,128)(2,1)S(1)}, bf16[16,6144]{1,0:T(8,128)(2,1)S(1)}, u32[]{:S(2)}, u32[]{:S(2)}) collective-permute-start(bf16[16,6144]{1,0:T(8,128)(2,1)S(1)} %get-tuple-element.217), channel_id=1, source_target_pairs={{0,2},{1,3},{2,0},{3,1},{4,6},{5,7},{6,4},{7,5},{8,10},{9,11},{10,... | collective-permute-start | bytes 589832 | tf_op jit(solution)/shard_map/ppermute | solution.py:718
  174.0 8.4 %collective-permute-start.43 = (bf16[16,2176]{1,0:T(8,128)(2,1)S(1)}, bf16[16,2176]{1,0:T(8,128)(2,1)S(1)}, u32[]{:S(2)}, u32[]{:S(2)}) collective-permute-start(bf16[16,2176]{1,0:T(8,128)(2,1)S(1)} %get-tuple-element.212), channel_id=1, source_target_pairs={{0,2},{1,3},{2,0},{3,1},{4,6},{5,7},{6,4},{7,5},{8,10},{9,11},{10,... | collective-permute-start | bytes 208904 | tf_op jit(solution)/shard_map/ppermute | solution.py:718
  174.7 7.8 %collective-permute-start.44 = (bf16[16,2176]{1,0:T(8,128)(2,1)S(1)}, bf16[16,2176]{1,0:T(8,128)(2,1)S(1)}, u32[]{:S(2)}, u32[]{:S(2)}) collective-permute-start(bf16[16,2176]{1,0:T(8,128)(2,1)S(1)} %get-tuple-element.213), channel_id=1, source_target_pairs={{0,4},{1,5},{2,6},{3,7},{4,0},{5,1},{6,2},{7,3},{8,12},{9,13},{10,... | collective-permute-start | bytes 208904 | tf_op jit(solution)/shard_map/ppermute | solution.py:718
  176.9 7.7 %collective-permute-start.45 = (bf16[16,2176]{1,0:T(8,128)(2,1)S(1)}, bf16[16,2176]{1,0:T(8,128)(2,1)S(1)}, u32[]{:S(2)}, u32[]{:S(2)}) collective-permute-start(bf16[16,2176]{1,0:T(8,128)(2,1)S(1)} %get-tuple-element.214), channel_id=1, source_target_pairs={{0,6},{1,7},{2,4},{3,5},{4,2},{5,3},{6,0},{7,1},{8,14},{9,15},{10,... | collective-permute-start | bytes 208904 | tf_op jit(solution)/shard_map/ppermute | solution.py:718
  (22 other events, 460.8 us)
